TPU v7x, 128 devices: a whole 4x4x4 slice. The times are simulated.
128 devices in a mesh: mp: 16 (over y, x), hidden: 8 (over z, core).
Axes of the slice: x: 4, y: 4, z: 4, core: 2. Of those that a mesh axis runs over, the one named last changes fastest.
Arguments:
- states: bfloat16 [512, 16384], P(None, 'mp'), may hold values from -6 to 6
- gate_codes: bfloat16 [16384, 26624], P('mp', 'hidden'), may hold values from -127 to 127, as said below
- gate_scales: float32 [128, 26624], P('mp', 'hidden'), may hold values from 7.8125e-05 to 0.000703125
- up_codes: bfloat16 [16384, 26624], P('mp', 'hidden'), may hold values from -127 to 127, as said below
- up_scales: float32 [128, 26624], P('mp', 'hidden'), may hold values from 7.8125e-05 to 0.000703125
- down_codes: bfloat16 [26624, 16384], P('hidden', 'mp'), may hold values from -127 to 127, as said below
- down_scales: float32 [208, 16384], P('hidden', 'mp'), may hold values from 1.2257258e-05 to 0.000110315326
Outputs:
- output: bfloat16 [512, 16384], P(None, 'mp')
Inputs may be any that keep to these rules, and one draw needn't show every extreme that they name: `gate_codes`: whole numbers. `up_codes`: whole numbers. `down_codes`: whole numbers.
All inputs are finite; a program needn't handle non-finite values. Where the computation divides by a largest or mean magnitude, that divisor is 1e-20 or more.
Results may differ from a plain program's by a relative error of at most 0.02.
Values may be sent and summed in bfloat16 or wider, within the bound.
No kernel may reach another device: no remote copies, remote signals or barrier semaphores. Data moves between devices by JAX's collectives and lax.ppermute only.
A program may use at most 128 MiB of HBM per device.

v0:
```python
import jax
import jax.numpy as jnp
from jax import lax
from jax.sharding import PartitionSpec as P

BLOCK = 128


epsilon = 1e-06


def in_one_piece(arrays, axis, split_dim, concat_dim, along):
    ends, at = ([], 0)
    for a in arrays[:-1]:
        at += a.shape[along]
        ends.append(at)
    both = jnp.concatenate(arrays, axis=along)
    return tuple(
        jnp.split(
            lax.all_to_all(both, axis, split_axis=split_dim, concat_axis=concat_dim, tiled=True),
            ends,
            axis=along,
        )
    )


def split_up(array, dim, peers):
    lengths = array.shape
    blocks = array.reshape(*lengths[:dim], peers, lengths[dim] // peers, *lengths[dim + 1 :])
    return jnp.moveaxis(blocks, dim, 0)


def sent_and_summed(array, axis, dim):
    peers = lax.axis_size(axis)
    blocks = lax.all_to_all(split_up(array, dim, peers), axis, 0, 0, tiled=True)
    return jnp.sum(blocks.astype(jnp.float32), axis=0)


def joined_along(blocks, dim):
    lengths = list(blocks.shape[1:])
    lengths[dim] *= blocks.shape[0]
    return jnp.moveaxis(blocks, 0, dim).reshape(lengths)


def copy_for_each(array, axis):
    copies = jnp.broadcast_to(array, (lax.axis_size(axis), *array.shape))
    return lax.all_to_all(copies, axis, split_axis=0, concat_axis=0, tiled=True)


def collect(array, axis, dim):
    return joined_along(copy_for_each(array, axis), dim)


def dequantize(quantized, scales):
    depth, columns = quantized.shape
    groups = scales.shape[0]
    blocks = quantized.astype(jnp.float32).reshape(groups, depth // groups, columns)
    return (blocks * scales[:, None, :]).reshape(depth, columns).astype(jnp.bfloat16)


def encode(values):
    row_count, columns = values.shape
    blocks = values.reshape(row_count, columns // BLOCK, BLOCK)
    maxima = (jnp.max(jnp.abs(blocks), axis=-1) + epsilon).astype(jnp.bfloat16)
    factor = 127.0 / maxima.astype(jnp.float32)
    codes = (blocks * factor[..., None]).astype(jnp.bfloat16)
    return (codes.reshape(row_count, columns), maxima)


def decode(codes, maxima):
    row_count, columns = codes.shape
    blocks = codes.astype(jnp.float32).reshape(row_count, columns // BLOCK, BLOCK)
    step_size = maxima.astype(jnp.float32) / 127.0
    return (blocks * step_size[..., None]).reshape(row_count, columns)


def body(states, gate_codes, gate_scales, up_codes, up_scales, down_codes, down_scales):
    gate_w = dequantize(gate_codes, gate_scales)
    up_w = dequantize(up_codes, up_scales)
    columns = gate_w.shape[1]
    row_count = states.shape[0]
    senders = lax.axis_size("mp")
    own_rows = row_count // senders
    gate_part = jnp.dot(states, gate_w, preferred_element_type=jnp.float32)
    up_part = jnp.dot(states, up_w, preferred_element_type=jnp.float32)
    gate_enc, gate_max = encode(gate_part)
    up_enc, up_max = encode(up_part)
    codes = jnp.concatenate([gate_enc, up_enc], axis=1)
    scales = jnp.concatenate([gate_max, up_max], axis=1)
    got_codes, got_scales = in_one_piece((codes, scales), "mp", 0, 0, 1)
    summed = decode(got_codes, got_scales).reshape(senders, own_rows, 2 * columns).sum(axis=0)
    swiglu = jax.nn.silu(summed[:, :columns]) * summed[:, columns:]
    act_codes, act_scales = encode(swiglu)
    all_codes, all_scales = (
        lax.all_gather(act_codes, "mp", axis=0, tiled=True),
        lax.all_gather(act_scales, "mp", axis=0, tiled=True),
    )
    activation = decode(all_codes, all_scales).astype(jnp.bfloat16)
    down_w = dequantize(down_codes, down_scales)
    share = row_count // lax.axis_size("hidden")
    mine_sum = sent_and_summed(
        jnp.dot(activation, down_w, preferred_element_type=jnp.float32).astype(jnp.bfloat16),
        "hidden",
        0,
    )
    residual = lax.dynamic_slice_in_dim(states, lax.axis_index("hidden") * share, share, 0)
    finished = (mine_sum + residual.astype(jnp.float32)).astype(jnp.bfloat16)
    return collect(finished, "hidden", 0)


def solution(mesh):
    in_specs = (
        P(None, "mp"),
        P("mp", "hidden"),
        P("mp", "hidden"),
        P("mp", "hidden"),
        P("mp", "hidden"),
        P("hidden", "mp"),
        P("hidden", "mp"),
    )
    out_specs = P(None, "mp")
    return jax.shard_map(body, mesh=mesh, in_specs=in_specs, out_specs=out_specs, check_vma=False)
```

profile of v0, /device:TPU:1, one launch (start us, length us, event | category | flops | bytes accessed | tf_op | source)
XLA Modules:
  0.0 296.4 jit_solution(4620286258072862822)
XLA Ops:
  6.5 0.0 copy-start.2
  6.5 0.0 all-gather.2.cloned.1.call-start
  6.5 4.3 %fusion.2 = bf16[1024,3328]{1,0:T(8,128)(2,1)S(1)} fusion(bf16[1024,3328]{1,0:T(8,128)(2,1)} %param.10, f32[8,3328]{1,0:T(8,128)} %param.11), kind=kLoop, calls=%fused_computation.5 | loop fusion | flops 10223616 | bytes 13737984 | tf_op jit(solution)/shard_map/convert_element_type | solution.py:58
  10.8 0.0 copy-done.2
  10.8 7.1 %bitcast_abs_fusion = (f32[512,3328]{0,1:T(8,128)}, f32[3328,512]{1,0:T(8,128)}) fusion(bf16[1024,3328]{1,0:T(8,128)(2,1)S(1)} %fusion.2, bf16[512,1024]{1,0:T(8,128)(2,1)S(1)} %copy-done.2), kind=kOutput, calls=%fused_computation.10 | convolution fusion | flops 3491364864 | bytes 21495808 | tf_op jit(solution)/shard_map/dot_general | solution.py:85
  17.9 3.9 %reduce_max.28 = f32[512,26]{0,1:T(8,128)S(1)} reduce(f32[512,26,128]{0,2,1:T(8,128)} %bitcast.54, f32[]{:T(128)} %constant.11.clone.1), dimensions={2}, to_apply=%region_1.0 | reduce | flops 1690624 | bytes 6868996 | tf_op jit(solution)/shard_map/reduce_max | solution.py:64
  21.8 0.0 copy-start.1
  21.8 4.0 %fusion.4 = bf16[512,3328]{0,1:T(8,128)(2,1)S(1)} fusion(f32[3328,512]{1,0:T(8,128)} %get-tuple-element.14, f32[512,26]{0,1:T(8,128)S(1)} %get-tuple-element.7), kind=kLoop, calls=%fused_computation.9 | loop fusion | flops 3407872 | bytes 10276864 | tf_op jit(solution)/shard_map/convert_element_type | solution.py:66
  25.8 3.7 %copy.21 = bf16[512,3328]{1,0:T(8,128)(2,1)} copy(bf16[512,3328]{0,1:T(8,128)(2,1)S(1)} %fusion.4) | data formatting | bytes 6815744 | tf_op jit(solution)/shard_map/convert_element_type | solution.py:66
  29.4 0.0 copy-done.1
  29.4 0.0 copy-start.3
  29.4 4.3 %fusion.3 = bf16[1024,3328]{1,0:T(8,128)(2,1)S(1)} fusion(bf16[1024,3328]{1,0:T(8,128)(2,1)} %param.8, f32[8,3328]{1,0:T(8,128)S(1)} %copy-done.1), kind=kLoop, calls=%fused_computation.7 | loop fusion | flops 10223616 | bytes 13737984 | tf_op jit(solution)/shard_map/convert_element_type | solution.py:58
  33.7 0.0 copy-done.3
  33.7 7.1 %bitcast_abs_fusion.1 = (f32[512,3328]{0,1:T(8,128)}, f32[3328,512]{1,0:T(8,128)}) fusion(bf16[1024,3328]{1,0:T(8,128)(2,1)S(1)} %fusion.3, bf16[512,1024]{1,0:T(8,128)(2,1)S(1)} %copy-done.3), kind=kOutput, calls=%fused_computation.13 | convolution fusion | flops 3491364864 | bytes 21495808 | tf_op jit(solution)/shard_map/dot_general | solution.py:84
  40.8 3.9 %reduce_max.27 = f32[512,26]{0,1:T(8,128)S(1)} reduce(f32[512,26,128]{0,2,1:T(8,128)} %bitcast.55, f32[]{:T(128)} %constant.11.clone.1), dimensions={2}, to_apply=%region_0.0 | reduce | flops 1690624 | bytes 6868996 | tf_op jit(solution)/shard_map/reduce_max | solution.py:64
  44.6 3.9 %fusion.5 = bf16[512,3328]{0,1:T(8,128)(2,1)S(1)} fusion(f32[3328,512]{1,0:T(8,128)} %get-tuple-element.12, f32[512,26]{0,1:T(8,128)S(1)} %get-tuple-element.9), kind=kLoop, calls=%fused_computation.12 | loop fusion | flops 3407872 | bytes 10276864 | tf_op jit(solution)/shard_map/convert_element_type | solution.py:66
  48.6 3.7 %copy.20 = bf16[512,3328]{1,0:T(8,128)(2,1)} copy(bf16[512,3328]{0,1:T(8,128)(2,1)S(1)} %fusion.5) | data formatting | bytes 6815744 | tf_op jit(solution)/shard_map/convert_element_type | solution.py:66
  52.2 0.1 copy.26
  52.4 0.1 copy.27
  52.5 11.9 %concatenate.10 = bf16[16,32,6708]{2,1,0:T(8,128)(2,1)} concatenate(bf16[16,32,3328]{2,1,0:T(8,128)(2,1)} %bitcast.53, bf16[16,32,3328]{2,1,0:T(8,128)(2,1)} %bitcast.52, bf16[16,32,26]{2,1,0:T(8,128)(2,1)S(1)} %bitcast.58, bf16[16,32,26]{2,1,0:T(8,128)(2,1)S(1)} %bitcast.59), dimensions={2} | concatenate | bytes 13737984 | tf_op jit(solution)/shard_map/concatenate | solution.py:17
  64.4 86.8 %all_to_all.19 = bf16[16,32,6708]{2,1,0:T(8,128)(2,1)S(1)} all-to-all(bf16[16,32,6708]{2,1,0:T(8,128)(2,1)} %concatenate.10), channel_id=1, replica_groups=mesh['mp'=16,'hidden'=8] {'mp'}, dimensions={0} | all-to-all | bytes 13737984 | tf_op jit(solution)/shard_map/all_to_all | solution.py:20
  151.2 3.3 %split.8 = bf16[512,6656]{1,0:T(8,128)(2,1)} slice(bf16[512,6708]{1,0:T(8,128)(2,1)S(1)} %bitcast.49), slice={[0:512], [0:6656]} | slice | bytes 13631488 | tf_op jit(solution)/shard_map/split | solution.py:19
  154.5 8.6 %mul.110 = f32[512,52,128]{2,1,0:T(8,128)} broadcast(f32[512,52]{1,0:T(8,128)S(1)} %convert_multiply_fusion.1), dimensions={0,1} | broadcast | bytes 13737984 | tf_op jit(solution)/shard_map/mul | solution.py:74
  163.1 15.6 %mul.111 = f32[16,32,6656]{2,1,0:T(8,128)} reshape(f32[512,52,128]{2,1,0:T(8,128)} %mul.110) | data formatting | bytes 27262976 | tf_op jit(solution)/shard_map/mul | solution.py:74
  178.8 0.0 copy-start
  178.8 8.9 %fusion = f32[32,6656]{1,0:T(8,128)S(1)} fusion(f32[16,32,6656]{2,1,0:T(8,128)} %mul.111, bf16[16,32,6656]{2,1,0:T(8,128)(2,1)} %bitcast.51), kind=kLoop, calls=%fused_computation.1 | loop fusion | flops 10010624 | bytes 21299200 | tf_op jit(solution)/shard_map/reduce_sum | solution.py:91
  187.7 0.1 fusion.9
  187.8 0.1 abs.23
  187.9 0.2 reduce_max.29
  188.2 0.2 mul.115
  188.4 1.0 fusion.8
  189.3 0.0 all-gather.2.cloned.1.call-update
  189.4 0.0 copy-done
  189.4 7.8 %fusion.1 = bf16[3328,1024]{1,0:T(8,128)(2,1)} fusion(bf16[3328,1024]{1,0:T(8,128)(2,1)} %param.12, f32[26,1024]{1,0:T(8,128)S(1)} %copy-done), kind=kLoop, calls=%fused_computation.3 | loop fusion | flops 10223616 | bytes 13737984 | tf_op jit(solution)/shard_map/convert_element_type | solution.py:58
  197.1 17.0 %all_gather.7 = bf16[512,26]{1,0:T(8,128)(2,1)S(1)} all-gather(bf16[32,26]{1,0:T(8,128)(2,1)S(1)} %get-tuple-element.6), channel_id=1, replica_groups=mesh['mp'=16,'hidden'=8] {'mp'}, dimensions={0}, use_global_device_ids=true | all-gather | bytes 28288 | tf_op jit(solution)/shard_map/all_gather | solution.py:96
  214.1 0.1 copy.24
  214.2 3.6 %mul.118 = f32[512,26,128]{0,2,1:T(8,128)} broadcast(f32[512,26]{0,1:T(8,128)S(1)} %convert_multiply_fusion.2), dimensions={0,1} | broadcast | bytes 6868992 | tf_op jit(solution)/shard_map/mul | solution.py:74
  217.9 7.7 %copy.25 = f32[512,3328]{1,0:T(8,128)} copy(f32[512,3328]{0,1:T(8,128)} %bitcast.50) | data formatting | bytes 13631488 | tf_op jit(solution)/shard_map/mul | solution.py:74
  225.5 12.4 %all-gather.2.cloned.1.call-done = bf16[512,3328]{1,0:T(8,128)(2,1)} async-done(((bf16[32,3328]{1,0:T(8,128)(2,1)}), bf16[512,3328]{1,0:T(8,128)(2,1)}) %all-gather.2.cloned.1.call-update) | async-done | bytes 3407888 | tf_op jit(solution)/shard_map/all_gather | solution.py:95
  237.9 10.6 %fusion.7 = bf16[512,1024]{1,0:T(8,128)(2,1)} fusion(bf16[3328,1024]{1,0:T(8,128)(2,1)} %fusion.1, f32[512,3328]{1,0:T(8,128)} %copy.25, bf16[512,3328]{1,0:T(8,128)(2,1)} %all-gather.2.cloned.1.call-done), kind=kOutput, calls=%fused_computation.17 | convolution fusion | flops 3495297024 | bytes 18087936 | tf_op jit(solution)/shard_map/dot_general | solution.py:102
  248.5 5.4 %all-to-all-start.1 = ((bf16[8,64,1024]{2,1,0:T(8,128)(2,1)}), bf16[8,64,1024]{2,1,0:T(8,128)(2,1)S(1)}, u32[]{:S(2)}, u32[]{:S(2)}) async-start(bf16[8,64,1024]{2,1,0:T(8,128)(2,1)} %bitcast.16), calls=%async_computation.1 | async-start | bytes 2097152 | tf_op jit(solution)/shard_map/all_to_all | solution.py:35
  253.9 15.1 %all-to-all-done.1 = bf16[8,64,1024]{2,1,0:T(8,128)(2,1)S(1)} async-done(((bf16[8,64,1024]{2,1,0:T(8,128)(2,1)}), bf16[8,64,1024]{2,1,0:T(8,128)(2,1)S(1)}, u32[]{:S(2)}, u32[]{:S(2)}) %all-to-all-start.1) | async-done | bytes 1048608 | tf_op jit(solution)/shard_map/all_to_all | solution.py:35
  269.0 0.2 convert_reduce_fusion
  269.2 0.9 add_convert_fusion
  270.2 0.1 broadcast_in_dim.2
  270.3 18.4 %all_to_all.20 = bf16[8,64,1024]{2,1,0:T(8,128)(2,1)S(1)} all-to-all(bf16[8,64,1024]{2,1,0:T(8,128)(2,1)S(1)} %broadcast_in_dim.2), channel_id=1, replica_groups=mesh['mp'=16,'hidden'=8] {'hidden'}, dimensions={0} | all-to-all | bytes 2097152 | tf_op jit(solution)/shard_map/all_to_all | solution.py:47
  288.6 1.0 copy.31
  (5 shorter events, 0.1 us)
Async XLA Ops:
  6.5 4.3 %copy-start.2 = (bf16[512,1024]{1,0:T(8,128)(2,1)S(1)}, bf16[512,1024]{1,0:T(8,128)(2,1)}, u32[]{:S(2)}) copy-start(bf16[512,1024]{1,0:T(8,128)(2,1)} %param.7) | copy-start | bytes 3145732
  6.5 231.4 %all-gather.2.cloned.1.call-start = ((), (), s32[]{:S(2)}) async-start(), calls=%async_computation.3 | async-start | bytes 3620864 | tf_op jit(solution)/shard_map/all_gather | solution.py:95
  21.8 7.6 %copy-start.1 = (f32[8,3328]{1,0:T(8,128)S(1)}, f32[8,3328]{1,0:T(8,128)}, u32[]{:S(2)}) copy-start(f32[8,3328]{1,0:T(8,128)} %param.9) | copy-start | bytes 319492
  29.4 4.3 %copy-start.3 = (bf16[512,1024]{1,0:T(8,128)(2,1)S(1)}, bf16[512,1024]{1,0:T(8,128)(2,1)}, u32[]{:S(2)}) copy-start(bf16[512,1024]{1,0:T(8,128)(2,1)} %param.7) | copy-start | bytes 3145732
  178.8 10.6 %copy-start = (f32[26,1024]{1,0:T(8,128)S(1)}, f32[26,1024]{1,0:T(8,128)}, u32[]{:S(2)}) copy-start(f32[26,1024]{1,0:T(8,128)} %param.13) | copy-start | bytes 319492
  248.5 20.5 %all-to-all-start.1 = ((bf16[8,64,1024]{2,1,0:T(8,128)(2,1)}), bf16[8,64,1024]{2,1,0:T(8,128)(2,1)S(1)}, u32[]{:S(2)}, u32[]{:S(2)}) async-start(bf16[8,64,1024]{2,1,0:T(8,128)(2,1)} %bitcast.16), calls=%async_computation.1 | async-start | bytes 2097152 | tf_op jit(solution)/shard_map/all_to_all | solution.py:35
Sparse Core Ops, SparseCore 0:
  189.5 48.4 all-gather.1
where the time goes:
time: 298 us; the launch traced here: 296 us
  blocking collectives  122 us (41%)
  local copies, waits for them, and re-layouts  59.8 us (20%)
  other arithmetic  43.4 us (15%)
  waiting for transfers between devices  27.5 us (9%)
  matrix products  24.7 us (8%)
  between operations  13.5 us (5%)
  starting transfers between devices  5.45 us (2%)
    all_to_all x1, blocking collectives, in_one_piece(): lax.all_to_all(both, axis, split_axis=split_dim, concat_axis=concat_dim,...  86.8 us
    mul x4, local copies, waits for them, and re-layouts, decode(): return (blocks * step_size[..., None]).reshape(row_count, columns)  35.5 us
    all_to_all x1, blocking collectives, copy_for_each(): return lax.all_to_all(copies, axis, split_axis=0, concat_axis=0, tiled=True)  18.4 us
    all_gather x1, blocking collectives, body(): lax.all_gather(act_scales, 'mp', axis=0, tiled=True)  17 us
    convert_element_type x3, other arithmetic, dequantize(): (blocks * scales[:, None, :]).reshape(depth, columns).astype(jnp.bfloat16)  16.3 us
    all_to_all x1, waiting for transfers between devices, sent_and_summed(): blocks = lax.all_to_all(split_up(array, dim, peers), axis, 0, 0, tiled=True)  15.1 us
    all_gather x1, waiting for transfers between devices, body(): lax.all_gather(act_codes, 'mp', axis=0, tiled=True)  12.4 us
    concatenate x1, local copies, waits for them, and re-layouts, in_one_piece(): both = jnp.concatenate(arrays, axis=along)  11.9 us
  transfers between devices with their start and end apart: 2, of which 2 were waited for; matrix products, arithmetic and copies ran while one was open for 6% of the time, Pallas kernels for 0%

commit v1 on v0

v1 whole, which is shorter than its diff:
```python
import jax
import jax.numpy as jnp
from jax import lax
from jax.sharding import Mesh, PartitionSpec as P

BLOCK = 128
SIDE = 4
PLANE = ("y", "x", "core")


def hop(array, which, shift):
    pairs = []
    for y in range(SIDE):
        for x in range(SIDE):
            for c in range(2):
                if (c + which) % 2 == 0:
                    to = (y, (x + shift) % SIDE)
                else:
                    to = ((y + shift) % SIDE, x)
                pairs.append(((y * SIDE + x) * 2 + c, (to[0] * SIDE + to[1]) * 2 + c))
    return lax.ppermute(array, PLANE, pairs)


def hop_z(array, shift):
    return lax.ppermute(array, "z", [(i, (i + shift) % SIDE) for i in range(SIDE)])


def other_core(array):
    return lax.ppermute(array, "core", [(0, 1), (1, 0)])


def dequantize(quantized, scales):
    depth, columns = quantized.shape
    groups = scales.shape[0]
    blocks = quantized.astype(jnp.float32).reshape(groups, depth // groups, columns)
    return (blocks * scales[:, None, :]).reshape(depth, columns).astype(jnp.bfloat16)


def total(*terms):
    out = terms[0].astype(jnp.float32)
    for t in terms[1:]:
        out = out + t.astype(jnp.float32)
    return out


def scattered(gates, ups, which):
    relay_up = hop(ups[2], which, 1)
    relay_gate = hop(gates[2], which, -1)
    own_gate = hop(gates[1], which, 1)
    own_up = hop(ups[3], which, -1)
    sum_up = hop(total(ups[1], relay_up).astype(jnp.bfloat16), which, 1)
    sum_gate = hop(total(gates[3], relay_gate).astype(jnp.bfloat16), which, -1)
    return total(gates[0], own_gate, sum_gate), total(ups[0], sum_up, own_up)


def gathered(own, which):
    half = own.shape[0] // 2
    ahead_top = hop(own[:half], which, -1)
    behind_low = hop(own[half:], which, 1)
    ahead_low = hop(own[half:], which, -1)
    behind_top = hop(own[:half], which, 1)
    far_top = hop(ahead_top, which, -1)
    far_low = hop(behind_low, which, 1)
    return [own, (ahead_top, ahead_low), (far_top, far_low), (behind_top, behind_low)]


def gathered_small(own, which):
    return [own, hop(own, which, -1), hop(own, which, 2), hop(own, which, 1)]


def body(states, gate_codes, gate_scales, up_codes, up_scales, down_codes, down_scales):
    rows, width = states.shape
    columns = gate_codes.shape[1]
    core = lax.axis_index("core")
    ix, iy, iz = lax.axis_index("x"), lax.axis_index("y"), lax.axis_index("z")
    first = jnp.where(core == 0, ix, iy)
    second = jnp.where(core == 0, iy, ix)
    piece = rows // (SIDE * SIDE)
    turned = states.reshape(SIDE, SIDE, piece, width)
    turned = lax.dynamic_slice_in_dim(jnp.concatenate([turned, turned[:3]], 0), first, SIDE, 0)
    turned = lax.dynamic_slice_in_dim(jnp.concatenate([turned, turned[:, :3]], 1), second, SIDE, 1)
    turned = turned.reshape(rows, width)

    gate_w = dequantize(gate_codes, gate_scales)
    up_w = dequantize(up_codes, up_scales)
    gate = jnp.dot(turned, gate_w, preferred_element_type=jnp.float32).astype(jnp.bfloat16)
    up = jnp.dot(turned, up_w, preferred_element_type=jnp.float32).astype(jnp.bfloat16)
    q = rows // SIDE
    gates = [gate[k * q : (k + 1) * q] for k in range(SIDE)]
    ups = [up[k * q : (k + 1) * q] for k in range(SIDE)]
    gate, up = scattered(gates, ups, 0)
    gate, up = gate.astype(jnp.bfloat16), up.astype(jnp.bfloat16)
    gates = [gate[k * piece : (k + 1) * piece] for k in range(SIDE)]
    ups = [up[k * piece : (k + 1) * piece] for k in range(SIDE)]
    gate, up = scattered(gates, ups, 1)
    act = (jax.nn.silu(gate) * up).astype(jnp.bfloat16)

    parts = gathered_small(act, 1)
    line = jnp.zeros((SIDE, piece, columns), jnp.bfloat16)
    for k, part in enumerate(parts):
        line = lax.dynamic_update_slice_in_dim(line, part[None], (second + k) % SIDE, 0)
    line = line.reshape(q, columns)
    parts = gathered(line, 0)
    full = jnp.zeros((SIDE, 2, q // 2, columns), jnp.bfloat16)
    full = lax.dynamic_update_slice(full, line.reshape(1, 2, q // 2, columns), (first, 0, 0, 0))
    for k in range(1, SIDE):
        for h in range(2):
            full = lax.dynamic_update_slice(full, parts[k][h][None, None], ((first + k) % SIDE, h, 0, 0))
    activation = full.reshape(rows, columns)

    down_w = dequantize(down_codes, down_scales)
    part = jnp.dot(activation, down_w, preferred_element_type=jnp.float32).astype(jnp.bfloat16)
    half = rows // 2
    share = half // SIDE
    mine = lax.dynamic_slice_in_dim(part, core * half, half, 0)
    theirs = other_core(lax.dynamic_slice_in_dim(part, (1 - core) * half, half, 0))
    both = total(mine, theirs).astype(jnp.bfloat16).reshape(SIDE, share, width)

    def for_z(k):
        return lax.dynamic_index_in_dim(both, (iz + k) % SIDE, 0, keepdims=False)

    mine = total(for_z(0), hop_z(for_z(1), 1), hop_z(for_z(3), -1), hop_z(for_z(2), 2))
    residual = lax.dynamic_slice_in_dim(states, core * half + iz * share, share, 0)
    done = (mine + residual.astype(jnp.float32)).astype(jnp.bfloat16)
    pieces = [done, hop_z(done, -1), hop_z(done, 2), hop_z(done, 1)]
    mine = jnp.zeros((SIDE, share, width), jnp.bfloat16)
    for k, p in enumerate(pieces):
        mine = lax.dynamic_update_slice_in_dim(mine, p[None], (iz + k) % SIDE, 0)
    mine = mine.reshape(half, width)
    theirs = other_core(mine)
    out = jnp.zeros((rows, width), jnp.bfloat16)
    out = lax.dynamic_update_slice_in_dim(out, mine, core * half, 0)
    return lax.dynamic_update_slice_in_dim(out, theirs, (1 - core) * half, 0)


def solution(mesh):
    grid = Mesh(mesh.devices.reshape(SIDE, SIDE, SIDE, 2), ("y", "x", "z", "core"))
    mp, hidden = ("y", "x"), ("z", "core")
    in_specs = (
        P(None, mp),
        P(mp, hidden),
        P(mp, hidden),
        P(mp, hidden),
        P(mp, hidden),
        P(hidden, mp),
        P(hidden, mp),
    )
    return jax.shard_map(body, mesh=grid, in_specs=in_specs, out_specs=P(None, mp), check_vma=False)
```

time: 298 us -> 148 us (0.50)
  blocking collectives: 122 us -> 0 us
  local copies, waits for them, and re-layouts: 59.8 us -> 4.59 us
  starting transfers between devices: 5.45 us -> 45.3 us
  waiting for transfers between devices: 27.5 us -> 61.6 us
  other arithmetic: 43.4 us -> 20.9 us
  between operations: 13.5 us -> 0.48 us
  matrix products: 24.7 us -> 14.7 us
    all_to_all x2 -> x0, blocking collectives: 105 us -> none  [the longest x1 86.8 us: in_one_piece(): lax.all_to_all(both, axis, split_axis=split_dim, concat_axis=concat_dim,...]
    ppermute x0 -> x29, waiting for transfers between devices: none -> 61.6 us  [the longest x21 47.8 us: hop(): return lax.ppermute(array, PLANE, pairs)]
    ppermute x0 -> x29, starting transfers between devices: none -> 45.3 us  [the longest x21 26.9 us: hop(): return lax.ppermute(array, PLANE, pairs)]
    mul x5 -> x0, local copies, waits for them, and re-layouts: 35.7 us -> none  [the longest x4 35.5 us: decode(): return (blocks * step_size[..., None]).reshape(row_count, columns)]
    all_gather x1 -> x0, blocking collectives: 17 us -> none  [body(): lax.all_gather(act_scales, 'mp', axis=0, tiled=True)]
    all_to_all x1 -> x0, waiting for transfers between devices: 15.1 us -> none  [sent_and_summed(): blocks = lax.all_to_all(split_up(array, dim, peers), axis, 0, 0, tiled=True)]
    all_gather x1 -> x0, waiting for transfers between devices: 12.4 us -> none  [body(): lax.all_gather(act_codes, 'mp', axis=0, tiled=True)]
    concatenate x1 -> x0, local copies, waits for them, and re-layouts: 11.9 us -> none  [in_one_piece(): both = jnp.concatenate(arrays, axis=along)]
  transfers between devices with their start and end apart: 2 -> 29, of which waited for: 2 -> 19; matrix products, arithmetic and copies ran while one was open for 6% -> 12% of each run, Pallas kernels for 0% -> 0%
where the time goes in v1:
time: 148 us
  waiting for transfers between devices  61.6 us (42%)
  starting transfers between devices  45.3 us (31%)
  other arithmetic  20.9 us (14%)
  matrix products  14.7 us (10%)
  local copies, waits for them, and re-layouts  4.59 us (3%)
    ppermute x21, waiting for transfers between devices, hop(): return lax.ppermute(array, PLANE, pairs)  47.8 us
    ppermute x21, starting transfers between devices, hop(): return lax.ppermute(array, PLANE, pairs)  26.9 us
    convert_element_type x3, other arithmetic, dequantize(): (blocks * scales[:, None, :]).reshape(depth, columns).astype(jnp.bfloat16)  13.2 us
    ppermute x2, starting transfers between devices, other_core(): return lax.ppermute(array, 'core', [(0, 1), (1, 0)])  11 us
    ppermute x6, waiting for transfers between devices, hop_z(): lax.ppermute(array, 'z', [(i, (i + shift) % SIDE) for i in range(SIDE)])  10.9 us
    ppermute x6, starting transfers between devices, hop_z(): lax.ppermute(array, 'z', [(i, (i + shift) % SIDE) for i in range(SIDE)])  7.5 us
    dot_general x1, matrix products, body(): jnp.dot(turned, gate_w, preferred_element_type=jnp.float32)  5.58 us
    dot_general x1, matrix products, body(): jnp.dot(turned, up_w, preferred_element_type=jnp.float32)  5.44 us
  transfers between devices with their start and end apart: 29, of which 19 were waited for; matrix products, arithmetic and copies ran while one was open for 12% of the time, Pallas kernels for 0%

profile of v1, /device:TPU:1, one launch (start us, length us, event | category | flops | bytes accessed | tf_op | source)
XLA Modules:
  0.0 147.6 jit_solution(8300396373853100667)
XLA Ops:
  0.0 1.2 slice.71
  1.2 1.6 %fusion.4 = bf16[4,4,32,1024]{3,2,1,0:T(8,128)(2,1)S(1)} fusion(s32[]{:T(128)S(6)} %select_n.129, bf16[4,4,32,1024]{3,2,1,0:T(8,128)(2,1)} %bitcast.68, bf16[3,4,32,1024]{3,2,1,0:T(8,128)(2,1)S(1)} %bitcast.70), kind=kLoop, calls=%fused_computation.18 | loop fusion | flops 524288 | bytes 2883588 | tf_op jit(solution)/shard_map/concatenate | solution.py:80
  2.9 1.3 fusion.3
  4.2 4.2 %fusion.2 = bf16[1024,3328]{1,0:T(8,128)(2,1)S(1)} fusion(bf16[1024,3328]{1,0:T(8,128)(2,1)} %param.8, f32[8,3328]{1,0:T(8,128)S(1)} %copy-done.5), kind=kLoop, calls=%fused_computation.5 | loop fusion | flops 10223616 | bytes 13737984 | tf_op jit(solution)/shard_map/convert_element_type | solution.py:36
  8.4 5.6 %convolution_convert_fusion.1 = bf16[512,3328]{1,0:T(8,128)(2,1)S(1)} fusion(bf16[512,1024]{1,0:T(8,128)(2,1)} %bitcast.75, bf16[1024,3328]{1,0:T(8,128)(2,1)S(1)} %fusion.2), kind=kOutput, calls=%fused_computation.7 | convolution fusion | flops 3491364864 | bytes 11272192 | tf_op jit(solution)/shard_map/dot_general | solution.py:86
  14.0 1.3 fusion.10
  15.3 3.3 %collective-permute-start.1 = (bf16[128,3328]{1,0:T(8,128)(2,1)}, bf16[128,3328]{1,0:T(8,128)(2,1)S(1)}, u32[]{:S(2)}, u32[]{:S(2)}) collective-permute-start(bf16[128,3328]{1,0:T(8,128)(2,1)} %get-tuple-element.10), channel_id=1, source_target_pairs={{0,24},{1,97},{8,0},{9,105},{16,8},{17,113},{24,16},{25,121},{32,5... | collective-permute-start | bytes 2555912 | tf_op jit(solution)/shard_map/ppermute | solution.py:21
  18.6 1.2 fusion.1
  19.9 5.4 %convolution_convert_fusion = bf16[512,3328]{1,0:T(8,128)(2,1)S(1)} fusion(bf16[512,1024]{1,0:T(8,128)(2,1)} %bitcast.76, bf16[1024,3328]{1,0:T(8,128)(2,1)S(1)} %fusion.1), kind=kOutput, calls=%fused_computation.6 | convolution fusion | flops 3491364864 | bytes 11272192 | tf_op jit(solution)/shard_map/dot_general | solution.py:87
  25.4 0.1 fusion.11
  25.5 0.9 collective-permute-start.6
  26.4 1.9 %collective-permute-start.8 = (bf16[128,3328]{1,0:T(8,128)(2,1)S(1)}, bf16[128,3328]{1,0:T(8,128)(2,1)S(1)}, u32[]{:S(2)}, u32[]{:S(2)}) collective-permute-start(bf16[128,3328]{1,0:T(8,128)(2,1)S(1)} %get-tuple-element.12), channel_id=1, source_target_pairs={{0,24},{1,97},{8,0},{9,105},{16,8},{17,113},{24,16},{25,121},{32,5... | collective-permute-start | bytes 2555912 | tf_op jit(solution)/shard_map/ppermute | solution.py:21
  28.3 0.3 collective-permute-done.1
  28.6 0.3 add_convert_fusion.3
  28.8 3.5 %collective-permute-start.2 = (bf16[128,3328]{1,0:T(8,128)(2,1)S(1)}, bf16[128,3328]{1,0:T(8,128)(2,1)S(1)}, u32[]{:S(2)}, u32[]{:S(2)}) collective-permute-start(bf16[128,3328]{1,0:T(8,128)(2,1)S(1)} %add_convert_fusion.3), channel_id=1, source_target_pairs={{0,24},{1,97},{8,0},{9,105},{16,8},{17,113},{24,16},{25,121},{32,5... | collective-permute-start | bytes 2555912 | tf_op jit(solution)/shard_map/ppermute | solution.py:21
  32.3 8.7 %collective-permute-done.6 = bf16[128,3328]{1,0:T(8,128)(2,1)S(1)} collective-permute-done((bf16[128,3328]{1,0:T(8,128)(2,1)S(1)}, bf16[128,3328]{1,0:T(8,128)(2,1)S(1)}, u32[]{:S(2)}, u32[]{:S(2)}) %collective-permute-start.6) | collective-permute-done | bytes 852000 | tf_op jit(solution)/shard_map/ppermute | solution.py:21
  41.0 0.2 add_convert_fusion.1
  41.2 0.1 collective-permute-start.7
  41.3 6.0 %collective-permute-done.2 = bf16[128,3328]{1,0:T(8,128)(2,1)S(1)} collective-permute-done((bf16[128,3328]{1,0:T(8,128)(2,1)S(1)}, bf16[128,3328]{1,0:T(8,128)(2,1)S(1)}, u32[]{:S(2)}, u32[]{:S(2)}) %collective-permute-start.2) | collective-permute-done | bytes 852000 | tf_op jit(solution)/shard_map/ppermute | solution.py:21
  47.3 1.5 %add_convert_fusion.2 = bf16[128,3328]{1,0:T(8,128)(2,1)S(1)} fusion(bf16[128,3328]{1,0:T(8,128)(2,1)S(1)} %collective-permute-done.2, bf16[128,3328]{1,0:T(8,128)(2,1)} %collective-permute-done, bf16[512,3328]{1,0:T(8,128)(2,1)S(1)} %copy-done.2), kind=kLoop, calls=%fused_computation.14 | loop fusion | flops 2555904 | bytes 3407872 | tf_op jit(solution)/shard_map/convert_element_type | solution.py:92
  48.9 2.5 %collective-permute-start.4 = (bf16[32,3328]{1,0:T(8,128)(2,1)S(1)}, bf16[32,3328]{1,0:T(8,128)(2,1)S(1)}, u32[]{:S(2)}, u32[]{:S(2)}) collective-permute-start(bf16[32,3328]{1,0:T(8,128)(2,1)S(1)} %get-tuple-element.16), channel_id=1, source_target_pairs={{0,96},{1,25},{8,104},{9,1},{16,112},{17,9},{24,120},{25,17},{32,0... | collective-permute-start | bytes 638984 | tf_op jit(solution)/shard_map/ppermute | solution.py:21
  51.4 2.9 %collective-permute-done.7 = bf16[128,3328]{1,0:T(8,128)(2,1)S(1)} collective-permute-done((bf16[128,3328]{1,0:T(8,128)(2,1)S(1)}, bf16[128,3328]{1,0:T(8,128)(2,1)S(1)}, u32[]{:S(2)}, u32[]{:S(2)}) %collective-permute-start.7) | collective-permute-done | bytes 852000 | tf_op jit(solution)/shard_map/ppermute | solution.py:21
  54.3 0.3 add_convert_fusion
  54.7 0.7 collective-permute-start.9
  55.4 2.1 %collective-permute-start.11 = (bf16[32,3328]{1,0:T(8,128)(2,1)S(1)}, bf16[32,3328]{1,0:T(8,128)(2,1)S(1)}, u32[]{:S(2)}, u32[]{:S(2)}) collective-permute-start(bf16[32,3328]{1,0:T(8,128)(2,1)S(1)} %get-tuple-element.18), channel_id=1, source_target_pairs={{0,96},{1,25},{8,104},{9,1},{16,112},{17,9},{24,120},{25,17},{32,0... | collective-permute-start | bytes 638984 | tf_op jit(solution)/shard_map/ppermute | solution.py:21
  57.5 1.0 collective-permute-start.5
  58.5 2.1 %collective-permute-done.9 = bf16[32,3328]{1,0:T(8,128)(2,1)S(1)} collective-permute-done((bf16[32,3328]{1,0:T(8,128)(2,1)S(1)}, bf16[32,3328]{1,0:T(8,128)(2,1)S(1)}, u32[]{:S(2)}, u32[]{:S(2)}) %collective-permute-start.9) | collective-permute-done | bytes 213024 | tf_op jit(solution)/shard_map/ppermute | solution.py:21
  60.7 0.1 collective-permute-start.10
  60.8 1.8 %collective-permute-done.5 = bf16[32,3328]{1,0:T(8,128)(2,1)S(1)} collective-permute-done((bf16[32,3328]{1,0:T(8,128)(2,1)S(1)}, bf16[32,3328]{1,0:T(8,128)(2,1)S(1)}, u32[]{:S(2)}, u32[]{:S(2)}) %collective-permute-start.5) | collective-permute-done | bytes 213024 | tf_op jit(solution)/shard_map/ppermute | solution.py:21
  62.6 4.1 %collective-permute-done.10 = bf16[32,3328]{1,0:T(8,128)(2,1)} collective-permute-done((bf16[32,3328]{1,0:T(8,128)(2,1)S(1)}, bf16[32,3328]{1,0:T(8,128)(2,1)}, u32[]{:S(2)}, u32[]{:S(2)}) %collective-permute-start.10) | collective-permute-done | bytes 213024 | tf_op jit(solution)/shard_map/ppermute | solution.py:21
  66.8 1.2 bitcast_dynamic-update-slice_fusion.9
  68.0 0.1 collective-permute-start.12
  68.2 7.8 %fusion = bf16[3328,1024]{1,0:T(8,128)(2,1)} fusion(bf16[3328,1024]{1,0:T(8,128)(2,1)} %param.12, f32[26,1024]{1,0:T(8,128)S(1)} %copy-done.4), kind=kLoop, calls=%fused_computation.1 | loop fusion | flops 10223616 | bytes 13737984 | tf_op jit(solution)/shard_map/convert_element_type | solution.py:36
  76.0 0.6 collective-permute-start.13
  76.6 0.8 collective-permute-start.14
  77.4 4.9 %collective-permute-done.13 = bf16[32,3328]{1,0:T(8,128)(2,1)S(1)} collective-permute-done((bf16[32,3328]{1,0:T(8,128)(2,1)S(1)}, bf16[32,3328]{1,0:T(8,128)(2,1)S(1)}, u32[]{:S(2)}, u32[]{:S(2)}) %collective-permute-start.13) | collective-permute-done | bytes 213024 | tf_op jit(solution)/shard_map/ppermute | solution.py:21
  82.3 2.2 %collective-permute-done.14 = bf16[32,3328]{1,0:T(8,128)(2,1)S(1)} collective-permute-done((bf16[32,3328]{1,0:T(8,128)(2,1)S(1)}, bf16[32,3328]{1,0:T(8,128)(2,1)S(1)}, u32[]{:S(2)}, u32[]{:S(2)}) %collective-permute-start.14) | collective-permute-done | bytes 213024 | tf_op jit(solution)/shard_map/ppermute | solution.py:21
  84.5 3.2 %collective-permute-start.16 = (bf16[64,3328]{1,0:T(8,128)(2,1)S(1)}, bf16[64,3328]{1,0:T(8,128)(2,1)S(1)}, u32[]{:S(2)}, u32[]{:S(2)}) collective-permute-start(bf16[64,3328]{1,0:T(8,128)(2,1)S(1)} %bitcast.79), channel_id=1, source_target_pairs={{0,24},{1,97},{8,0},{9,105},{16,8},{17,113},{24,16},{25,121},{32,5... | collective-permute-start | bytes 1277960 | tf_op jit(solution)/shard_map/ppermute | solution.py:21
  87.8 2.7 %collective-permute-start.15 = (bf16[64,3328]{1,0:T(8,128)(2,1)S(1)}, bf16[64,3328]{1,0:T(8,128)(2,1)S(1)}, u32[]{:S(2)}, u32[]{:S(2)}) collective-permute-start(bf16[64,3328]{1,0:T(8,128)(2,1)S(1)} %bitcast.77), channel_id=1, source_target_pairs={{0,24},{1,97},{8,0},{9,105},{16,8},{17,113},{24,16},{25,121},{32,5... | collective-permute-start | bytes 1277960 | tf_op jit(solution)/shard_map/ppermute | solution.py:21
  90.5 0.2 broadcast_in_dim.59
  90.7 0.1 constant_dynamic-update-slice_fusion.2
  90.8 6.6 %collective-permute-done.15 = bf16[64,3328]{1,0:T(8,128)(2,1)S(1)} collective-permute-done((bf16[64,3328]{1,0:T(8,128)(2,1)S(1)}, bf16[64,3328]{1,0:T(8,128)(2,1)S(1)}, u32[]{:S(2)}, u32[]{:S(2)}) %collective-permute-start.15) | collective-permute-done | bytes 426016 | tf_op jit(solution)/shard_map/ppermute | solution.py:21
  97.4 3.4 %collective-permute-start.17 = (bf16[64,3328]{1,0:T(8,128)(2,1)S(1)}, bf16[64,3328]{1,0:T(8,128)(2,1)S(1)}, u32[]{:S(2)}, u32[]{:S(2)}) collective-permute-start(bf16[64,3328]{1,0:T(8,128)(2,1)S(1)} %collective-permute-done.15), channel_id=1, source_target_pairs={{0,24},{1,97},{8,0},{9,105},{16,8},{17,113},{24,16},{25,121},{32,5... | collective-permute-start | bytes 1277960 | tf_op jit(solution)/shard_map/ppermute | solution.py:21
  100.9 5.0 %collective-permute-done.17 = bf16[64,3328]{1,0:T(8,128)(2,1)S(1)} collective-permute-done((bf16[64,3328]{1,0:T(8,128)(2,1)S(1)}, bf16[64,3328]{1,0:T(8,128)(2,1)S(1)}, u32[]{:S(2)}, u32[]{:S(2)}) %collective-permute-start.17) | collective-permute-done | bytes 426016 | tf_op jit(solution)/shard_map/ppermute | solution.py:21
  106.0 3.1 %collective-permute-done.19 = bf16[64,3328]{1,0:T(8,128)(2,1)S(1)} collective-permute-done((bf16[64,3328]{1,0:T(8,128)(2,1)S(1)}, bf16[64,3328]{1,0:T(8,128)(2,1)S(1)}, u32[]{:S(2)}, u32[]{:S(2)}) %collective-permute-start.19) | collective-permute-done | bytes 426016 | tf_op jit(solution)/shard_map/ppermute | solution.py:21
  109.2 3.7 %convolution_convert_fusion.2 = bf16[512,1024]{1,0:T(8,128)(2,1)S(1)} fusion(bf16[512,3328]{1,0:T(8,128)(2,1)S(1)} %bitcast.69, bf16[3328,1024]{1,0:T(8,128)(2,1)S(1)} %copy-done), kind=kOutput, calls=%fused_computation.16 | convolution fusion | flops 3490185216 | bytes 11272192 | tf_op jit(solution)/shard_map/dot_general | solution.py:112
  112.9 7.3 %collective-permute-start.21 = (bf16[256,1024]{1,0:T(8,128)(2,1)S(1)}, bf16[256,1024]{1,0:T(8,128)(2,1)S(1)}, u32[]{:S(2)}, u32[]{:S(2)}) collective-permute-start(bf16[256,1024]{1,0:T(8,128)(2,1)S(1)} %constant_dynamic-slice_fusion), channel_id=1, source_target_pairs={{0,1},{1,0},{2,3},{3,2},{4,5},{5,4},{6,7},{7,6},{8,9},{9,8},{10,11... | collective-permute-start | bytes 1572872 | tf_op jit(solution)/shard_map/ppermute | solution.py:29
  120.2 1.5 %collective-permute-done.21 = bf16[256,1024]{1,0:T(8,128)(2,1)S(1)} collective-permute-done((bf16[256,1024]{1,0:T(8,128)(2,1)S(1)}, bf16[256,1024]{1,0:T(8,128)(2,1)S(1)}, u32[]{:S(2)}, u32[]{:S(2)}) %collective-permute-start.21) | collective-permute-done | bytes 524320 | tf_op jit(solution)/shard_map/ppermute | solution.py:29
  121.8 0.2 add_convert_fusion.4
  122.0 1.7 %collective-permute-start.22 = (bf16[64,1024]{1,0:T(8,128)(2,1)S(1)}, bf16[64,1024]{1,0:T(8,128)(2,1)S(1)}, u32[]{:S(2)}, u32[]{:S(2)}) collective-permute-start(bf16[64,1024]{1,0:T(8,128)(2,1)S(1)} %get-tuple-element.19), channel_id=1, source_target_pairs={{0,2},{2,4},{4,6},{6,0},{1,3},{3,5},{5,7},{7,1},{8,10},{10,12},{12... | collective-permute-start | bytes 393224 | tf_op jit(solution)/shard_map/ppermute | solution.py:25
  123.7 2.2 %collective-permute-start.23 = (bf16[64,1024]{1,0:T(8,128)(2,1)S(1)}, bf16[64,1024]{1,0:T(8,128)(2,1)S(1)}, u32[]{:S(2)}, u32[]{:S(2)}) collective-permute-start(bf16[64,1024]{1,0:T(8,128)(2,1)S(1)} %get-tuple-element.21), channel_id=1, source_target_pairs={{0,6},{2,0},{4,2},{6,4},{1,7},{3,1},{5,3},{7,5},{8,14},{10,8},{12,... | collective-permute-start | bytes 393224 | tf_op jit(solution)/shard_map/ppermute | solution.py:25
  125.9 1.2 collective-permute-start.24
  127.1 2.3 %collective-permute-done.22 = bf16[64,1024]{1,0:T(8,128)(2,1)S(1)} collective-permute-done((bf16[64,1024]{1,0:T(8,128)(2,1)S(1)}, bf16[64,1024]{1,0:T(8,128)(2,1)S(1)}, u32[]{:S(2)}, u32[]{:S(2)}) %collective-permute-start.22) | collective-permute-done | bytes 131104 | tf_op jit(solution)/shard_map/ppermute | solution.py:25
  129.4 3.7 %collective-permute-done.24 = bf16[64,1024]{1,0:T(8,128)(2,1)S(1)} collective-permute-done((bf16[64,1024]{1,0:T(8,128)(2,1)S(1)}, bf16[64,1024]{1,0:T(8,128)(2,1)S(1)}, u32[]{:S(2)}, u32[]{:S(2)}) %collective-permute-start.24) | collective-permute-done | bytes 131104 | tf_op jit(solution)/shard_map/ppermute | solution.py:25
  133.1 1.0 bitcast_dynamic-update-slice_fusion.13
  134.1 0.5 collective-permute-start.25
  134.6 1.9 %collective-permute-start.26 = (bf16[64,1024]{1,0:T(8,128)(2,1)S(1)}, bf16[64,1024]{1,0:T(8,128)(2,1)S(1)}, u32[]{:S(2)}, u32[]{:S(2)}) collective-permute-start(bf16[64,1024]{1,0:T(8,128)(2,1)S(1)} %get-tuple-element.6), channel_id=1, source_target_pairs={{0,4},{2,6},{4,0},{6,2},{1,5},{3,7},{5,1},{7,3},{8,12},{10,14},{12... | collective-permute-start | bytes 393224 | tf_op jit(solution)/shard_map/ppermute | solution.py:25
  136.5 1.5 %collective-permute-done.25 = bf16[64,1024]{1,0:T(8,128)(2,1)S(1)} collective-permute-done((bf16[64,1024]{1,0:T(8,128)(2,1)S(1)}, bf16[64,1024]{1,0:T(8,128)(2,1)S(1)}, u32[]{:S(2)}, u32[]{:S(2)}) %collective-permute-start.25) | collective-permute-done | bytes 131104 | tf_op jit(solution)/shard_map/ppermute | solution.py:25
  138.0 1.9 %collective-permute-done.26 = bf16[64,1024]{1,0:T(8,128)(2,1)S(1)} collective-permute-done((bf16[64,1024]{1,0:T(8,128)(2,1)S(1)}, bf16[64,1024]{1,0:T(8,128)(2,1)S(1)}, u32[]{:S(2)}, u32[]{:S(2)}) %collective-permute-start.26) | collective-permute-done | bytes 131104 | tf_op jit(solution)/shard_map/ppermute | solution.py:25
  139.9 1.6 %collective-permute-done.27 = bf16[64,1024]{1,0:T(8,128)(2,1)S(1)} collective-permute-done((bf16[64,1024]{1,0:T(8,128)(2,1)S(1)}, bf16[64,1024]{1,0:T(8,128)(2,1)S(1)}, u32[]{:S(2)}, u32[]{:S(2)}) %collective-permute-start.27) | collective-permute-done | bytes 131104 | tf_op jit(solution)/shard_map/ppermute | solution.py:25
  141.5 3.7 %collective-permute-start.28 = (bf16[256,1024]{1,0:T(8,128)(2,1)S(1)}, bf16[256,1024]{1,0:T(8,128)(2,1)S(1)}, u32[]{:S(2)}, u32[]{:S(2)}) collective-permute-start(bf16[256,1024]{1,0:T(8,128)(2,1)S(1)} %bitcast.73), channel_id=1, source_target_pairs={{0,1},{1,0},{2,3},{3,2},{4,5},{5,4},{6,7},{7,6},{8,9},{9,8},{10,11... | collective-permute-start | bytes 1572872 | tf_op jit(solution)/shard_map/ppermute | solution.py:29
  145.2 0.1 broadcast_in_dim.57
  145.4 1.3 collective-permute-done.28
  146.7 0.8 constant_dynamic-update-slice_fusion.1
  (58 shorter events, 0.9 us)
Async XLA Ops:
  1.2 3.0 %copy-start.5 = (f32[8,3328]{1,0:T(8,128)S(1)}, f32[8,3328]{1,0:T(8,128)}, u32[]{:S(2)}) copy-start(f32[8,3328]{1,0:T(8,128)} %param.9) | copy-start | bytes 319492
  8.4 10.2 %slice-start = ((s8[6815744]{0:T(1024)(128)(4,1)}), s8[4194304]{0:T(1024)(128)(4,1)S(1)}, s32[]{:S(2)}) async-start(s8[6815744]{0:T(1024)(128)(4,1)} %bitcast.66), calls=%async_computation | async-start | bytes 8388608
  8.4 10.2 %slice-start.1 = ((s8[6815744]{0:T(1024)(128)(4,1)}), s8[2621440]{0:T(1024)(128)(4,1)S(1)}, s32[]{:S(2)}) async-start(s8[6815744]{0:T(1024)(128)(4,1)} %bitcast.66), calls=%async_computation.1 | async-start | bytes 5242880
  14.0 4.6 %copy-start.1 = (bf16[512,3328]{1,0:T(8,128)(2,1)}, bf16[512,3328]{1,0:T(8,128)(2,1)S(1)}, u32[]{:S(2)}) copy-start(bf16[512,3328]{1,0:T(8,128)(2,1)S(1)} %convolution_convert_fusion.1) | copy-start | bytes 10223620
  14.0 4.6 %copy-start.6 = (f32[8,3328]{1,0:T(8,128)S(1)}, f32[8,3328]{1,0:T(8,128)}, u32[]{:S(2)}) copy-start(f32[8,3328]{1,0:T(8,128)} %param.11) | copy-start | bytes 319492
  15.3 13.2 %collective-permute-start.1 = (bf16[128,3328]{1,0:T(8,128)(2,1)}, bf16[128,3328]{1,0:T(8,128)(2,1)S(1)}, u32[]{:S(2)}, u32[]{:S(2)}) collective-permute-start(bf16[128,3328]{1,0:T(8,128)(2,1)} %get-tuple-element.10), channel_id=1, source_target_pairs={{0,24},{1,97},{8,0},{9,105},{16,8},{17,113},{24,16},{25,121},{32,5... | collective-permute-start | bytes 2555912 | tf_op jit(solution)/shard_map/ppermute | solution.py:21
  18.6 22.7 %collective-permute-start = (bf16[128,3328]{1,0:T(8,128)(2,1)}, bf16[128,3328]{1,0:T(8,128)(2,1)}, u32[]{:S(2)}, u32[]{:S(2)}) collective-permute-start(bf16[128,3328]{1,0:T(8,128)(2,1)} %get-tuple-element.9), channel_id=1, source_target_pairs={{0,8},{1,33},{8,16},{9,41},{16,24},{17,49},{24,0},{25,57},{32,40},... | collective-permute-start | bytes 2555912 | tf_op jit(solution)/shard_map/ppermute | solution.py:21
  25.4 3.2 %copy-start.2 = (bf16[512,3328]{1,0:T(8,128)(2,1)S(1)}, bf16[512,3328]{1,0:T(8,128)(2,1)}, u32[]{:S(2)}) copy-start(bf16[512,3328]{1,0:T(8,128)(2,1)} %copy-done.1) | copy-start | bytes 10223620
  25.5 15.5 %collective-permute-start.6 = (bf16[128,3328]{1,0:T(8,128)(2,1)S(1)}, bf16[128,3328]{1,0:T(8,128)(2,1)S(1)}, u32[]{:S(2)}, u32[]{:S(2)}) collective-permute-start(bf16[128,3328]{1,0:T(8,128)(2,1)S(1)} %get-tuple-element.11), channel_id=1, source_target_pairs={{0,8},{1,33},{8,16},{9,41},{16,24},{17,49},{24,0},{25,57},{32,40},... | collective-permute-start | bytes 2555912 | tf_op jit(solution)/shard_map/ppermute | solution.py:21
  26.4 25.1 %collective-permute-start.8 = (bf16[128,3328]{1,0:T(8,128)(2,1)S(1)}, bf16[128,3328]{1,0:T(8,128)(2,1)S(1)}, u32[]{:S(2)}, u32[]{:S(2)}) collective-permute-start(bf16[128,3328]{1,0:T(8,128)(2,1)S(1)} %get-tuple-element.12), channel_id=1, source_target_pairs={{0,24},{1,97},{8,0},{9,105},{16,8},{17,113},{24,16},{25,121},{32,5... | collective-permute-start | bytes 2555912 | tf_op jit(solution)/shard_map/ppermute | solution.py:21
  28.8 18.5 %collective-permute-start.2 = (bf16[128,3328]{1,0:T(8,128)(2,1)S(1)}, bf16[128,3328]{1,0:T(8,128)(2,1)S(1)}, u32[]{:S(2)}, u32[]{:S(2)}) collective-permute-start(bf16[128,3328]{1,0:T(8,128)(2,1)S(1)} %add_convert_fusion.3), channel_id=1, source_target_pairs={{0,24},{1,97},{8,0},{9,105},{16,8},{17,113},{24,16},{25,121},{32,5... | collective-permute-start | bytes 2555912 | tf_op jit(solution)/shard_map/ppermute | solution.py:21
  41.2 13.1 %collective-permute-start.7 = (bf16[128,3328]{1,0:T(8,128)(2,1)S(1)}, bf16[128,3328]{1,0:T(8,128)(2,1)S(1)}, u32[]{:S(2)}, u32[]{:S(2)}) collective-permute-start(bf16[128,3328]{1,0:T(8,128)(2,1)S(1)} %add_convert_fusion.1), channel_id=1, source_target_pairs={{0,8},{1,33},{8,16},{9,41},{16,24},{17,49},{24,0},{25,57},{32,40},... | collective-permute-start | bytes 2555912 | tf_op jit(solution)/shard_map/ppermute | solution.py:21
  48.9 8.6 %collective-permute-start.4 = (bf16[32,3328]{1,0:T(8,128)(2,1)S(1)}, bf16[32,3328]{1,0:T(8,128)(2,1)S(1)}, u32[]{:S(2)}, u32[]{:S(2)}) collective-permute-start(bf16[32,3328]{1,0:T(8,128)(2,1)S(1)} %get-tuple-element.16), channel_id=1, source_target_pairs={{0,96},{1,25},{8,104},{9,1},{16,112},{17,9},{24,120},{25,17},{32,0... | collective-permute-start | bytes 638984 | tf_op jit(solution)/shard_map/ppermute | solution.py:21
  51.4 16.8 %copy-start.4 = (f32[26,1024]{1,0:T(8,128)S(1)}, f32[26,1024]{1,0:T(8,128)}, u32[]{:S(2)}) copy-start(f32[26,1024]{1,0:T(8,128)} %param.13) | copy-start | bytes 319492
  51.4 9.4 %collective-permute-start.3 = (bf16[32,3328]{1,0:T(8,128)(2,1)S(1)}, bf16[32,3328]{1,0:T(8,128)(2,1)S(1)}, u32[]{:S(2)}, u32[]{:S(2)}) collective-permute-start(bf16[32,3328]{1,0:T(8,128)(2,1)S(1)} %get-tuple-element.15), channel_id=1, source_target_pairs={{0,32},{1,9},{8,40},{9,17},{16,48},{17,25},{24,56},{25,1},{32,64},... | collective-permute-start | bytes 638984 | tf_op jit(solution)/shard_map/ppermute | solution.py:21
  54.7 6.0 %collective-permute-start.9 = (bf16[32,3328]{1,0:T(8,128)(2,1)S(1)}, bf16[32,3328]{1,0:T(8,128)(2,1)S(1)}, u32[]{:S(2)}, u32[]{:S(2)}) collective-permute-start(bf16[32,3328]{1,0:T(8,128)(2,1)S(1)} %get-tuple-element.17), channel_id=1, source_target_pairs={{0,32},{1,9},{8,40},{9,17},{16,48},{17,25},{24,56},{25,1},{32,64},... | collective-permute-start | bytes 638984 | tf_op jit(solution)/shard_map/ppermute | solution.py:21
  55.4 5.4 %collective-permute-start.11 = (bf16[32,3328]{1,0:T(8,128)(2,1)S(1)}, bf16[32,3328]{1,0:T(8,128)(2,1)S(1)}, u32[]{:S(2)}, u32[]{:S(2)}) collective-permute-start(bf16[32,3328]{1,0:T(8,128)(2,1)S(1)} %get-tuple-element.18), channel_id=1, source_target_pairs={{0,96},{1,25},{8,104},{9,1},{16,112},{17,9},{24,120},{25,17},{32,0... | collective-permute-start | bytes 638984 | tf_op jit(solution)/shard_map/ppermute | solution.py:21
  57.5 5.2 %collective-permute-start.5 = (bf16[32,3328]{1,0:T(8,128)(2,1)S(1)}, bf16[32,3328]{1,0:T(8,128)(2,1)S(1)}, u32[]{:S(2)}, u32[]{:S(2)}) collective-permute-start(bf16[32,3328]{1,0:T(8,128)(2,1)S(1)} %add_convert_fusion.6), channel_id=1, source_target_pairs={{0,96},{1,25},{8,104},{9,1},{16,112},{17,9},{24,120},{25,17},{32,0... | collective-permute-start | bytes 638984 | tf_op jit(solution)/shard_map/ppermute | solution.py:21
  60.7 6.1 %collective-permute-start.10 = (bf16[32,3328]{1,0:T(8,128)(2,1)S(1)}, bf16[32,3328]{1,0:T(8,128)(2,1)}, u32[]{:S(2)}, u32[]{:S(2)}) collective-permute-start(bf16[32,3328]{1,0:T(8,128)(2,1)S(1)} %add_convert_fusion.5), channel_id=1, source_target_pairs={{0,32},{1,9},{8,40},{9,17},{16,48},{17,25},{24,56},{25,1},{32,64},... | collective-permute-start | bytes 638984 | tf_op jit(solution)/shard_map/ppermute | solution.py:21
  68.0 9.3 %collective-permute-start.12 = (bf16[32,3328]{1,0:T(8,128)(2,1)S(1)}, bf16[32,3328]{1,0:T(8,128)(2,1)S(1)}, u32[]{:S(2)}, u32[]{:S(2)}) collective-permute-start(bf16[32,3328]{1,0:T(8,128)(2,1)S(1)} %get-tuple-element.8), channel_id=1, source_target_pairs={{0,96},{1,25},{8,104},{9,1},{16,112},{17,9},{24,120},{25,17},{32,0... | collective-permute-start | bytes 638984 | tf_op jit(solution)/shard_map/ppermute | solution.py:21
  76.0 6.3 %collective-permute-start.13 = (bf16[32,3328]{1,0:T(8,128)(2,1)S(1)}, bf16[32,3328]{1,0:T(8,128)(2,1)S(1)}, u32[]{:S(2)}, u32[]{:S(2)}) collective-permute-start(bf16[32,3328]{1,0:T(8,128)(2,1)S(1)} %get-tuple-element.8), channel_id=1, source_target_pairs={{0,64},{1,17},{8,72},{9,25},{16,80},{17,1},{24,88},{25,9},{32,96},... | collective-permute-start | bytes 638984 | tf_op jit(solution)/shard_map/ppermute | solution.py:21
  76.6 7.9 %collective-permute-start.14 = (bf16[32,3328]{1,0:T(8,128)(2,1)S(1)}, bf16[32,3328]{1,0:T(8,128)(2,1)S(1)}, u32[]{:S(2)}, u32[]{:S(2)}) collective-permute-start(bf16[32,3328]{1,0:T(8,128)(2,1)S(1)} %get-tuple-element.8), channel_id=1, source_target_pairs={{0,32},{1,9},{8,40},{9,17},{16,48},{17,25},{24,56},{25,1},{32,64},... | collective-permute-start | bytes 638984 | tf_op jit(solution)/shard_map/ppermute | solution.py:21
  84.5 16.3 %collective-permute-start.16 = (bf16[64,3328]{1,0:T(8,128)(2,1)S(1)}, bf16[64,3328]{1,0:T(8,128)(2,1)S(1)}, u32[]{:S(2)}, u32[]{:S(2)}) collective-permute-start(bf16[64,3328]{1,0:T(8,128)(2,1)S(1)} %bitcast.79), channel_id=1, source_target_pairs={{0,24},{1,97},{8,0},{9,105},{16,8},{17,113},{24,16},{25,121},{32,5... | collective-permute-start | bytes 1277960 | tf_op jit(solution)/shard_map/ppermute | solution.py:21
  87.8 13.1 %collective-permute-start.18 = (bf16[64,3328]{1,0:T(8,128)(2,1)S(1)}, bf16[64,3328]{1,0:T(8,128)(2,1)S(1)}, u32[]{:S(2)}, u32[]{:S(2)}) collective-permute-start(bf16[64,3328]{1,0:T(8,128)(2,1)S(1)} %bitcast.80), channel_id=1, source_target_pairs={{0,8},{1,33},{8,16},{9,41},{16,24},{17,49},{24,0},{25,57},{32,40},... | collective-permute-start | bytes 1277960 | tf_op jit(solution)/shard_map/ppermute | solution.py:21
  87.8 9.6 %collective-permute-start.15 = (bf16[64,3328]{1,0:T(8,128)(2,1)S(1)}, bf16[64,3328]{1,0:T(8,128)(2,1)S(1)}, u32[]{:S(2)}, u32[]{:S(2)}) collective-permute-start(bf16[64,3328]{1,0:T(8,128)(2,1)S(1)} %bitcast.77), channel_id=1, source_target_pairs={{0,24},{1,97},{8,0},{9,105},{16,8},{17,113},{24,16},{25,121},{32,5... | collective-permute-start | bytes 1277960 | tf_op jit(solution)/shard_map/ppermute | solution.py:21
  90.5 18.6 %collective-permute-start.20 = (bf16[64,3328]{1,0:T(8,128)(2,1)S(1)}, bf16[64,3328]{1,0:T(8,128)(2,1)S(1)}, u32[]{:S(2)}, u32[]{:S(2)}) collective-permute-start(bf16[64,3328]{1,0:T(8,128)(2,1)S(1)} %bitcast.78), channel_id=1, source_target_pairs={{0,8},{1,33},{8,16},{9,41},{16,24},{17,49},{24,0},{25,57},{32,40},... | collective-permute-start | bytes 1277960 | tf_op jit(solution)/shard_map/ppermute | solution.py:21
  90.7 18.5 %copy-start = (bf16[3328,1024]{1,0:T(8,128)(2,1)S(1)}, bf16[3328,1024]{1,0:T(8,128)(2,1)}, u32[]{:S(2)}) copy-start(bf16[3328,1024]{1,0:T(8,128)(2,1)} %fusion) | copy-start | bytes 20447236
  97.4 8.5 %collective-permute-start.17 = (bf16[64,3328]{1,0:T(8,128)(2,1)S(1)}, bf16[64,3328]{1,0:T(8,128)(2,1)S(1)}, u32[]{:S(2)}, u32[]{:S(2)}) collective-permute-start(bf16[64,3328]{1,0:T(8,128)(2,1)S(1)} %collective-permute-done.15), channel_id=1, source_target_pairs={{0,24},{1,97},{8,0},{9,105},{16,8},{17,113},{24,16},{25,121},{32,5... | collective-permute-start | bytes 1277960 | tf_op jit(solution)/shard_map/ppermute | solution.py:21
  100.8 8.2 %collective-permute-start.19 = (bf16[64,3328]{1,0:T(8,128)(2,1)S(1)}, bf16[64,3328]{1,0:T(8,128)(2,1)S(1)}, u32[]{:S(2)}, u32[]{:S(2)}) collective-permute-start(bf16[64,3328]{1,0:T(8,128)(2,1)S(1)} %collective-permute-done.18), channel_id=1, source_target_pairs={{0,8},{1,33},{8,16},{9,41},{16,24},{17,49},{24,0},{25,57},{32,40},... | collective-permute-start | bytes 1277960 | tf_op jit(solution)/shard_map/ppermute | solution.py:21
  112.9 8.8 %collective-permute-start.21 = (bf16[256,1024]{1,0:T(8,128)(2,1)S(1)}, bf16[256,1024]{1,0:T(8,128)(2,1)S(1)}, u32[]{:S(2)}, u32[]{:S(2)}) collective-permute-start(bf16[256,1024]{1,0:T(8,128)(2,1)S(1)} %constant_dynamic-slice_fusion), channel_id=1, source_target_pairs={{0,1},{1,0},{2,3},{3,2},{4,5},{5,4},{6,7},{7,6},{8,9},{9,8},{10,11... | collective-permute-start | bytes 1572872 | tf_op jit(solution)/shard_map/ppermute | solution.py:29
  122.0 7.4 %collective-permute-start.22 = (bf16[64,1024]{1,0:T(8,128)(2,1)S(1)}, bf16[64,1024]{1,0:T(8,128)(2,1)S(1)}, u32[]{:S(2)}, u32[]{:S(2)}) collective-permute-start(bf16[64,1024]{1,0:T(8,128)(2,1)S(1)} %get-tuple-element.19), channel_id=1, source_target_pairs={{0,2},{2,4},{4,6},{6,0},{1,3},{3,5},{5,7},{7,1},{8,10},{10,12},{12... | collective-permute-start | bytes 393224 | tf_op jit(solution)/shard_map/ppermute | solution.py:25
  123.7 5.7 %collective-permute-start.23 = (bf16[64,1024]{1,0:T(8,128)(2,1)S(1)}, bf16[64,1024]{1,0:T(8,128)(2,1)S(1)}, u32[]{:S(2)}, u32[]{:S(2)}) collective-permute-start(bf16[64,1024]{1,0:T(8,128)(2,1)S(1)} %get-tuple-element.21), channel_id=1, source_target_pairs={{0,6},{2,0},{4,2},{6,4},{1,7},{3,1},{5,3},{7,5},{8,14},{10,8},{12,... | collective-permute-start | bytes 393224 | tf_op jit(solution)/shard_map/ppermute | solution.py:25
  125.9 7.2 %collective-permute-start.24 = (bf16[64,1024]{1,0:T(8,128)(2,1)S(1)}, bf16[64,1024]{1,0:T(8,128)(2,1)S(1)}, u32[]{:S(2)}, u32[]{:S(2)}) collective-permute-start(bf16[64,1024]{1,0:T(8,128)(2,1)S(1)} %get-tuple-element.20), channel_id=1, source_target_pairs={{0,4},{2,6},{4,0},{6,2},{1,5},{3,7},{5,1},{7,3},{8,12},{10,14},{12... | collective-permute-start | bytes 393224 | tf_op jit(solution)/shard_map/ppermute | solution.py:25
  134.1 3.9 %collective-permute-start.25 = (bf16[64,1024]{1,0:T(8,128)(2,1)S(1)}, bf16[64,1024]{1,0:T(8,128)(2,1)S(1)}, u32[]{:S(2)}, u32[]{:S(2)}) collective-permute-start(bf16[64,1024]{1,0:T(8,128)(2,1)S(1)} %get-tuple-element.6), channel_id=1, source_target_pairs={{0,6},{2,0},{4,2},{6,4},{1,7},{3,1},{5,3},{7,5},{8,14},{10,8},{12,... | collective-permute-start | bytes 393224 | tf_op jit(solution)/shard_map/ppermute | solution.py:25
  134.6 5.3 %collective-permute-start.26 = (bf16[64,1024]{1,0:T(8,128)(2,1)S(1)}, bf16[64,1024]{1,0:T(8,128)(2,1)S(1)}, u32[]{:S(2)}, u32[]{:S(2)}) collective-permute-start(bf16[64,1024]{1,0:T(8,128)(2,1)S(1)} %get-tuple-element.6), channel_id=1, source_target_pairs={{0,4},{2,6},{4,0},{6,2},{1,5},{3,7},{5,1},{7,3},{8,12},{10,14},{12... | collective-permute-start | bytes 393224 | tf_op jit(solution)/shard_map/ppermute | solution.py:25
  136.5 5.0 %collective-permute-start.27 = (bf16[64,1024]{1,0:T(8,128)(2,1)S(1)}, bf16[64,1024]{1,0:T(8,128)(2,1)S(1)}, u32[]{:S(2)}, u32[]{:S(2)}) collective-permute-start(bf16[64,1024]{1,0:T(8,128)(2,1)S(1)} %get-tuple-element.6), channel_id=1, source_target_pairs={{0,2},{2,4},{4,6},{6,0},{1,3},{3,5},{5,7},{7,1},{8,10},{10,12},{12... | collective-permute-start | bytes 393224 | tf_op jit(solution)/shard_map/ppermute | solution.py:25
  141.5 5.2 %collective-permute-start.28 = (bf16[256,1024]{1,0:T(8,128)(2,1)S(1)}, bf16[256,1024]{1,0:T(8,128)(2,1)S(1)}, u32[]{:S(2)}, u32[]{:S(2)}) collective-permute-start(bf16[256,1024]{1,0:T(8,128)(2,1)S(1)} %bitcast.73), channel_id=1, source_target_pairs={{0,1},{1,0},{2,3},{3,2},{4,5},{5,4},{6,7},{7,6},{8,9},{9,8},{10,11... | collective-permute-start | bytes 1572872 | tf_op jit(solution)/shard_map/ppermute | solution.py:29
  145.4 1.4 copy-start.3

commit v2 on v1

v2 whole, which is shorter than its diff:
```python
import functools

import jax
import jax.numpy as jnp
from jax import lax
from jax.experimental import pallas as pl
from jax.experimental.pallas import tpu as pltpu
from jax.sharding import Mesh, PartitionSpec as P

BLOCK = 128
SIDE = 4
TILES = (512, 896, 896, 1024)
DOWN_TILE = 512
PARTS = ((0, 0, 1), (0, 1, 3), (1, 0, 1), (1, 1, 3), (2, 0, 2), (2, 2, 2), (3, 0, 1), (3, 1, 3))
PLANE = ("y", "x", "core")


def hop(array, which, shift):
    pairs = []
    for y in range(SIDE):
        for x in range(SIDE):
            for c in range(2):
                if (c + which) % 2 == 0:
                    to = (y, (x + shift) % SIDE)
                else:
                    to = ((y + shift) % SIDE, x)
                pairs.append(((y * SIDE + x) * 2 + c, (to[0] * SIDE + to[1]) * 2 + c))
    return lax.ppermute(array, PLANE, pairs)


def hop_z(array, shift):
    return lax.ppermute(array, "z", [(i, (i + shift) % SIDE) for i in range(SIDE)])


def other_core(array):
    return lax.ppermute(array, "core", [(0, 1), (1, 0)])


def total(*terms):
    out = terms[0].astype(jnp.float32)
    for t in terms[1:]:
        out = out + t.astype(jnp.float32)
    return out


def rounded(*terms):
    return total(*terms).astype(jnp.bfloat16)


def weights(codes, scales):
    depth, columns = codes.shape
    groups = depth // BLOCK
    blocks = codes.astype(jnp.float32).reshape(groups, BLOCK, columns)
    return (blocks * scales[:, None, :]).reshape(depth, columns).astype(jnp.bfloat16)


def up_kernel(piece, place, states, gate_codes, gate_scales, up_codes, up_scales, *rest):
    outs, (turned, code_buf, scale_buf, out_buf, row_sem, code_sem, scale_sem, out_sem) = rest[:5], rest[5:]
    columns = gate_codes.shape[1]
    own, low1, top3, plus, minus = outs
    q = SIDE * piece
    half = q // 2
    targets = (
        (own, 0, q),
        (plus, half, half),
        (low1, 0, half),
        (minus, 0, half),
        (plus, 0, half),
        (top3, 0, half),
        (minus, half, half),
    )
    tiles = []
    for width in TILES:
        tiles.append((sum(w for _, w in tiles), width))
    jobs = [(m, at, width) for at, width in tiles for m in range(2)]

    def copy_codes(n):
        m, at, width = jobs[n]
        source = (gate_codes, up_codes)[m]
        return pltpu.make_async_copy(
            source.at[:, pl.ds(at, width)], code_buf.at[m, :, pl.ds(at, width)], code_sem.at[n]
        )

    def copy_rows(k):
        block = lax.rem(place[0] + k // SIDE, SIDE) * SIDE + lax.rem(place[1] + k % SIDE, SIDE)
        start = pl.multiple_of(block * piece, piece)
        return pltpu.make_async_copy(
            states.at[pl.ds(start, piece), :], turned.at[pl.ds(k * piece, piece), :], row_sem.at[k]
        )

    def copy_out(n, t):
        m, at, width = jobs[n]
        ref, start, size = targets[t]
        row = sum(size for _, _, size in targets[:t])
        return pltpu.make_async_copy(
            out_buf.at[m, pl.ds(row, size), pl.ds(at, width)],
            ref.at[pl.ds(start, size), pl.ds(m * columns + at, width)],
            out_sem.at[n, t],
        )

    copy_scales = [
        pltpu.make_async_copy(ref, scale_buf.at[m], scale_sem.at[m]) for m, ref in enumerate((gate_scales, up_scales))
    ]
    for k in range(SIDE * SIDE):
        copy_rows(k).start()
    for copy in copy_scales:
        copy.start()
    for n in range(len(jobs)):
        copy_codes(n).start()
    for k in range(SIDE * SIDE):
        copy_rows(k).wait()
    for copy in copy_scales:
        copy.wait()
    for n, (m, at, width) in enumerate(jobs):
        copy_codes(n).wait()
        w = weights(code_buf[m, :, at : at + width], scale_buf[m, :, at : at + width])
        part = jnp.dot(turned[...], w, preferred_element_type=jnp.float32)
        out_buf[m, :, at : at + width] = part.astype(jnp.bfloat16)
        for t in range(len(targets)):
            copy_out(n, t).start()
    for n in range(len(jobs)):
        for t in range(len(targets)):
            copy_out(n, t).wait()


def partial_sums(place, states, gate_codes, gate_scales, up_codes, up_scales):
    rows, width = states.shape
    columns = gate_codes.shape[1]
    q = rows // SIDE
    anywhere = pl.BlockSpec(memory_space=pl.ANY)
    return pl.pallas_call(
        functools.partial(up_kernel, q // SIDE),
        out_shape=tuple(jax.ShapeDtypeStruct((n, 2 * columns), jnp.bfloat16) for n in (q, q // 2, q // 2, q, q)),
        in_specs=[pl.BlockSpec(memory_space=pltpu.SMEM)] + [anywhere] * 5,
        out_specs=(anywhere,) * 5,
        scratch_shapes=[
            pltpu.VMEM((rows, width), jnp.bfloat16),
            pltpu.VMEM((2, width, columns), jnp.bfloat16),
            pltpu.VMEM((2, *gate_scales.shape), jnp.float32),
            pltpu.VMEM((2, rows, columns), jnp.bfloat16),
            pltpu.SemaphoreType.DMA((SIDE * SIDE,)),
            pltpu.SemaphoreType.DMA((2 * len(TILES),)),
            pltpu.SemaphoreType.DMA((2,)),
            pltpu.SemaphoreType.DMA((2 * len(TILES), 7)),
        ],
        compiler_params=pltpu.CompilerParams(vmem_limit_bytes=60 * 1024 * 1024),
        cost_estimate=pl.CostEstimate(
            flops=4 * rows * width * columns,
            bytes_accessed=4 * width * columns + 4 * rows * columns,
            transcendentals=0,
        ),
        name="partial_sums",
    )(place, states, gate_codes, gate_scales, up_codes, up_scales)


def down_kernel(piece, place, *rest):
    parts, (codes, scales, mine, theirs, act) = rest[:8], rest[8:]
    for (a, b, count), part in zip(PARTS, parts):
        for k in range(count):
            block = lax.rem(place[0] + a, SIDE) * SIDE + lax.rem(place[1] + b + k, SIDE)
            swap = lax.rem(lax.div(block, 2 * SIDE) + place[3], 2)
            ahead = lax.rem(lax.div(lax.rem(block, 2 * SIDE), 2) + SIDE - place[2], SIDE)
            at = (swap * SIDE + ahead) * 2 + lax.rem(block, 2)
            act[pl.ds(pl.multiple_of(at * piece, piece), piece), :] = part[k * piece : (k + 1) * piece, :]
    width = codes.shape[1]
    half = act.shape[0] // 2
    for at in range(0, width, DOWN_TILE):
        tile = slice(at, at + DOWN_TILE)
        out = jnp.dot(act[...], weights(codes[:, tile], scales[:, tile]), preferred_element_type=jnp.float32)
        out = out.astype(jnp.bfloat16)
        theirs[:, :, tile] = out[half:].reshape(SIDE, half // SIDE, DOWN_TILE)
        mine[:, :, tile] = out[:half].reshape(SIDE, half // SIDE, DOWN_TILE)


def down_sums(place, parts, codes, scales):
    depth, width = codes.shape
    rows = sum(p.shape[0] for p in parts)
    piece = rows // (SIDE * SIDE)
    vmem = pl.BlockSpec(memory_space=pltpu.VMEM)
    shape = jax.ShapeDtypeStruct((SIDE, rows // 2 // SIDE, width), jnp.bfloat16)
    return pl.pallas_call(
        functools.partial(down_kernel, piece),
        out_shape=(shape, shape),
        in_specs=[pl.BlockSpec(memory_space=pltpu.SMEM)] + [vmem] * 10,
        out_specs=(vmem, vmem),
        scratch_shapes=[pltpu.VMEM((rows, depth), jnp.bfloat16)],
        compiler_params=pltpu.CompilerParams(vmem_limit_bytes=24 * 1024 * 1024),
        cost_estimate=pl.CostEstimate(
            flops=2 * rows * depth * width, bytes_accessed=2 * (depth * width + rows * depth), transcendentals=0
        ),
        name="down_sums",
    )(place, *parts, codes, scales)


def sent_along_first(parts):
    own, low1, top3, plus, minus = parts
    half = own.shape[0] // 2
    plus = hop(plus, 0, 1)
    minus = hop(minus, 0, -1)
    sum_low = hop(rounded(low1, plus[:half]), 0, 1)
    sum_top = hop(rounded(top3, minus[:half]), 0, -1)
    top = rounded(own[:half], plus[half:], sum_top)
    low = rounded(own[half:], sum_low, minus[half:])
    piece = half // 2
    return top[:piece], top[piece:], low[:piece], low[piece:]


def sent_along_second(parts):
    return total(parts[0], hop(parts[1], 1, 1), hop(parts[3], 1, -1), hop(parts[2], 1, 2))


def body(states, gate_codes, gate_scales, up_codes, up_scales, down_codes, down_scales):
    rows, width = states.shape
    columns = gate_codes.shape[1]
    core = lax.axis_index("core")
    ix, iy, iz = lax.axis_index("x"), lax.axis_index("y"), lax.axis_index("z")
    first = jnp.where(core == 0, ix, iy)
    second = jnp.where(core == 0, iy, ix)
    place = jnp.stack([first, second, iz, core]).astype(jnp.int32)
    piece = rows // (SIDE * SIDE)

    parts = partial_sums(place, states, gate_codes, gate_scales, up_codes, up_scales)
    both = sent_along_second(sent_along_first(parts))
    gate, up = both[:, :columns], both[:, columns:]
    act = (jax.nn.silu(gate) * up).astype(jnp.bfloat16)

    side = jnp.concatenate([hop(act, 1, -1), hop(act, 1, 2), hop(act, 1, 1)], 0)
    ahead, behind = hop(act, 0, -1), hop(act, 0, 1)
    ahead_side, behind_side = hop(side, 0, -1), hop(side, 0, 1)
    ahead, behind, ahead_side, behind_side = lax.optimization_barrier((ahead, behind, ahead_side, behind_side))
    far01 = hop(jnp.concatenate([ahead, ahead_side[:piece]], 0), 0, -1)
    far23 = hop(behind_side[piece:], 0, 1)
    parts = (act, side, ahead, ahead_side, far01, far23, behind, behind_side)

    mine, theirs = down_sums(place, parts, down_codes, down_scales)
    both = rounded(mine, other_core(theirs))
    half = rows // 2
    share = half // SIDE
    got = total(both[0], hop_z(both[1], 1), hop_z(both[3], -1), hop_z(both[2], 2))
    residual = lax.dynamic_slice_in_dim(states, core * half + iz * share, share, 0)
    done = rounded(got, residual)
    mine = jnp.stack([done, hop_z(done, -1), hop_z(done, 2), hop_z(done, 1)])
    theirs = other_core(mine)
    out = jnp.zeros((2, SIDE, share, width), jnp.bfloat16)
    for k in range(SIDE):
        out = lax.dynamic_update_slice(out, mine[k][None, None], (core, (iz + k) % SIDE, 0, 0))
    for k in range(SIDE):
        out = lax.dynamic_update_slice(out, theirs[k][None, None], (1 - core, (iz + k) % SIDE, 0, 0))
    return out.reshape(rows, width)


def solution(mesh):
    grid = Mesh(mesh.devices.reshape(SIDE, SIDE, SIDE, 2), ("y", "x", "z", "core"))
    mp, hidden = ("y", "x"), ("z", "core")
    in_specs = (
        P(None, mp),
        P(mp, hidden),
        P(mp, hidden),
        P(mp, hidden),
        P(mp, hidden),
        P(hidden, mp),
        P(hidden, mp),
    )
    return jax.shard_map(body, mesh=grid, in_specs=in_specs, out_specs=P(None, mp), check_vma=False)
```

time: 148 us -> 146 us (0.986)
  Pallas kernels: 0 us -> 20.8 us
  waiting for transfers between devices: 61.6 us -> 80.9 us
  other arithmetic: 20.9 us -> 4.43 us
  matrix products: 14.7 us -> 0 us
  starting transfers between devices: 45.3 us -> 37.7 us
  local copies, waits for them, and re-layouts: 4.59 us -> 1.43 us
    pallas_call x0 -> x2, Pallas kernels: none -> 20.8 us  [the longest x1 16.2 us: partial_sums(): pl.pallas_call(functools.partial(up_kernel, q // SIDE), out_shape=tuple((...]
    ppermute x21 -> x16, waiting for transfers between devices: 47.8 us -> 67 us  [hop(): return lax.ppermute(array, PLANE, pairs)]
    dot_general x3 -> x0, matrix products: 14.7 us -> none  [the longest x1 5.58 us: body(): jnp.dot(turned, gate_w, preferred_element_type=jnp.float32)]
    convert_element_type x10 -> x5, other arithmetic: 15.8 us -> 2.51 us  [the longest x4 2.38 us: rounded(): return total(*terms).astype(jnp.bfloat16)]
    ppermute x21 -> x16, starting transfers between devices: 26.9 us -> 18.7 us  [hop(): return lax.ppermute(array, PLANE, pairs)]
    concatenate x2 -> x1, other arithmetic: 2.92 us -> 0.03 us  [body(): far01 = hop(jnp.concatenate([ahead, ahead_side[:piece]], 0), 0, -1)]
    slice x7 -> x4, local copies, waits for them, and re-layouts: 2.77 us -> 0.13 us  [the longest x2 0.09 us: sent_along_first(): return (top[:piece], top[piece:], low[:piece], low[piece:])]
  transfers between devices with their start and end apart: 29 -> 24, of which waited for: 19 -> 18; matrix products, arithmetic and copies ran while one was open for 12% -> 1% of each run, Pallas kernels for 0% -> 0%
where the time goes in v2:
time: 146 us
  waiting for transfers between devices  80.9 us (55%)
  starting transfers between devices  37.7 us (26%)
  Pallas kernels  20.8 us (14%)
  other arithmetic  4.43 us (3%)
    ppermute x16, waiting for transfers between devices, hop(): return lax.ppermute(array, PLANE, pairs)  67 us
    ppermute x16, starting transfers between devices, hop(): return lax.ppermute(array, PLANE, pairs)  18.7 us
    pallas_call x1, Pallas kernels, partial_sums(): pl.pallas_call(functools.partial(up_kernel, q // SIDE), out_shape=tuple((...  16.2 us
    ppermute x2, starting transfers between devices, other_core(): return lax.ppermute(array, 'core', [(0, 1), (1, 0)])  11.5 us
    ppermute x6, waiting for transfers between devices, hop_z(): lax.ppermute(array, 'z', [(i, (i + shift) % SIDE) for i in range(SIDE)])  10.9 us
    ppermute x6, starting transfers between devices, hop_z(): lax.ppermute(array, 'z', [(i, (i + shift) % SIDE) for i in range(SIDE)])  7.54 us
    pallas_call x1, Pallas kernels, down_sums(): pl.pallas_call(functools.partial(down_kernel, piece), out_shape=(shape, s...  4.57 us
    ppermute x2, waiting for transfers between devices, other_core(): return lax.ppermute(array, 'core', [(0, 1), (1, 0)])  3.01 us
  transfers between devices with their start and end apart: 24, of which 18 were waited for; matrix products, arithmetic and copies ran while one was open for 1% of the time, Pallas kernels for 0%

profile of v2, /device:TPU:1, one launch (start us, length us, event | category | flops | bytes accessed | tf_op | source)
XLA Modules:
  0.0 145.5 jit_solution(17025576593516033160)
XLA Ops:
  0.0 0.6 pad_add_fusion.place
  0.6 16.2 %partial_sums.1 = (bf16[128,6656]{1,0:T(8,128)(2,1)}, bf16[64,6656]{1,0:T(8,128)(2,1)}, bf16[64,6656]{1,0:T(8,128)(2,1)}, bf16[128,6656]{1,0:T(8,128)(2,1)}, bf16[128,6656]{1,0:T(8,128)(2,1)}) custom-call(s32[4]{0:T(128)} %pad_add_fusion.place, bf16[512,1024]{1,0:T(8,128)(2,1)} %states.1, bf16[1024,3328]{1,0:T(8,128)(2,1)} %gate_codes.1, ...), custom_call_target="tpu_custom_call" | custom-call | flops 6979321856 | bytes 20447232 | tf_op jit(solution)/shard_map/partial_sums/pallas_call | solution.py:131
  16.9 2.2 %collective-permute-start = (bf16[128,6656]{1,0:T(8,128)(2,1)}, bf16[128,6656]{1,0:T(8,128)(2,1)S(1)}, u32[]{:S(2)}, u32[]{:S(2)}) collective-permute-start(bf16[128,6656]{1,0:T(8,128)(2,1)} %get-tuple-element.17), channel_id=1, source_target_pairs={{0,8},{1,33},{8,16},{9,41},{16,24},{17,49},{24,0},{25,57},{32,40},... | collective-permute-start | bytes 5111816 | tf_op jit(solution)/shard_map/ppermute | solution.py:28
  19.1 1.5 %collective-permute-start.1 = (bf16[128,6656]{1,0:T(8,128)(2,1)}, bf16[128,6656]{1,0:T(8,128)(2,1)S(1)}, u32[]{:S(2)}, u32[]{:S(2)}) collective-permute-start(bf16[128,6656]{1,0:T(8,128)(2,1)} %get-tuple-element.19), channel_id=1, source_target_pairs={{0,24},{1,97},{8,0},{9,105},{16,8},{17,113},{24,16},{25,121},{32,5... | collective-permute-start | bytes 5111816 | tf_op jit(solution)/shard_map/ppermute | solution.py:28
  20.6 19.6 %collective-permute-done = bf16[128,6656]{1,0:T(8,128)(2,1)S(1)} collective-permute-done((bf16[128,6656]{1,0:T(8,128)(2,1)}, bf16[128,6656]{1,0:T(8,128)(2,1)S(1)}, u32[]{:S(2)}, u32[]{:S(2)}) %collective-permute-start) | collective-permute-done | bytes 1703968 | tf_op jit(solution)/shard_map/ppermute | solution.py:28
  40.2 1.4 add_convert_fusion.1
  41.6 0.1 collective-permute-start.4
  41.7 0.0 collective-permute-done.1
  41.7 0.2 add_convert_fusion.3
  41.9 2.7 %collective-permute-start.2 = (bf16[64,6656]{1,0:T(8,128)(2,1)S(1)}, bf16[64,6656]{1,0:T(8,128)(2,1)S(1)}, u32[]{:S(2)}, u32[]{:S(2)}) collective-permute-start(bf16[64,6656]{1,0:T(8,128)(2,1)S(1)} %add_convert_fusion.3), channel_id=1, source_target_pairs={{0,24},{1,97},{8,0},{9,105},{16,8},{17,113},{24,16},{25,121},{32,5... | collective-permute-start | bytes 2555912 | tf_op jit(solution)/shard_map/ppermute | solution.py:28
  44.6 10.1 %collective-permute-done.4 = bf16[64,6656]{1,0:T(8,128)(2,1)S(1)} collective-permute-done((bf16[64,6656]{1,0:T(8,128)(2,1)S(1)}, bf16[64,6656]{1,0:T(8,128)(2,1)S(1)}, u32[]{:S(2)}, u32[]{:S(2)}) %collective-permute-start.4) | collective-permute-done | bytes 852000 | tf_op jit(solution)/shard_map/ppermute | solution.py:28
  54.7 0.0 collective-permute-done.2
  54.7 0.6 add_convert_fusion.2
  55.3 0.0 slice-start.1
  55.4 0.1 fusion.10
  55.4 2.6 %collective-permute-start.5 = (bf16[32,6656]{1,0:T(8,128)(2,1)S(1)}, bf16[32,6656]{1,0:T(8,128)(2,1)S(1)}, u32[]{:S(2)}, u32[]{:S(2)}) collective-permute-start(bf16[32,6656]{1,0:T(8,128)(2,1)S(1)} %get-tuple-element.31), channel_id=1, source_target_pairs={{0,96},{1,25},{8,104},{9,1},{16,112},{17,9},{24,120},{25,17},{32,0... | collective-permute-start | bytes 1277960 | tf_op jit(solution)/shard_map/ppermute | solution.py:28
  58.0 0.0 collective-permute-start.6
  58.0 0.7 collective-permute-start.3
  58.8 8.9 %collective-permute-done.5 = bf16[32,6656]{1,0:T(8,128)(2,1)S(1)} collective-permute-done((bf16[32,6656]{1,0:T(8,128)(2,1)S(1)}, bf16[32,6656]{1,0:T(8,128)(2,1)S(1)}, u32[]{:S(2)}, u32[]{:S(2)}) %collective-permute-start.5) | collective-permute-done | bytes 426016 | tf_op jit(solution)/shard_map/ppermute | solution.py:28
  67.6 0.0 collective-permute-done.6
  67.6 3.5 %collective-permute-done.3 = bf16[32,6656]{1,0:T(8,128)(2,1)S(1)} collective-permute-done((bf16[32,6656]{1,0:T(8,128)(2,1)S(1)}, bf16[32,6656]{1,0:T(8,128)(2,1)S(1)}, u32[]{:S(2)}, u32[]{:S(2)}) %collective-permute-start.3) | collective-permute-done | bytes 426016 | tf_op jit(solution)/shard_map/ppermute | solution.py:28
  71.1 0.2 convert_add_fusion
  71.3 0.1 fusion.rest_0_
  71.5 0.0 copy-start.1
  71.5 0.6 collective-permute-start.7
  72.1 0.0 collective-permute-start.8
  72.1 0.9 collective-permute-start.9
  73.0 3.2 %collective-permute-done.7 = bf16[32,3328]{1,0:T(8,128)(2,1)S(1)} collective-permute-done((bf16[32,3328]{1,0:T(8,128)(2,1)S(1)}, bf16[32,3328]{1,0:T(8,128)(2,1)S(1)}, u32[]{:S(2)}, u32[]{:S(2)}) %collective-permute-start.7) | collective-permute-done | bytes 213024 | tf_op jit(solution)/shard_map/ppermute | solution.py:28
  76.3 2.1 %collective-permute-done.8 = bf16[32,3328]{1,0:T(8,128)(2,1)S(1)} collective-permute-done((bf16[32,3328]{1,0:T(8,128)(2,1)S(1)}, bf16[32,3328]{1,0:T(8,128)(2,1)S(1)}, u32[]{:S(2)}, u32[]{:S(2)}) %collective-permute-start.8) | collective-permute-done | bytes 213024 | tf_op jit(solution)/shard_map/ppermute | solution.py:28
  78.4 2.5 %collective-permute-done.9 = bf16[32,3328]{1,0:T(8,128)(2,1)S(1)} collective-permute-done((bf16[32,3328]{1,0:T(8,128)(2,1)S(1)}, bf16[32,3328]{1,0:T(8,128)(2,1)S(1)}, u32[]{:S(2)}, u32[]{:S(2)}) %collective-permute-start.9) | collective-permute-done | bytes 213024 | tf_op jit(solution)/shard_map/ppermute | solution.py:28
  80.9 3.0 %collective-permute-start.12 = (bf16[96,3328]{1,0:T(8,128)(2,1)S(1)}, bf16[96,3328]{1,0:T(8,128)(2,1)S(1)}, u32[]{:S(2)}, u32[]{:S(2)}) collective-permute-start(bf16[96,3328]{1,0:T(8,128)(2,1)S(1)} %constant_dynamic-update-slice_fusion.rest_1_), channel_id=1, source_target_pairs={{0,24},{1,97},{8,0},{9,105},{16,8},{17,113},{24,16},{25,121},{32,5... | collective-permute-start | bytes 1916936 | tf_op jit(solution)/shard_map/ppermute | solution.py:28
  83.9 0.0 collective-permute-start.13
  83.9 2.7 %collective-permute-start.10 = (bf16[32,3328]{1,0:T(8,128)(2,1)S(1)}, bf16[32,3328]{1,0:T(8,128)(2,1)S(1)}, u32[]{:S(2)}, u32[]{:S(2)}) collective-permute-start(bf16[32,3328]{1,0:T(8,128)(2,1)S(1)} %fusion.rest_0_), channel_id=1, source_target_pairs={{0,24},{1,97},{8,0},{9,105},{16,8},{17,113},{24,16},{25,121},{32,5... | collective-permute-start | bytes 638984 | tf_op jit(solution)/shard_map/ppermute | solution.py:28
  86.6 7.0 %collective-permute-done.10.rest_2_ = bf16[32,3328]{1,0:T(8,128)(2,1)S(1)} collective-permute-done((bf16[32,3328]{1,0:T(8,128)(2,1)S(1)}, bf16[32,3328]{1,0:T(8,128)(2,1)S(1)}, u32[]{:S(2)}, u32[]{:S(2)}) %collective-permute-start.10) | collective-permute-done | bytes 213024 | tf_op jit(solution)/shard_map/ppermute | solution.py:28
  93.5 3.4 %collective-permute-done.11.rest_6_ = bf16[32,3328]{1,0:T(8,128)(2,1)S(1)} collective-permute-done((bf16[32,3328]{1,0:T(8,128)(2,1)S(1)}, bf16[32,3328]{1,0:T(8,128)(2,1)S(1)}, u32[]{:S(2)}, u32[]{:S(2)}) %collective-permute-start.11) | collective-permute-done | bytes 213024 | tf_op jit(solution)/shard_map/ppermute | solution.py:28
  97.0 0.0 collective-permute-done.12.rest_3_
  97.0 0.0 collective-permute-done.13.rest_7_
  97.0 0.1 collective-permute-start.14
  97.1 1.5 %collective-permute-start.15 = (bf16[64,3328]{1,0:T(8,128)(2,1)S(1)}, bf16[64,3328]{1,0:T(8,128)(2,1)S(1)}, u32[]{:S(2)}, u32[]{:S(2)}) collective-permute-start(bf16[64,3328]{1,0:T(8,128)(2,1)S(1)} %slice.79), channel_id=1, source_target_pairs={{0,8},{1,33},{8,16},{9,41},{16,24},{17,49},{24,0},{25,57},{32,40},... | collective-permute-start | bytes 1277960 | tf_op jit(solution)/shard_map/ppermute | solution.py:28
  98.7 5.4 %collective-permute-done.14.rest_4_ = bf16[64,3328]{1,0:T(8,128)(2,1)S(1)} collective-permute-done((bf16[64,3328]{1,0:T(8,128)(2,1)S(1)}, bf16[64,3328]{1,0:T(8,128)(2,1)S(1)}, u32[]{:S(2)}, u32[]{:S(2)}) %collective-permute-start.14) | collective-permute-done | bytes 426016 | tf_op jit(solution)/shard_map/ppermute | solution.py:28
  104.1 1.3 collective-permute-done.15.rest_5_
  105.4 4.6 %down_sums.1 = (bf16[4,64,1024]{2,1,0:T(8,128)(2,1)S(1)}, bf16[4,64,1024]{2,1,0:T(8,128)(2,1)S(1)}) custom-call(s32[4]{0:T(128)S(1)} %copy-done, bf16[32,3328]{1,0:T(8,128)(2,1)S(1)} %fusion.rest_0_, bf16[96,3328]{1,0:T(8,128)(2,1)S(1)} %constant_dynamic-update-slice_fusion.rest_1_, bf16[32,3328]{1,0:T(8,128)(2,1)S(1)} %collective-permute-done.10.rest_2_, ...), custom_call_target="tpu_custom_call" | custom-call | flops 3489660928 | bytes 10223616 | tf_op jit(solution)/shard_map/down_sums/pallas_call | solution.py:181
  110.0 7.8 %collective-permute-start.16 = (bf16[4,64,1024]{2,1,0:T(8,128)(2,1)S(1)}, bf16[4,64,1024]{2,1,0:T(8,128)(2,1)S(1)}, u32[]{:S(2)}, u32[]{:S(2)}) collective-permute-start(bf16[4,64,1024]{2,1,0:T(8,128)(2,1)S(1)} %get-tuple-element.26), channel_id=1, source_target_pairs={{0,1},{1,0},{2,3},{3,2},{4,5},{5,4},{6,7},{7,6},{8,9},{9,8},{10,11... | collective-permute-start | bytes 1572872 | tf_op jit(solution)/shard_map/ppermute | solution.py:36
  117.8 1.5 %collective-permute-done.16 = bf16[4,64,1024]{2,1,0:T(8,128)(2,1)S(1)} collective-permute-done((bf16[4,64,1024]{2,1,0:T(8,128)(2,1)S(1)}, bf16[4,64,1024]{2,1,0:T(8,128)(2,1)S(1)}, u32[]{:S(2)}, u32[]{:S(2)}) %collective-permute-start.16) | collective-permute-done | bytes 524320 | tf_op jit(solution)/shard_map/ppermute | solution.py:36
  119.4 0.2 add_convert_fusion.4
  119.6 1.7 %collective-permute-start.17 = (bf16[64,1024]{1,0:T(8,128)(2,1)S(1)}, bf16[64,1024]{1,0:T(8,128)(2,1)S(1)}, u32[]{:S(2)}, u32[]{:S(2)}) collective-permute-start(bf16[64,1024]{1,0:T(8,128)(2,1)S(1)} %get-tuple-element.33), channel_id=1, source_target_pairs={{0,2},{2,4},{4,6},{6,0},{1,3},{3,5},{5,7},{7,1},{8,10},{10,12},{12... | collective-permute-start | bytes 393224 | tf_op jit(solution)/shard_map/ppermute | solution.py:32
  121.3 2.2 %collective-permute-start.18 = (bf16[64,1024]{1,0:T(8,128)(2,1)S(1)}, bf16[64,1024]{1,0:T(8,128)(2,1)S(1)}, u32[]{:S(2)}, u32[]{:S(2)}) collective-permute-start(bf16[64,1024]{1,0:T(8,128)(2,1)S(1)} %get-tuple-element.35), channel_id=1, source_target_pairs={{0,6},{2,0},{4,2},{6,4},{1,7},{3,1},{5,3},{7,5},{8,14},{10,8},{12,... | collective-permute-start | bytes 393224 | tf_op jit(solution)/shard_map/ppermute | solution.py:32
  123.5 1.3 collective-permute-start.19
  124.7 2.2 %collective-permute-done.17 = bf16[64,1024]{1,0:T(8,128)(2,1)S(1)} collective-permute-done((bf16[64,1024]{1,0:T(8,128)(2,1)S(1)}, bf16[64,1024]{1,0:T(8,128)(2,1)S(1)}, u32[]{:S(2)}, u32[]{:S(2)}) %collective-permute-start.17) | collective-permute-done | bytes 131104 | tf_op jit(solution)/shard_map/ppermute | solution.py:32
  127.0 0.0 collective-permute-done.18
  127.0 3.7 %collective-permute-done.19 = bf16[64,1024]{1,0:T(8,128)(2,1)S(1)} collective-permute-done((bf16[64,1024]{1,0:T(8,128)(2,1)S(1)}, bf16[64,1024]{1,0:T(8,128)(2,1)S(1)}, u32[]{:S(2)}, u32[]{:S(2)}) %collective-permute-start.19) | collective-permute-done | bytes 131104 | tf_op jit(solution)/shard_map/ppermute | solution.py:32
  130.6 0.1 broadcast_in_dim.3
  130.7 1.0 bitcast_dynamic-update-slice_fusion.3
  131.8 0.6 collective-permute-start.20
  132.3 1.8 %collective-permute-start.21 = (bf16[64,1024]{1,0:T(8,128)(2,1)S(1)}, bf16[64,1024]{1,0:T(8,128)(2,1)S(1)}, u32[]{:S(2)}, u32[]{:S(2)}) collective-permute-start(bf16[64,1024]{1,0:T(8,128)(2,1)S(1)} %get-tuple-element.28), channel_id=1, source_target_pairs={{0,4},{2,6},{4,0},{6,2},{1,5},{3,7},{5,1},{7,3},{8,12},{10,14},{12... | collective-permute-start | bytes 393224 | tf_op jit(solution)/shard_map/ppermute | solution.py:32
  134.1 0.0 collective-permute-start.22
  134.2 1.5 %collective-permute-done.20 = bf16[64,1024]{1,0:T(8,128)(2,1)S(1)} collective-permute-done((bf16[64,1024]{1,0:T(8,128)(2,1)S(1)}, bf16[64,1024]{1,0:T(8,128)(2,1)S(1)}, u32[]{:S(2)}, u32[]{:S(2)}) %collective-permute-start.20) | collective-permute-done | bytes 131104 | tf_op jit(solution)/shard_map/ppermute | solution.py:32
  135.6 2.0 %collective-permute-done.21 = bf16[64,1024]{1,0:T(8,128)(2,1)S(1)} collective-permute-done((bf16[64,1024]{1,0:T(8,128)(2,1)S(1)}, bf16[64,1024]{1,0:T(8,128)(2,1)S(1)}, u32[]{:S(2)}, u32[]{:S(2)}) %collective-permute-start.21) | collective-permute-done | bytes 131104 | tf_op jit(solution)/shard_map/ppermute | solution.py:32
  137.6 1.5 %collective-permute-done.22 = bf16[64,1024]{1,0:T(8,128)(2,1)S(1)} collective-permute-done((bf16[64,1024]{1,0:T(8,128)(2,1)S(1)}, bf16[64,1024]{1,0:T(8,128)(2,1)S(1)}, u32[]{:S(2)}, u32[]{:S(2)}) %collective-permute-start.22) | collective-permute-done | bytes 131104 | tf_op jit(solution)/shard_map/ppermute | solution.py:32
  139.2 0.1 pad_maximum_fusion
  139.3 3.7 %collective-permute-start.23 = (bf16[4,64,1024]{2,1,0:T(8,128)(2,1)S(1)}, bf16[4,64,1024]{2,1,0:T(8,128)(2,1)S(1)}, u32[]{:S(2)}, u32[]{:S(2)}) collective-permute-start(bf16[4,64,1024]{2,1,0:T(8,128)(2,1)S(1)} %pad_maximum_fusion), channel_id=1, source_target_pairs={{0,1},{1,0},{2,3},{3,2},{4,5},{5,4},{6,7},{7,6},{8,9},{9,8},{10,11... | collective-permute-start | bytes 1572872 | tf_op jit(solution)/shard_map/ppermute | solution.py:36
  143.0 1.5 %collective-permute-done.23 = bf16[4,64,1024]{2,1,0:T(8,128)(2,1)S(1)} collective-permute-done((bf16[4,64,1024]{2,1,0:T(8,128)(2,1)S(1)}, bf16[4,64,1024]{2,1,0:T(8,128)(2,1)S(1)}, u32[]{:S(2)}, u32[]{:S(2)}) %collective-permute-start.23) | collective-permute-done | bytes 524320 | tf_op jit(solution)/shard_map/ppermute | solution.py:36
  144.5 0.0 copy-start.3
  144.6 1.0 copy-done.3
  (27 shorter events, 0.3 us)
Async XLA Ops:
  16.9 24.8 %copy-start.4 = (bf16[64,6656]{1,0:T(8,128)(2,1)S(1)}, bf16[64,6656]{1,0:T(8,128)(2,1)}, u32[]{:S(2)}) copy-start(bf16[64,6656]{1,0:T(8,128)(2,1)} %get-tuple-element.18) | copy-start | bytes 2555908
  16.9 23.3 %collective-permute-start = (bf16[128,6656]{1,0:T(8,128)(2,1)}, bf16[128,6656]{1,0:T(8,128)(2,1)S(1)}, u32[]{:S(2)}, u32[]{:S(2)}) collective-permute-start(bf16[128,6656]{1,0:T(8,128)(2,1)} %get-tuple-element.17), channel_id=1, source_target_pairs={{0,8},{1,33},{8,16},{9,41},{16,24},{17,49},{24,0},{25,57},{32,40},... | collective-permute-start | bytes 5111816 | tf_op jit(solution)/shard_map/ppermute | solution.py:28
  19.1 22.6 %collective-permute-start.1 = (bf16[128,6656]{1,0:T(8,128)(2,1)}, bf16[128,6656]{1,0:T(8,128)(2,1)S(1)}, u32[]{:S(2)}, u32[]{:S(2)}) collective-permute-start(bf16[128,6656]{1,0:T(8,128)(2,1)} %get-tuple-element.19), channel_id=1, source_target_pairs={{0,24},{1,97},{8,0},{9,105},{16,8},{17,113},{24,16},{25,121},{32,5... | collective-permute-start | bytes 5111816 | tf_op jit(solution)/shard_map/ppermute | solution.py:28
  41.6 13.1 %copy-start.2 = (bf16[128,6656]{1,0:T(8,128)(2,1)S(1)}, bf16[128,6656]{1,0:T(8,128)(2,1)}, u32[]{:S(2)}) copy-start(bf16[128,6656]{1,0:T(8,128)(2,1)} %get-tuple-element.16) | copy-start | bytes 5111812
  41.6 13.1 %collective-permute-start.4 = (bf16[64,6656]{1,0:T(8,128)(2,1)S(1)}, bf16[64,6656]{1,0:T(8,128)(2,1)S(1)}, u32[]{:S(2)}, u32[]{:S(2)}) collective-permute-start(bf16[64,6656]{1,0:T(8,128)(2,1)S(1)} %add_convert_fusion.1), channel_id=1, source_target_pairs={{0,8},{1,33},{8,16},{9,41},{16,24},{17,49},{24,0},{25,57},{32,40},... | collective-permute-start | bytes 2555912 | tf_op jit(solution)/shard_map/ppermute | solution.py:28
  41.9 12.8 %collective-permute-start.2 = (bf16[64,6656]{1,0:T(8,128)(2,1)S(1)}, bf16[64,6656]{1,0:T(8,128)(2,1)S(1)}, u32[]{:S(2)}, u32[]{:S(2)}) collective-permute-start(bf16[64,6656]{1,0:T(8,128)(2,1)S(1)} %add_convert_fusion.3), channel_id=1, source_target_pairs={{0,24},{1,97},{8,0},{9,105},{16,8},{17,113},{24,16},{25,121},{32,5... | collective-permute-start | bytes 2555912 | tf_op jit(solution)/shard_map/ppermute | solution.py:28
  54.7 50.7 %slice-start = ((s8[6815744]{0:T(1024)(128)(4,1)}), s8[4194304]{0:T(1024)(128)(4,1)S(1)}, s32[]{:S(2)}) async-start(s8[6815744]{0:T(1024)(128)(4,1)} %bitcast.45), calls=%async_computation | async-start | bytes 8388608
  55.3 50.1 %slice-start.1 = ((s8[6815744]{0:T(1024)(128)(4,1)}), s8[2621440]{0:T(1024)(128)(4,1)S(1)}, s32[]{:S(2)}) async-start(s8[6815744]{0:T(1024)(128)(4,1)} %bitcast.45), calls=%async_computation.1 | async-start | bytes 5242880
  55.4 12.2 %collective-permute-start.5 = (bf16[32,6656]{1,0:T(8,128)(2,1)S(1)}, bf16[32,6656]{1,0:T(8,128)(2,1)S(1)}, u32[]{:S(2)}, u32[]{:S(2)}) collective-permute-start(bf16[32,6656]{1,0:T(8,128)(2,1)S(1)} %get-tuple-element.31), channel_id=1, source_target_pairs={{0,96},{1,25},{8,104},{9,1},{16,112},{17,9},{24,120},{25,17},{32,0... | collective-permute-start | bytes 1277960 | tf_op jit(solution)/shard_map/ppermute | solution.py:28
  58.0 9.6 %collective-permute-start.6 = (bf16[32,6656]{1,0:T(8,128)(2,1)S(1)}, bf16[32,6656]{1,0:T(8,128)(2,1)S(1)}, u32[]{:S(2)}, u32[]{:S(2)}) collective-permute-start(bf16[32,6656]{1,0:T(8,128)(2,1)S(1)} %get-tuple-element.32), channel_id=1, source_target_pairs={{0,64},{1,17},{8,72},{9,25},{16,80},{17,1},{24,88},{25,9},{32,96},... | collective-permute-start | bytes 1277960 | tf_op jit(solution)/shard_map/ppermute | solution.py:28
  58.0 13.1 %collective-permute-start.3 = (bf16[32,6656]{1,0:T(8,128)(2,1)S(1)}, bf16[32,6656]{1,0:T(8,128)(2,1)S(1)}, u32[]{:S(2)}, u32[]{:S(2)}) collective-permute-start(bf16[32,6656]{1,0:T(8,128)(2,1)S(1)} %slice.91), channel_id=1, source_target_pairs={{0,32},{1,9},{8,40},{9,17},{16,48},{17,25},{24,56},{25,1},{32,64},... | collective-permute-start | bytes 1277960 | tf_op jit(solution)/shard_map/ppermute | solution.py:28
  71.5 33.9 %copy-start = (s32[4]{0:T(128)S(1)}, s32[4]{0:T(128)}, u32[]{:S(2)}) copy-start(s32[4]{0:T(128)} %pad_add_fusion.place) | copy-start | bytes 52
  71.5 33.9 %copy-start.1 = (f32[26,1024]{1,0:T(8,128)S(1)}, f32[26,1024]{1,0:T(8,128)}, u32[]{:S(2)}) copy-start(f32[26,1024]{1,0:T(8,128)} %rest_9_.1) | copy-start | bytes 319492
  71.5 4.8 %collective-permute-start.7 = (bf16[32,3328]{1,0:T(8,128)(2,1)S(1)}, bf16[32,3328]{1,0:T(8,128)(2,1)S(1)}, u32[]{:S(2)}, u32[]{:S(2)}) collective-permute-start(bf16[32,3328]{1,0:T(8,128)(2,1)S(1)} %fusion.rest_0_), channel_id=1, source_target_pairs={{0,96},{1,25},{8,104},{9,1},{16,112},{17,9},{24,120},{25,17},{32,0... | collective-permute-start | bytes 638984 | tf_op jit(solution)/shard_map/ppermute | solution.py:28
  72.1 6.3 %collective-permute-start.8 = (bf16[32,3328]{1,0:T(8,128)(2,1)S(1)}, bf16[32,3328]{1,0:T(8,128)(2,1)S(1)}, u32[]{:S(2)}, u32[]{:S(2)}) collective-permute-start(bf16[32,3328]{1,0:T(8,128)(2,1)S(1)} %fusion.rest_0_), channel_id=1, source_target_pairs={{0,64},{1,17},{8,72},{9,25},{16,80},{17,1},{24,88},{25,9},{32,96},... | collective-permute-start | bytes 638984 | tf_op jit(solution)/shard_map/ppermute | solution.py:28
  72.1 8.8 %collective-permute-start.9 = (bf16[32,3328]{1,0:T(8,128)(2,1)S(1)}, bf16[32,3328]{1,0:T(8,128)(2,1)S(1)}, u32[]{:S(2)}, u32[]{:S(2)}) collective-permute-start(bf16[32,3328]{1,0:T(8,128)(2,1)S(1)} %fusion.rest_0_), channel_id=1, source_target_pairs={{0,32},{1,9},{8,40},{9,17},{16,48},{17,25},{24,56},{25,1},{32,64},... | collective-permute-start | bytes 638984 | tf_op jit(solution)/shard_map/ppermute | solution.py:28
  80.9 16.1 %collective-permute-start.12 = (bf16[96,3328]{1,0:T(8,128)(2,1)S(1)}, bf16[96,3328]{1,0:T(8,128)(2,1)S(1)}, u32[]{:S(2)}, u32[]{:S(2)}) collective-permute-start(bf16[96,3328]{1,0:T(8,128)(2,1)S(1)} %constant_dynamic-update-slice_fusion.rest_1_), channel_id=1, source_target_pairs={{0,24},{1,97},{8,0},{9,105},{16,8},{17,113},{24,16},{25,121},{32,5... | collective-permute-start | bytes 1916936 | tf_op jit(solution)/shard_map/ppermute | solution.py:28
  83.9 13.1 %collective-permute-start.13 = (bf16[96,3328]{1,0:T(8,128)(2,1)S(1)}, bf16[96,3328]{1,0:T(8,128)(2,1)S(1)}, u32[]{:S(2)}, u32[]{:S(2)}) collective-permute-start(bf16[96,3328]{1,0:T(8,128)(2,1)S(1)} %constant_dynamic-update-slice_fusion.rest_1_), channel_id=1, source_target_pairs={{0,8},{1,33},{8,16},{9,41},{16,24},{17,49},{24,0},{25,57},{32,40},... | collective-permute-start | bytes 1916936 | tf_op jit(solution)/shard_map/ppermute | solution.py:28
  83.9 9.6 %collective-permute-start.10 = (bf16[32,3328]{1,0:T(8,128)(2,1)S(1)}, bf16[32,3328]{1,0:T(8,128)(2,1)S(1)}, u32[]{:S(2)}, u32[]{:S(2)}) collective-permute-start(bf16[32,3328]{1,0:T(8,128)(2,1)S(1)} %fusion.rest_0_), channel_id=1, source_target_pairs={{0,24},{1,97},{8,0},{9,105},{16,8},{17,113},{24,16},{25,121},{32,5... | collective-permute-start | bytes 638984 | tf_op jit(solution)/shard_map/ppermute | solution.py:28
  86.6 10.4 %collective-permute-start.11 = (bf16[32,3328]{1,0:T(8,128)(2,1)S(1)}, bf16[32,3328]{1,0:T(8,128)(2,1)S(1)}, u32[]{:S(2)}, u32[]{:S(2)}) collective-permute-start(bf16[32,3328]{1,0:T(8,128)(2,1)S(1)} %fusion.rest_0_), channel_id=1, source_target_pairs={{0,8},{1,33},{8,16},{9,41},{16,24},{17,49},{24,0},{25,57},{32,40},... | collective-permute-start | bytes 638984 | tf_op jit(solution)/shard_map/ppermute | solution.py:28
  97.0 7.0 %collective-permute-start.14 = (bf16[64,3328]{1,0:T(8,128)(2,1)S(1)}, bf16[64,3328]{1,0:T(8,128)(2,1)S(1)}, u32[]{:S(2)}, u32[]{:S(2)}) collective-permute-start(bf16[64,3328]{1,0:T(8,128)(2,1)S(1)} %pad_maximum_fusion.1), channel_id=1, source_target_pairs={{0,24},{1,97},{8,0},{9,105},{16,8},{17,113},{24,16},{25,121},{32,5... | collective-permute-start | bytes 1277960 | tf_op jit(solution)/shard_map/ppermute | solution.py:28
  97.1 8.3 %collective-permute-start.15 = (bf16[64,3328]{1,0:T(8,128)(2,1)S(1)}, bf16[64,3328]{1,0:T(8,128)(2,1)S(1)}, u32[]{:S(2)}, u32[]{:S(2)}) collective-permute-start(bf16[64,3328]{1,0:T(8,128)(2,1)S(1)} %slice.79), channel_id=1, source_target_pairs={{0,8},{1,33},{8,16},{9,41},{16,24},{17,49},{24,0},{25,57},{32,40},... | collective-permute-start | bytes 1277960 | tf_op jit(solution)/shard_map/ppermute | solution.py:28
  110.0 9.4 %collective-permute-start.16 = (bf16[4,64,1024]{2,1,0:T(8,128)(2,1)S(1)}, bf16[4,64,1024]{2,1,0:T(8,128)(2,1)S(1)}, u32[]{:S(2)}, u32[]{:S(2)}) collective-permute-start(bf16[4,64,1024]{2,1,0:T(8,128)(2,1)S(1)} %get-tuple-element.26), channel_id=1, source_target_pairs={{0,1},{1,0},{2,3},{3,2},{4,5},{5,4},{6,7},{7,6},{8,9},{9,8},{10,11... | collective-permute-start | bytes 1572872 | tf_op jit(solution)/shard_map/ppermute | solution.py:36
  119.6 7.4 %collective-permute-start.17 = (bf16[64,1024]{1,0:T(8,128)(2,1)S(1)}, bf16[64,1024]{1,0:T(8,128)(2,1)S(1)}, u32[]{:S(2)}, u32[]{:S(2)}) collective-permute-start(bf16[64,1024]{1,0:T(8,128)(2,1)S(1)} %get-tuple-element.33), channel_id=1, source_target_pairs={{0,2},{2,4},{4,6},{6,0},{1,3},{3,5},{5,7},{7,1},{8,10},{10,12},{12... | collective-permute-start | bytes 393224 | tf_op jit(solution)/shard_map/ppermute | solution.py:32
  121.3 5.7 %collective-permute-start.18 = (bf16[64,1024]{1,0:T(8,128)(2,1)S(1)}, bf16[64,1024]{1,0:T(8,128)(2,1)S(1)}, u32[]{:S(2)}, u32[]{:S(2)}) collective-permute-start(bf16[64,1024]{1,0:T(8,128)(2,1)S(1)} %get-tuple-element.35), channel_id=1, source_target_pairs={{0,6},{2,0},{4,2},{6,4},{1,7},{3,1},{5,3},{7,5},{8,14},{10,8},{12,... | collective-permute-start | bytes 393224 | tf_op jit(solution)/shard_map/ppermute | solution.py:32
  123.5 7.2 %collective-permute-start.19 = (bf16[64,1024]{1,0:T(8,128)(2,1)S(1)}, bf16[64,1024]{1,0:T(8,128)(2,1)S(1)}, u32[]{:S(2)}, u32[]{:S(2)}) collective-permute-start(bf16[64,1024]{1,0:T(8,128)(2,1)S(1)} %get-tuple-element.34), channel_id=1, source_target_pairs={{0,4},{2,6},{4,0},{6,2},{1,5},{3,7},{5,1},{7,3},{8,12},{10,14},{12... | collective-permute-start | bytes 393224 | tf_op jit(solution)/shard_map/ppermute | solution.py:32
  131.8 3.9 %collective-permute-start.20 = (bf16[64,1024]{1,0:T(8,128)(2,1)S(1)}, bf16[64,1024]{1,0:T(8,128)(2,1)S(1)}, u32[]{:S(2)}, u32[]{:S(2)}) collective-permute-start(bf16[64,1024]{1,0:T(8,128)(2,1)S(1)} %get-tuple-element.28), channel_id=1, source_target_pairs={{0,6},{2,0},{4,2},{6,4},{1,7},{3,1},{5,3},{7,5},{8,14},{10,8},{12,... | collective-permute-start | bytes 393224 | tf_op jit(solution)/shard_map/ppermute | solution.py:32
  132.3 5.3 %collective-permute-start.21 = (bf16[64,1024]{1,0:T(8,128)(2,1)S(1)}, bf16[64,1024]{1,0:T(8,128)(2,1)S(1)}, u32[]{:S(2)}, u32[]{:S(2)}) collective-permute-start(bf16[64,1024]{1,0:T(8,128)(2,1)S(1)} %get-tuple-element.28), channel_id=1, source_target_pairs={{0,4},{2,6},{4,0},{6,2},{1,5},{3,7},{5,1},{7,3},{8,12},{10,14},{12... | collective-permute-start | bytes 393224 | tf_op jit(solution)/shard_map/ppermute | solution.py:32
  134.1 5.0 %collective-permute-start.22 = (bf16[64,1024]{1,0:T(8,128)(2,1)S(1)}, bf16[64,1024]{1,0:T(8,128)(2,1)S(1)}, u32[]{:S(2)}, u32[]{:S(2)}) collective-permute-start(bf16[64,1024]{1,0:T(8,128)(2,1)S(1)} %get-tuple-element.28), channel_id=1, source_target_pairs={{0,2},{2,4},{4,6},{6,0},{1,3},{3,5},{5,7},{7,1},{8,10},{10,12},{12... | collective-permute-start | bytes 393224 | tf_op jit(solution)/shard_map/ppermute | solution.py:32
  139.3 5.2 %collective-permute-start.23 = (bf16[4,64,1024]{2,1,0:T(8,128)(2,1)S(1)}, bf16[4,64,1024]{2,1,0:T(8,128)(2,1)S(1)}, u32[]{:S(2)}, u32[]{:S(2)}) collective-permute-start(bf16[4,64,1024]{2,1,0:T(8,128)(2,1)S(1)} %pad_maximum_fusion), channel_id=1, source_target_pairs={{0,1},{1,0},{2,3},{3,2},{4,5},{5,4},{6,7},{7,6},{8,9},{9,8},{10,11... | collective-permute-start | bytes 1572872 | tf_op jit(solution)/shard_map/ppermute | solution.py:36
  144.5 1.0 copy-start.3

commit v3 on v2

v3 whole, which is shorter than its diff:
```python
import functools

import jax
import jax.numpy as jnp
from jax import lax
from jax.experimental import pallas as pl
from jax.experimental.pallas import tpu as pltpu
from jax.sharding import Mesh, PartitionSpec as P

BLOCK = 128
SIDE = 4
TILES = (512, 896, 896, 1024)
DEPTH = 2
DOWN_TILE = 512
PARTS = ((0, 0, 4), (1, 0, 4), (2, 0, 4), (3, 0, 4))
PLANE = ("y", "x", "core")


def hop(array, which, shift):
    pairs = []
    for y in range(SIDE):
        for x in range(SIDE):
            for c in range(2):
                if (c + which) % 2 == 0:
                    to = (y, (x + shift) % SIDE)
                else:
                    to = ((y + shift) % SIDE, x)
                pairs.append(((y * SIDE + x) * 2 + c, (to[0] * SIDE + to[1]) * 2 + c))
    return lax.ppermute(array, PLANE, pairs)


def hop_z(array, shift):
    return lax.ppermute(array, "z", [(i, (i + shift) % SIDE) for i in range(SIDE)])


def other_core(array):
    return lax.ppermute(array, "core", [(0, 1), (1, 0)])


def total(*terms):
    out = terms[0].astype(jnp.float32)
    for t in terms[1:]:
        out = out + t.astype(jnp.float32)
    return out


def rounded(*terms):
    return total(*terms).astype(jnp.bfloat16)


def weights(codes, scales):
    depth, columns = codes.shape
    groups = depth // BLOCK
    blocks = codes.astype(jnp.float32).reshape(groups, BLOCK, columns)
    return (blocks * scales[:, None, :]).reshape(depth, columns).astype(jnp.bfloat16)


def places():
    x, y, z, core = (lax.axis_index(name) for name in ("x", "y", "z", "core"))
    return jnp.where(core == 0, x, y), jnp.where(core == 0, y, x), z, core


def up_kernel(piece, halves, ends, states, gate_codes, gate_scales, up_codes, up_scales, *rest):
    outs, rest = rest[: len(ends)], rest[len(ends) :]
    turned, code_buf, scale_buf, out_buf, row_sem, code_sem, scale_sem, out_sem = rest
    place = places()
    columns = gate_codes.shape[1]
    size = 2 * piece
    tiles = []
    for width in TILES:
        tiles.append((sum(w for _, w in tiles), width))
    jobs = [(m, at, width) for at, width in tiles for m in range(2)]
    blocks = [(a, 2 * h + k) for a, h in halves for k in range(2)]

    def copy_codes(n):
        m, at, width = jobs[n]
        source = (gate_codes, up_codes)[m]
        return pltpu.make_async_copy(
            source.at[:, pl.ds(at, width)], code_buf.at[m, :, pl.ds(at, width)], code_sem.at[n]
        )

    def copy_rows(k):
        a, b = blocks[k]
        block = lax.rem(place[0] + a, SIDE) * SIDE + lax.rem(place[1] + b, SIDE)
        start = pl.multiple_of(block * piece, piece)
        return pltpu.make_async_copy(
            states.at[pl.ds(start, piece), :], turned.at[pl.ds(k * piece, piece), :], row_sem.at[k]
        )

    def copy_out(n, t):
        m, at, width = jobs[n]
        row = sum(ends[:t])
        return pltpu.make_async_copy(
            out_buf.at[m, pl.ds(row * size, ends[t] * size), pl.ds(at, width)],
            outs[t].at[:, pl.ds(m * columns + at, width)],
            out_sem.at[n, t],
        )

    copy_scales = [
        pltpu.make_async_copy(ref, scale_buf.at[m], scale_sem.at[m]) for m, ref in enumerate((gate_scales, up_scales))
    ]
    for k in range(len(blocks)):
        copy_rows(k).start()
    for copy in copy_scales:
        copy.start()
    for n in range(DEPTH):
        copy_codes(n).start()
    for k in range(len(blocks)):
        copy_rows(k).wait()
    for copy in copy_scales:
        copy.wait()
    for n, (m, at, width) in enumerate(jobs):
        copy_codes(n).wait()
        if n + DEPTH < len(jobs):
            copy_codes(n + DEPTH).start()
        w = weights(code_buf[m, :, at : at + width], scale_buf[m, :, at : at + width])
        part = jnp.dot(turned[...], w, preferred_element_type=jnp.float32)
        out_buf[m, :, at : at + width] = part.astype(jnp.bfloat16)
        for t in range(len(ends)):
            copy_out(n, t).start()
    for n in range(len(jobs)):
        for t in range(len(ends)):
            copy_out(n, t).wait()


def partial_sums(halves, ends, states, gate_codes, gate_scales, up_codes, up_scales):
    width = states.shape[1]
    columns = gate_codes.shape[1]
    piece = states.shape[0] // (SIDE * SIDE)
    rows = 2 * piece * len(halves)
    anywhere = pl.BlockSpec(memory_space=pl.ANY)
    return pl.pallas_call(
        functools.partial(up_kernel, piece, halves, ends),
        out_shape=tuple(jax.ShapeDtypeStruct((2 * piece * n, 2 * columns), jnp.bfloat16) for n in ends),
        in_specs=[anywhere] * 5,
        out_specs=(anywhere,) * len(ends),
        scratch_shapes=[
            pltpu.VMEM((rows, width), jnp.bfloat16),
            pltpu.VMEM((2, width, columns), jnp.bfloat16),
            pltpu.VMEM((2, *gate_scales.shape), jnp.float32),
            pltpu.VMEM((2, rows, columns), jnp.bfloat16),
            pltpu.SemaphoreType.DMA((2 * len(halves),)),
            pltpu.SemaphoreType.DMA((2 * len(TILES),)),
            pltpu.SemaphoreType.DMA((2,)),
            pltpu.SemaphoreType.DMA((2 * len(TILES), len(ends))),
        ],
        compiler_params=pltpu.CompilerParams(vmem_limit_bytes=60 * 1024 * 1024),
        cost_estimate=pl.CostEstimate(
            flops=4 * rows * width * columns,
            bytes_accessed=4 * width * columns + 4 * rows * columns,
            transcendentals=0,
        ),
        name="partial_sums",
    )(states, gate_codes, gate_scales, up_codes, up_scales)


def fetch_kernel(codes, scales, out, code_buf, scale_buf, sem):
    depth = 2 * BLOCK
    count = codes.shape[0] // depth

    def copy(n):
        at = pl.ds(n * depth, depth)
        return pltpu.make_async_copy(codes.at[at, :], code_buf.at[at, :], sem.at[n])

    copy_scales = pltpu.make_async_copy(scales, scale_buf, sem.at[count])
    copy_scales.start()
    for n in range(count):
        copy(n).start()
    copy_scales.wait()
    for n in range(count):
        copy(n).wait()
        at = slice(n * depth, (n + 1) * depth)
        out[at, :] = weights(code_buf[at, :], scale_buf[2 * n : 2 * n + 2, :])


def fetched_weights(codes, scales):
    anywhere = pl.BlockSpec(memory_space=pl.ANY)
    return pl.pallas_call(
        fetch_kernel,
        out_shape=jax.ShapeDtypeStruct(codes.shape, jnp.bfloat16),
        in_specs=[anywhere, anywhere],
        out_specs=pl.BlockSpec(memory_space=pltpu.VMEM),
        scratch_shapes=[
            pltpu.VMEM(codes.shape, codes.dtype),
            pltpu.VMEM(scales.shape, scales.dtype),
            pltpu.SemaphoreType.DMA((codes.shape[0] // BLOCK // 2 + 1,)),
        ],
        compiler_params=pltpu.CompilerParams(vmem_limit_bytes=16 * 1024 * 1024),
        cost_estimate=pl.CostEstimate(flops=codes.size, bytes_accessed=2 * codes.size, transcendentals=0),
        name="fetched_weights",
    )(codes, scales)


def down_kernel(piece, *rest):
    parts, (down_w, mine, theirs, act) = rest[:4], rest[4:]
    place = places()
    for (a, b, count), part in zip(PARTS, parts):
        for k in range(count):
            block = lax.rem(place[0] + a, SIDE) * SIDE + lax.rem(place[1] + b + k, SIDE)
            swap = lax.rem(lax.div(block, 2 * SIDE) + place[3], 2)
            ahead = lax.rem(lax.div(lax.rem(block, 2 * SIDE), 2) + SIDE - place[2], SIDE)
            at = (swap * SIDE + ahead) * 2 + lax.rem(block, 2)
            act[pl.ds(pl.multiple_of(at * piece, piece), piece), :] = part[k * piece : (k + 1) * piece, :]
    width = down_w.shape[1]
    half = act.shape[0] // 2
    for at in range(0, width, DOWN_TILE):
        tile = slice(at, at + DOWN_TILE)
        out = jnp.dot(act[...], down_w[:, tile], preferred_element_type=jnp.float32)
        out = out.astype(jnp.bfloat16)
        theirs[:, :, tile] = out[half:].reshape(SIDE, half // SIDE, DOWN_TILE)
        mine[:, :, tile] = out[:half].reshape(SIDE, half // SIDE, DOWN_TILE)


def down_sums(parts, down_w):
    depth, width = down_w.shape
    rows = sum(p.shape[0] for p in parts)
    piece = rows // (SIDE * SIDE)
    vmem = pl.BlockSpec(memory_space=pltpu.VMEM)
    shape = jax.ShapeDtypeStruct((SIDE, rows // 2 // SIDE, width), jnp.bfloat16)
    return pl.pallas_call(
        functools.partial(down_kernel, piece),
        out_shape=(shape, shape),
        in_specs=[vmem] * 5,
        out_specs=(vmem, vmem),
        scratch_shapes=[pltpu.VMEM((rows, depth), jnp.bfloat16)],
        compiler_params=pltpu.CompilerParams(vmem_limit_bytes=24 * 1024 * 1024),
        cost_estimate=pl.CostEstimate(
            flops=2 * rows * depth * width, bytes_accessed=2 * (depth * width + rows * depth), transcendentals=0
        ),
        name="down_sums",
    )(*parts, down_w)


def sent_along_second(parts):
    return total(parts[0], hop(parts[1], 1, 1), hop(parts[3], 1, -1), hop(parts[2], 1, 2))


def body(states, gate_codes, gate_scales, up_codes, up_scales, down_codes, down_scales):
    rows, width = states.shape
    columns = gate_codes.shape[1]
    core = lax.axis_index("core")
    iz = lax.axis_index("z")
    piece = rows // (SIDE * SIDE)

    sums = functools.partial(partial_sums, states=states, gate_codes=gate_codes)
    sums = functools.partial(sums, gate_scales=gate_scales, up_codes=up_codes, up_scales=up_scales)
    top2, low2 = sums(((2, 0), (2, 1)), (1, 1))
    passed_low, passed_top = hop(low2, 0, 1), hop(top2, 0, -1)
    top1, low1, top3, low3, own = sums(((1, 0), (1, 1), (3, 0), (3, 1), (0, 0), (0, 1)), (1, 1, 1, 1, 2))
    plus = jnp.concatenate([top1, rounded(low1, passed_low)], 0)
    minus = jnp.concatenate([rounded(top3, passed_top), low3], 0)
    plus, minus = hop(plus, 0, 1), hop(minus, 0, -1)
    line = rounded(own, plus, minus)
    line = [line[k * piece : (k + 1) * piece] for k in range(SIDE)]
    both = sent_along_second(line)
    gate, up = both[:, :columns], both[:, columns:]
    act = (jax.nn.silu(gate) * up).astype(jnp.bfloat16)

    line = jnp.concatenate([act, hop(act, 1, -1), hop(act, 1, 2), hop(act, 1, 1)], 0)
    residual = lax.dynamic_slice_in_dim(states, core * (rows // 2) + iz * (rows // 8), rows // 8, 0)
    line, residual, down_codes, down_scales = lax.optimization_barrier((line, residual, down_codes, down_scales))
    down_w = fetched_weights(down_codes, down_scales)
    parts = (line, hop(line, 0, -1), hop(line, 0, 2), hop(line, 0, 1))

    mine, theirs = down_sums(parts, down_w)
    both = rounded(mine, other_core(theirs))
    half = rows // 2
    share = half // SIDE
    got = total(both[0], hop_z(both[1], 1), hop_z(both[3], -1), hop_z(both[2], 2))
    done = lax.optimization_barrier(rounded(got, residual))
    mine = jnp.stack([done, hop_z(done, -1), hop_z(done, 2), hop_z(done, 1)])
    theirs = other_core(mine)
    out = jnp.zeros((2, SIDE, share, width), jnp.bfloat16)
    for k in range(SIDE):
        out = lax.dynamic_update_slice(out, mine[k][None, None], (core, (iz + k) % SIDE, 0, 0))
    for k in range(SIDE):
        out = lax.dynamic_update_slice(out, theirs[k][None, None], (1 - core, (iz + k) % SIDE, 0, 0))
    return out.reshape(rows, width)


def solution(mesh):
    grid = Mesh(mesh.devices.reshape(SIDE, SIDE, SIDE, 2), ("y", "x", "z", "core"))
    mp, hidden = ("y", "x"), ("z", "core")
    in_specs = (
        P(None, mp),
        P(mp, hidden),
        P(mp, hidden),
        P(mp, hidden),
        P(mp, hidden),
        P(hidden, mp),
        P(hidden, mp),
    )
    return jax.shard_map(body, mesh=grid, in_specs=in_specs, out_specs=P(None, mp), check_vma=False)
```

time: 146 us -> 134 us (0.918)
  waiting for transfers between devices: 80.9 us -> 67.7 us
  starting transfers between devices: 37.7 us -> 31.4 us
  local copies, waits for them, and re-layouts: 1.43 us -> 6.18 us
  Pallas kernels: 20.8 us -> 25.3 us
    ppermute x16 -> x13, waiting for transfers between devices: 67 us -> 52.6 us  [hop(): return lax.ppermute(array, PLANE, pairs)]
    pallas_call x1 -> x3, Pallas kernels: 16.2 us -> 21.3 us  [the longest x2 19.4 us: partial_sums(): pl.pallas_call(functools.partial(up_kernel, piece, halves, ends), out_sha...]
    ppermute x2, starting transfers between devices: 11.5 us -> 6.8 us  [other_core(): return lax.ppermute(array, 'core', [(0, 1), (1, 0)])]
    unnamed x16 -> x14, local copies, waits for them, and re-layouts: 1.02 us -> 4.9 us
    ppermute x16 -> x13, starting transfers between devices: 18.7 us -> 16.4 us  [hop(): return lax.ppermute(array, PLANE, pairs)]
  transfers between devices with their start and end apart: 24 -> 21, of which waited for: 18 -> 15; matrix products, arithmetic and copies ran while one was open for 1% -> 2% of each run, Pallas kernels for 0% -> 9%
where the time goes in v3:
time: 134 us
  waiting for transfers between devices  67.7 us (51%)
  starting transfers between devices  31.4 us (23%)
  Pallas kernels  25.3 us (19%)
  local copies, waits for them, and re-layouts  6.18 us (5%)
  other arithmetic  3.2 us (2%)
    ppermute x13, waiting for transfers between devices, hop(): return lax.ppermute(array, PLANE, pairs)  52.6 us
    pallas_call x2, Pallas kernels, partial_sums(): pl.pallas_call(functools.partial(up_kernel, piece, halves, ends), out_sha...  19.4 us
    ppermute x13, starting transfers between devices, hop(): return lax.ppermute(array, PLANE, pairs)  16.4 us
    ppermute x6, waiting for transfers between devices, hop_z(): lax.ppermute(array, 'z', [(i, (i + shift) % SIDE) for i in range(SIDE)])  12.1 us
    ppermute x6, starting transfers between devices, hop_z(): lax.ppermute(array, 'z', [(i, (i + shift) % SIDE) for i in range(SIDE)])  8.22 us
    ppermute x2, starting transfers between devices, other_core(): return lax.ppermute(array, 'core', [(0, 1), (1, 0)])  6.8 us
    unnamed x14, local copies, waits for them, and re-layouts  4.9 us
    pallas_call x1, Pallas kernels, down_sums(): pl.pallas_call(functools.partial(down_kernel, piece), out_shape=(shape, s...  3.94 us
  transfers between devices with their start and end apart: 21, of which 15 were waited for; matrix products, arithmetic and copies ran while one was open for 2% of the time, Pallas kernels for 9%

profile of v3, /device:TPU:1, one launch (start us, length us, event | category | flops | bytes accessed | tf_op | source)
XLA Modules:
  0.0 134.1 jit_solution(1724175511208039207)
XLA Ops:
  0.0 8.8 %partial_sums.3 = (bf16[64,6656]{1,0:T(8,128)(2,1)}, bf16[64,6656]{1,0:T(8,128)(2,1)}) custom-call(bf16[512,1024]{1,0:T(8,128)(2,1)} %states.3, bf16[1024,3328]{1,0:T(8,128)(2,1)} %gate_codes.3, f32[8,3328]{1,0:T(8,128)} %gate_scales.3, bf16[1024,3328]{1,0:T(8,128)(2,1)} %up_codes.3, f32[8,3328]{1,0:T(8,128)} %up_scales.3), custom_call_target="tpu_custom_call" | custom-call | flops 1744830464 | bytes 15335424 | tf_op jit(solution)/shard_map/partial_sums/pallas_call | solution.py:132
  8.8 2.2 %collective-permute-start = (bf16[64,6656]{1,0:T(8,128)(2,1)}, bf16[64,6656]{1,0:T(8,128)(2,1)S(1)}, u32[]{:S(2)}, u32[]{:S(2)}) collective-permute-start(bf16[64,6656]{1,0:T(8,128)(2,1)} %get-tuple-element.21), channel_id=1, source_target_pairs={{0,8},{1,33},{8,16},{9,41},{16,24},{17,49},{24,0},{25,57},{32,40},... | collective-permute-start | bytes 2555912 | tf_op jit(solution)/shard_map/ppermute | solution.py:29
  11.0 1.5 %collective-permute-start.2 = (bf16[64,6656]{1,0:T(8,128)(2,1)}, bf16[64,6656]{1,0:T(8,128)(2,1)S(1)}, u32[]{:S(2)}, u32[]{:S(2)}) collective-permute-start(bf16[64,6656]{1,0:T(8,128)(2,1)} %get-tuple-element.23), channel_id=1, source_target_pairs={{0,24},{1,97},{8,0},{9,105},{16,8},{17,113},{24,16},{25,121},{32,5... | collective-permute-start | bytes 2555912 | tf_op jit(solution)/shard_map/ppermute | solution.py:29
  12.5 10.6 %partial_sums.2 = (bf16[64,6656]{1,0:T(8,128)(2,1)}, bf16[64,6656]{1,0:T(8,128)(2,1)}, bf16[64,6656]{1,0:T(8,128)(2,1)}, bf16[64,6656]{1,0:T(8,128)(2,1)}, bf16[128,6656]{1,0:T(8,128)(2,1)}) custom-call(bf16[512,1024]{1,0:T(8,128)(2,1)} %states.3, bf16[1024,3328]{1,0:T(8,128)(2,1)} %gate_codes.3, f32[8,3328]{1,0:T(8,128)} %gate_scales.3, ...), custom_call_target="tpu_custom_call" | custom-call | flops 5234491392 | bytes 18743296 | tf_op jit(solution)/shard_map/partial_sums/pallas_call | solution.py:132
  23.1 0.0 copy-start.6
  23.2 0.0 collective-permute-done
  23.2 1.4 %add_convert_fusion.2 = bf16[64,6656]{1,0:T(8,128)(2,1)S(1)} fusion(bf16[64,6656]{1,0:T(8,128)(2,1)S(1)} %collective-permute-done, bf16[64,6656]{1,0:T(8,128)(2,1)} %get-tuple-element.20), kind=kLoop, calls=%fused_computation.4 | loop fusion | flops 1703936 | bytes 2555904 | tf_op jit(solution)/shard_map/convert_element_type | solution.py:48
  24.6 0.1 pad_maximum_fusion
  24.7 0.1 collective-permute-start.1
  24.8 0.0 collective-permute-done.2
  24.8 0.9 copy-done.4
  25.8 0.2 add_convert_fusion.1
  26.0 0.1 copy-done.5
  26.0 0.1 pad_maximum_fusion.1
  26.2 1.9 %collective-permute-start.3 = (bf16[128,6656]{1,0:T(8,128)(2,1)S(1)}, bf16[128,6656]{1,0:T(8,128)(2,1)S(1)}, u32[]{:S(2)}, u32[]{:S(2)}) collective-permute-start(bf16[128,6656]{1,0:T(8,128)(2,1)S(1)} %pad_maximum_fusion.1), channel_id=1, source_target_pairs={{0,24},{1,97},{8,0},{9,105},{16,8},{17,113},{24,16},{25,121},{32,5... | collective-permute-start | bytes 5111816 | tf_op jit(solution)/shard_map/ppermute | solution.py:29
  28.1 18.9 %collective-permute-done.1 = bf16[128,6656]{1,0:T(8,128)(2,1)S(1)} collective-permute-done((bf16[128,6656]{1,0:T(8,128)(2,1)S(1)}, bf16[128,6656]{1,0:T(8,128)(2,1)S(1)}, u32[]{:S(2)}, u32[]{:S(2)}) %collective-permute-start.1) | collective-permute-done | bytes 1703968 | tf_op jit(solution)/shard_map/ppermute | solution.py:29
  47.0 0.4 collective-permute-done.3
  47.4 0.6 add_convert_fusion
  48.0 0.1 fusion.9
  48.1 1.3 collective-permute-start.4
  49.4 1.5 %collective-permute-start.5 = (bf16[32,6656]{1,0:T(8,128)(2,1)S(1)}, bf16[32,6656]{1,0:T(8,128)(2,1)S(1)}, u32[]{:S(2)}, u32[]{:S(2)}) collective-permute-start(bf16[32,6656]{1,0:T(8,128)(2,1)S(1)} %get-tuple-element.33), channel_id=1, source_target_pairs={{0,96},{1,25},{8,104},{9,1},{16,112},{17,9},{24,120},{25,17},{32,0... | collective-permute-start | bytes 1277960 | tf_op jit(solution)/shard_map/ppermute | solution.py:29
  50.8 1.5 %collective-permute-start.6 = (bf16[32,6656]{1,0:T(8,128)(2,1)S(1)}, bf16[32,6656]{1,0:T(8,128)(2,1)S(1)}, u32[]{:S(2)}, u32[]{:S(2)}) collective-permute-start(bf16[32,6656]{1,0:T(8,128)(2,1)S(1)} %get-tuple-element.32), channel_id=1, source_target_pairs={{0,64},{1,17},{8,72},{9,25},{16,80},{17,1},{24,88},{25,9},{32,96},... | collective-permute-start | bytes 1277960 | tf_op jit(solution)/shard_map/ppermute | solution.py:29
  52.4 4.3 %collective-permute-done.4 = bf16[32,6656]{1,0:T(8,128)(2,1)S(1)} collective-permute-done((bf16[32,6656]{1,0:T(8,128)(2,1)S(1)}, bf16[32,6656]{1,0:T(8,128)(2,1)S(1)}, u32[]{:S(2)}, u32[]{:S(2)}) %collective-permute-start.4) | collective-permute-done | bytes 426016 | tf_op jit(solution)/shard_map/ppermute | solution.py:29
  56.6 0.0 collective-permute-done.5
  56.6 5.5 %collective-permute-done.6 = bf16[32,6656]{1,0:T(8,128)(2,1)S(1)} collective-permute-done((bf16[32,6656]{1,0:T(8,128)(2,1)S(1)}, bf16[32,6656]{1,0:T(8,128)(2,1)S(1)}, u32[]{:S(2)}, u32[]{:S(2)}) %collective-permute-start.6) | collective-permute-done | bytes 426016 | tf_op jit(solution)/shard_map/ppermute | solution.py:29
  62.2 0.2 convert_add_fusion
  62.4 0.0 copy-start.1
  62.4 0.1 fusion
  62.5 1.8 %collective-permute-start.7 = (bf16[32,3328]{1,0:T(8,128)(2,1)S(1)}, bf16[32,3328]{1,0:T(8,128)(2,1)S(1)}, u32[]{:S(2)}, u32[]{:S(2)}) collective-permute-start(bf16[32,3328]{1,0:T(8,128)(2,1)S(1)} %fusion), channel_id=1, source_target_pairs={{0,96},{1,25},{8,104},{9,1},{16,112},{17,9},{24,120},{25,17},{32,0... | collective-permute-start | bytes 638984 | tf_op jit(solution)/shard_map/ppermute | solution.py:29
  64.3 0.9 collective-permute-start.8
  65.2 0.0 collective-permute-start.9
  65.2 0.9 constant_dynamic-slice_fusion
  66.2 3.2 %collective-permute-done.7 = bf16[32,3328]{1,0:T(8,128)(2,1)S(1)} collective-permute-done((bf16[32,3328]{1,0:T(8,128)(2,1)S(1)}, bf16[32,3328]{1,0:T(8,128)(2,1)S(1)}, u32[]{:S(2)}, u32[]{:S(2)}) %collective-permute-start.7) | collective-permute-done | bytes 213024 | tf_op jit(solution)/shard_map/ppermute | solution.py:29
  69.4 1.2 collective-permute-done.8
  70.6 2.5 %collective-permute-done.9 = bf16[32,3328]{1,0:T(8,128)(2,1)S(1)} collective-permute-done((bf16[32,3328]{1,0:T(8,128)(2,1)S(1)}, bf16[32,3328]{1,0:T(8,128)(2,1)S(1)}, u32[]{:S(2)}, u32[]{:S(2)}) %collective-permute-start.9) | collective-permute-done | bytes 213024 | tf_op jit(solution)/shard_map/ppermute | solution.py:29
  73.1 0.1 pad_maximum_fusion.2.rest_0_
  73.1 3.0 %collective-permute-start.10 = (bf16[128,3328]{1,0:T(8,128)(2,1)S(1)}, bf16[128,3328]{1,0:T(8,128)(2,1)S(1)}, u32[]{:S(2)}, u32[]{:S(2)}) collective-permute-start(bf16[128,3328]{1,0:T(8,128)(2,1)S(1)} %pad_maximum_fusion.2.rest_0_), channel_id=1, source_target_pairs={{0,24},{1,97},{8,0},{9,105},{16,8},{17,113},{24,16},{25,121},{32,5... | collective-permute-start | bytes 2555912 | tf_op jit(solution)/shard_map/ppermute | solution.py:29
  76.1 0.7 collective-permute-start.12
  76.8 2.9 %copy-done = bf16[3328,1024]{1,0:T(8,128)(2,1)S(1)} copy-done((bf16[3328,1024]{1,0:T(8,128)(2,1)S(1)}, bf16[3328,1024]{1,0:T(8,128)(2,1)}, u32[]{:S(2)}) %copy-start) | copy-done | bytes 6815768
  79.7 1.9 %fetched_weights.1.rest_4_ = bf16[3328,1024]{1,0:T(8,128)(2,1)S(1)} custom-call(bf16[3328,1024]{1,0:T(8,128)(2,1)S(1)} %copy-done, f32[26,1024]{1,0:T(8,128)S(1)} %copy-done.1), custom_call_target="tpu_custom_call" | custom-call | flops 3407872 | bytes 6815744 | tf_op jit(solution)/shard_map/fetched_weights/pallas_call | solution.py:178
  81.7 13.2 %collective-permute-done.10.rest_1_ = bf16[128,3328]{1,0:T(8,128)(2,1)S(1)} collective-permute-done((bf16[128,3328]{1,0:T(8,128)(2,1)S(1)}, bf16[128,3328]{1,0:T(8,128)(2,1)S(1)}, u32[]{:S(2)}, u32[]{:S(2)}) %collective-permute-start.10) | collective-permute-done | bytes 852000 | tf_op jit(solution)/shard_map/ppermute | solution.py:29
  94.9 3.4 %collective-permute-done.12.rest_3_ = bf16[128,3328]{1,0:T(8,128)(2,1)S(1)} collective-permute-done((bf16[128,3328]{1,0:T(8,128)(2,1)S(1)}, bf16[128,3328]{1,0:T(8,128)(2,1)S(1)}, u32[]{:S(2)}, u32[]{:S(2)}) %collective-permute-start.12) | collective-permute-done | bytes 852000 | tf_op jit(solution)/shard_map/ppermute | solution.py:29
  98.3 3.9 %down_sums.1 = (bf16[4,64,1024]{2,1,0:T(8,128)(2,1)S(1)}, bf16[4,64,1024]{2,1,0:T(8,128)(2,1)S(1)}) custom-call(bf16[128,3328]{1,0:T(8,128)(2,1)S(1)} %pad_maximum_fusion.2.rest_0_, bf16[128,3328]{1,0:T(8,128)(2,1)S(1)} %collective-permute-done.10.rest_1_, bf16[128,3328]{1,0:T(8,128)(2,1)S(1)} %collective-permute-done.11.rest_2_, ...), custom_call_target="tpu_custom_call" | custom-call | flops 3489660928 | bytes 10223616 | tf_op jit(solution)/shard_map/down_sums/pallas_call | solution.py:220
  102.2 5.8 %collective-permute-start.13 = (bf16[4,64,1024]{2,1,0:T(8,128)(2,1)S(1)}, bf16[4,64,1024]{2,1,0:T(8,128)(2,1)S(1)}, u32[]{:S(2)}, u32[]{:S(2)}) collective-permute-start(bf16[4,64,1024]{2,1,0:T(8,128)(2,1)S(1)} %get-tuple-element.29), channel_id=1, source_target_pairs={{0,1},{1,0},{2,3},{3,2},{4,5},{5,4},{6,7},{7,6},{8,9},{9,8},{10,11... | collective-permute-start | bytes 1572872 | tf_op jit(solution)/shard_map/ppermute | solution.py:37
  108.0 1.5 %collective-permute-done.13 = bf16[4,64,1024]{2,1,0:T(8,128)(2,1)S(1)} collective-permute-done((bf16[4,64,1024]{2,1,0:T(8,128)(2,1)S(1)}, bf16[4,64,1024]{2,1,0:T(8,128)(2,1)S(1)}, u32[]{:S(2)}, u32[]{:S(2)}) %collective-permute-start.13) | collective-permute-done | bytes 524320 | tf_op jit(solution)/shard_map/ppermute | solution.py:37
  109.6 0.2 add_convert_fusion.3
  109.8 1.8 %collective-permute-start.14 = (bf16[64,1024]{1,0:T(8,128)(2,1)S(1)}, bf16[64,1024]{1,0:T(8,128)(2,1)S(1)}, u32[]{:S(2)}, u32[]{:S(2)}) collective-permute-start(bf16[64,1024]{1,0:T(8,128)(2,1)S(1)} %get-tuple-element.34), channel_id=1, source_target_pairs={{0,2},{2,4},{4,6},{6,0},{1,3},{3,5},{5,7},{7,1},{8,10},{10,12},{12... | collective-permute-start | bytes 393224 | tf_op jit(solution)/shard_map/ppermute | solution.py:33
  111.6 2.2 %collective-permute-start.15 = (bf16[64,1024]{1,0:T(8,128)(2,1)S(1)}, bf16[64,1024]{1,0:T(8,128)(2,1)S(1)}, u32[]{:S(2)}, u32[]{:S(2)}) collective-permute-start(bf16[64,1024]{1,0:T(8,128)(2,1)S(1)} %get-tuple-element.36), channel_id=1, source_target_pairs={{0,6},{2,0},{4,2},{6,4},{1,7},{3,1},{5,3},{7,5},{8,14},{10,8},{12,... | collective-permute-start | bytes 393224 | tf_op jit(solution)/shard_map/ppermute | solution.py:33
  113.8 1.2 collective-permute-start.16
  115.0 2.3 %collective-permute-done.14 = bf16[64,1024]{1,0:T(8,128)(2,1)S(1)} collective-permute-done((bf16[64,1024]{1,0:T(8,128)(2,1)S(1)}, bf16[64,1024]{1,0:T(8,128)(2,1)S(1)}, u32[]{:S(2)}, u32[]{:S(2)}) %collective-permute-start.14) | collective-permute-done | bytes 131104 | tf_op jit(solution)/shard_map/ppermute | solution.py:33
  117.3 3.7 %collective-permute-done.16 = bf16[64,1024]{1,0:T(8,128)(2,1)S(1)} collective-permute-done((bf16[64,1024]{1,0:T(8,128)(2,1)S(1)}, bf16[64,1024]{1,0:T(8,128)(2,1)S(1)}, u32[]{:S(2)}, u32[]{:S(2)}) %collective-permute-start.16) | collective-permute-done | bytes 131104 | tf_op jit(solution)/shard_map/ppermute | solution.py:33
  120.9 0.1 fusion.4
  121.0 0.1 collective-permute-start.18
  121.1 1.0 collective-permute-start.19
  122.1 1.9 %collective-permute-start.17 = (bf16[64,1024]{1,0:T(8,128)(2,1)S(1)}, bf16[64,1024]{1,0:T(8,128)(2,1)S(1)}, u32[]{:S(2)}, u32[]{:S(2)}) collective-permute-start(bf16[64,1024]{1,0:T(8,128)(2,1)S(1)} %fusion.4), channel_id=1, source_target_pairs={{0,6},{2,0},{4,2},{6,4},{1,7},{3,1},{5,3},{7,5},{8,14},{10,8},{12,... | collective-permute-start | bytes 393224 | tf_op jit(solution)/shard_map/ppermute | solution.py:33
  124.0 0.1 broadcast_in_dim.3
  124.2 2.3 %collective-permute-done.18 = bf16[64,1024]{1,0:T(8,128)(2,1)S(1)} collective-permute-done((bf16[64,1024]{1,0:T(8,128)(2,1)S(1)}, bf16[64,1024]{1,0:T(8,128)(2,1)S(1)}, u32[]{:S(2)}, u32[]{:S(2)}) %collective-permute-start.18) | collective-permute-done | bytes 131104 | tf_op jit(solution)/shard_map/ppermute | solution.py:33
  126.5 3.8 %collective-permute-done.19 = bf16[64,1024]{1,0:T(8,128)(2,1)S(1)} collective-permute-done((bf16[64,1024]{1,0:T(8,128)(2,1)S(1)}, bf16[64,1024]{1,0:T(8,128)(2,1)S(1)}, u32[]{:S(2)}, u32[]{:S(2)}) %collective-permute-start.19) | collective-permute-done | bytes 131104 | tf_op jit(solution)/shard_map/ppermute | solution.py:33
  130.4 0.0 collective-permute-done.17
  130.4 0.1 pad_maximum_fusion.3
  130.4 1.0 collective-permute-start.20
  131.5 1.5 %collective-permute-done.20 = bf16[4,64,1024]{2,1,0:T(8,128)(2,1)S(1)} collective-permute-done((bf16[4,64,1024]{2,1,0:T(8,128)(2,1)S(1)}, bf16[4,64,1024]{2,1,0:T(8,128)(2,1)S(1)}, u32[]{:S(2)}, u32[]{:S(2)}) %collective-permute-start.20) | collective-permute-done | bytes 524320 | tf_op jit(solution)/shard_map/ppermute | solution.py:37
  133.1 0.0 copy-start.3
  133.1 1.0 copy-done.3
  (19 shorter events, 0.2 us)
Async XLA Ops:
  8.8 14.4 %collective-permute-start = (bf16[64,6656]{1,0:T(8,128)(2,1)}, bf16[64,6656]{1,0:T(8,128)(2,1)S(1)}, u32[]{:S(2)}, u32[]{:S(2)}) collective-permute-start(bf16[64,6656]{1,0:T(8,128)(2,1)} %get-tuple-element.21), channel_id=1, source_target_pairs={{0,8},{1,33},{8,16},{9,41},{16,24},{17,49},{24,0},{25,57},{32,40},... | collective-permute-start | bytes 2555912 | tf_op jit(solution)/shard_map/ppermute | solution.py:29
  11.0 13.9 %collective-permute-start.2 = (bf16[64,6656]{1,0:T(8,128)(2,1)}, bf16[64,6656]{1,0:T(8,128)(2,1)S(1)}, u32[]{:S(2)}, u32[]{:S(2)}) collective-permute-start(bf16[64,6656]{1,0:T(8,128)(2,1)} %get-tuple-element.23), channel_id=1, source_target_pairs={{0,24},{1,97},{8,0},{9,105},{16,8},{17,113},{24,16},{25,121},{32,5... | collective-permute-start | bytes 2555912 | tf_op jit(solution)/shard_map/ppermute | solution.py:29
  23.1 1.5 %copy-start.6 = (bf16[64,6656]{1,0:T(8,128)(2,1)S(1)}, bf16[64,6656]{1,0:T(8,128)(2,1)}, u32[]{:S(2)}) copy-start(bf16[64,6656]{1,0:T(8,128)(2,1)} %get-tuple-element.19) | copy-start | bytes 2555908
  24.6 1.2 copy-start.4
  24.7 1.3 copy-start.5
  24.7 22.2 %collective-permute-start.1 = (bf16[128,6656]{1,0:T(8,128)(2,1)S(1)}, bf16[128,6656]{1,0:T(8,128)(2,1)S(1)}, u32[]{:S(2)}, u32[]{:S(2)}) collective-permute-start(bf16[128,6656]{1,0:T(8,128)(2,1)S(1)} %pad_maximum_fusion), channel_id=1, source_target_pairs={{0,8},{1,33},{8,16},{9,41},{16,24},{17,49},{24,0},{25,57},{32,40},... | collective-permute-start | bytes 5111816 | tf_op jit(solution)/shard_map/ppermute | solution.py:29
  26.0 21.3 %copy-start.2 = (bf16[128,6656]{1,0:T(8,128)(2,1)S(1)}, bf16[128,6656]{1,0:T(8,128)(2,1)}, u32[]{:S(2)}) copy-start(bf16[128,6656]{1,0:T(8,128)(2,1)} %get-tuple-element.18) | copy-start | bytes 5111812
  26.2 21.2 %collective-permute-start.3 = (bf16[128,6656]{1,0:T(8,128)(2,1)S(1)}, bf16[128,6656]{1,0:T(8,128)(2,1)S(1)}, u32[]{:S(2)}, u32[]{:S(2)}) collective-permute-start(bf16[128,6656]{1,0:T(8,128)(2,1)S(1)} %pad_maximum_fusion.1), channel_id=1, source_target_pairs={{0,24},{1,97},{8,0},{9,105},{16,8},{17,113},{24,16},{25,121},{32,5... | collective-permute-start | bytes 5111816 | tf_op jit(solution)/shard_map/ppermute | solution.py:29
  48.1 8.6 %collective-permute-start.4 = (bf16[32,6656]{1,0:T(8,128)(2,1)S(1)}, bf16[32,6656]{1,0:T(8,128)(2,1)S(1)}, u32[]{:S(2)}, u32[]{:S(2)}) collective-permute-start(bf16[32,6656]{1,0:T(8,128)(2,1)S(1)} %get-tuple-element.31), channel_id=1, source_target_pairs={{0,32},{1,9},{8,40},{9,17},{16,48},{17,25},{24,56},{25,1},{32,64},... | collective-permute-start | bytes 1277960 | tf_op jit(solution)/shard_map/ppermute | solution.py:29
  49.4 7.3 %collective-permute-start.5 = (bf16[32,6656]{1,0:T(8,128)(2,1)S(1)}, bf16[32,6656]{1,0:T(8,128)(2,1)S(1)}, u32[]{:S(2)}, u32[]{:S(2)}) collective-permute-start(bf16[32,6656]{1,0:T(8,128)(2,1)S(1)} %get-tuple-element.33), channel_id=1, source_target_pairs={{0,96},{1,25},{8,104},{9,1},{16,112},{17,9},{24,120},{25,17},{32,0... | collective-permute-start | bytes 1277960 | tf_op jit(solution)/shard_map/ppermute | solution.py:29
  50.8 11.3 %collective-permute-start.6 = (bf16[32,6656]{1,0:T(8,128)(2,1)S(1)}, bf16[32,6656]{1,0:T(8,128)(2,1)S(1)}, u32[]{:S(2)}, u32[]{:S(2)}) collective-permute-start(bf16[32,6656]{1,0:T(8,128)(2,1)S(1)} %get-tuple-element.32), channel_id=1, source_target_pairs={{0,64},{1,17},{8,72},{9,25},{16,80},{17,1},{24,88},{25,9},{32,96},... | collective-permute-start | bytes 1277960 | tf_op jit(solution)/shard_map/ppermute | solution.py:29
  62.4 14.4 %copy-start.1 = (f32[26,1024]{1,0:T(8,128)S(1)}, f32[26,1024]{1,0:T(8,128)}, u32[]{:S(2)}) copy-start(f32[26,1024]{1,0:T(8,128)} %scales) | copy-start | bytes 319492
  62.5 6.8 %collective-permute-start.7 = (bf16[32,3328]{1,0:T(8,128)(2,1)S(1)}, bf16[32,3328]{1,0:T(8,128)(2,1)S(1)}, u32[]{:S(2)}, u32[]{:S(2)}) collective-permute-start(bf16[32,3328]{1,0:T(8,128)(2,1)S(1)} %fusion), channel_id=1, source_target_pairs={{0,96},{1,25},{8,104},{9,1},{16,112},{17,9},{24,120},{25,17},{32,0... | collective-permute-start | bytes 638984 | tf_op jit(solution)/shard_map/ppermute | solution.py:29
  64.3 6.3 %collective-permute-start.8 = (bf16[32,3328]{1,0:T(8,128)(2,1)S(1)}, bf16[32,3328]{1,0:T(8,128)(2,1)S(1)}, u32[]{:S(2)}, u32[]{:S(2)}) collective-permute-start(bf16[32,3328]{1,0:T(8,128)(2,1)S(1)} %fusion), channel_id=1, source_target_pairs={{0,64},{1,17},{8,72},{9,25},{16,80},{17,1},{24,88},{25,9},{32,96},... | collective-permute-start | bytes 638984 | tf_op jit(solution)/shard_map/ppermute | solution.py:29
  65.2 7.8 %collective-permute-start.9 = (bf16[32,3328]{1,0:T(8,128)(2,1)S(1)}, bf16[32,3328]{1,0:T(8,128)(2,1)S(1)}, u32[]{:S(2)}, u32[]{:S(2)}) collective-permute-start(bf16[32,3328]{1,0:T(8,128)(2,1)S(1)} %fusion), channel_id=1, source_target_pairs={{0,32},{1,9},{8,40},{9,17},{16,48},{17,25},{24,56},{25,1},{32,64},... | collective-permute-start | bytes 638984 | tf_op jit(solution)/shard_map/ppermute | solution.py:29
  73.1 21.7 %collective-permute-start.10 = (bf16[128,3328]{1,0:T(8,128)(2,1)S(1)}, bf16[128,3328]{1,0:T(8,128)(2,1)S(1)}, u32[]{:S(2)}, u32[]{:S(2)}) collective-permute-start(bf16[128,3328]{1,0:T(8,128)(2,1)S(1)} %pad_maximum_fusion.2.rest_0_), channel_id=1, source_target_pairs={{0,24},{1,97},{8,0},{9,105},{16,8},{17,113},{24,16},{25,121},{32,5... | collective-permute-start | bytes 2555912 | tf_op jit(solution)/shard_map/ppermute | solution.py:29
  76.1 18.8 %collective-permute-start.11 = (bf16[128,3328]{1,0:T(8,128)(2,1)S(1)}, bf16[128,3328]{1,0:T(8,128)(2,1)S(1)}, u32[]{:S(2)}, u32[]{:S(2)}) collective-permute-start(bf16[128,3328]{1,0:T(8,128)(2,1)S(1)} %pad_maximum_fusion.2.rest_0_), channel_id=1, source_target_pairs={{0,16},{1,65},{8,24},{9,73},{16,0},{17,81},{24,8},{25,89},{32,48},... | collective-permute-start | bytes 2555912 | tf_op jit(solution)/shard_map/ppermute | solution.py:29
  76.1 22.2 %collective-permute-start.12 = (bf16[128,3328]{1,0:T(8,128)(2,1)S(1)}, bf16[128,3328]{1,0:T(8,128)(2,1)S(1)}, u32[]{:S(2)}, u32[]{:S(2)}) collective-permute-start(bf16[128,3328]{1,0:T(8,128)(2,1)S(1)} %pad_maximum_fusion.2.rest_0_), channel_id=1, source_target_pairs={{0,8},{1,33},{8,16},{9,41},{16,24},{17,49},{24,0},{25,57},{32,40},... | collective-permute-start | bytes 2555912 | tf_op jit(solution)/shard_map/ppermute | solution.py:29
  76.8 2.9 %copy-start = (bf16[3328,1024]{1,0:T(8,128)(2,1)S(1)}, bf16[3328,1024]{1,0:T(8,128)(2,1)}, u32[]{:S(2)}) copy-start(bf16[3328,1024]{1,0:T(8,128)(2,1)} %codes) | copy-start | bytes 20447236
  102.2 7.3 %collective-permute-start.13 = (bf16[4,64,1024]{2,1,0:T(8,128)(2,1)S(1)}, bf16[4,64,1024]{2,1,0:T(8,128)(2,1)S(1)}, u32[]{:S(2)}, u32[]{:S(2)}) collective-permute-start(bf16[4,64,1024]{2,1,0:T(8,128)(2,1)S(1)} %get-tuple-element.29), channel_id=1, source_target_pairs={{0,1},{1,0},{2,3},{3,2},{4,5},{5,4},{6,7},{7,6},{8,9},{9,8},{10,11... | collective-permute-start | bytes 1572872 | tf_op jit(solution)/shard_map/ppermute | solution.py:37
  109.8 7.5 %collective-permute-start.14 = (bf16[64,1024]{1,0:T(8,128)(2,1)S(1)}, bf16[64,1024]{1,0:T(8,128)(2,1)S(1)}, u32[]{:S(2)}, u32[]{:S(2)}) collective-permute-start(bf16[64,1024]{1,0:T(8,128)(2,1)S(1)} %get-tuple-element.34), channel_id=1, source_target_pairs={{0,2},{2,4},{4,6},{6,0},{1,3},{3,5},{5,7},{7,1},{8,10},{10,12},{12... | collective-permute-start | bytes 393224 | tf_op jit(solution)/shard_map/ppermute | solution.py:33
  111.6 5.7 %collective-permute-start.15 = (bf16[64,1024]{1,0:T(8,128)(2,1)S(1)}, bf16[64,1024]{1,0:T(8,128)(2,1)S(1)}, u32[]{:S(2)}, u32[]{:S(2)}) collective-permute-start(bf16[64,1024]{1,0:T(8,128)(2,1)S(1)} %get-tuple-element.36), channel_id=1, source_target_pairs={{0,6},{2,0},{4,2},{6,4},{1,7},{3,1},{5,3},{7,5},{8,14},{10,8},{12,... | collective-permute-start | bytes 393224 | tf_op jit(solution)/shard_map/ppermute | solution.py:33
  113.8 7.2 %collective-permute-start.16 = (bf16[64,1024]{1,0:T(8,128)(2,1)S(1)}, bf16[64,1024]{1,0:T(8,128)(2,1)S(1)}, u32[]{:S(2)}, u32[]{:S(2)}) collective-permute-start(bf16[64,1024]{1,0:T(8,128)(2,1)S(1)} %get-tuple-element.35), channel_id=1, source_target_pairs={{0,4},{2,6},{4,0},{6,2},{1,5},{3,7},{5,1},{7,3},{8,12},{10,14},{12... | collective-permute-start | bytes 393224 | tf_op jit(solution)/shard_map/ppermute | solution.py:33
  121.0 5.5 %collective-permute-start.18 = (bf16[64,1024]{1,0:T(8,128)(2,1)S(1)}, bf16[64,1024]{1,0:T(8,128)(2,1)S(1)}, u32[]{:S(2)}, u32[]{:S(2)}) collective-permute-start(bf16[64,1024]{1,0:T(8,128)(2,1)S(1)} %fusion.4), channel_id=1, source_target_pairs={{0,4},{2,6},{4,0},{6,2},{1,5},{3,7},{5,1},{7,3},{8,12},{10,14},{12... | collective-permute-start | bytes 393224 | tf_op jit(solution)/shard_map/ppermute | solution.py:33
  121.1 9.2 %collective-permute-start.19 = (bf16[64,1024]{1,0:T(8,128)(2,1)S(1)}, bf16[64,1024]{1,0:T(8,128)(2,1)S(1)}, u32[]{:S(2)}, u32[]{:S(2)}) collective-permute-start(bf16[64,1024]{1,0:T(8,128)(2,1)S(1)} %fusion.4), channel_id=1, source_target_pairs={{0,2},{2,4},{4,6},{6,0},{1,3},{3,5},{5,7},{7,1},{8,10},{10,12},{12... | collective-permute-start | bytes 393224 | tf_op jit(solution)/shard_map/ppermute | solution.py:33
  122.1 8.3 %collective-permute-start.17 = (bf16[64,1024]{1,0:T(8,128)(2,1)S(1)}, bf16[64,1024]{1,0:T(8,128)(2,1)S(1)}, u32[]{:S(2)}, u32[]{:S(2)}) collective-permute-start(bf16[64,1024]{1,0:T(8,128)(2,1)S(1)} %fusion.4), channel_id=1, source_target_pairs={{0,6},{2,0},{4,2},{6,4},{1,7},{3,1},{5,3},{7,5},{8,14},{10,8},{12,... | collective-permute-start | bytes 393224 | tf_op jit(solution)/shard_map/ppermute | solution.py:33
  130.4 2.5 %collective-permute-start.20 = (bf16[4,64,1024]{2,1,0:T(8,128)(2,1)S(1)}, bf16[4,64,1024]{2,1,0:T(8,128)(2,1)S(1)}, u32[]{:S(2)}, u32[]{:S(2)}) collective-permute-start(bf16[4,64,1024]{2,1,0:T(8,128)(2,1)S(1)} %pad_maximum_fusion.3), channel_id=1, source_target_pairs={{0,1},{1,0},{2,3},{3,2},{4,5},{5,4},{6,7},{7,6},{8,9},{9,8},{10,11... | collective-permute-start | bytes 1572872 | tf_op jit(solution)/shard_map/ppermute | solution.py:37
  133.1 1.0 copy-start.3

commit v4 on v3

--- a/solution.py
+++ b/solution.py
@@ -244,14 +244,15 @@
 
     sums = functools.partial(partial_sums, states=states, gate_codes=gate_codes)
     sums = functools.partial(sums, gate_scales=gate_scales, up_codes=up_codes, up_scales=up_scales)
-    top2, low2 = sums(((2, 0), (2, 1)), (1, 1))
+    top2, low2, top1, low3 = sums(((2, 0), (2, 1), (1, 0), (3, 1)), (1, 1, 1, 1))
     passed_low, passed_top = hop(low2, 0, 1), hop(top2, 0, -1)
-    top1, low1, top3, low3, own = sums(((1, 0), (1, 1), (3, 0), (3, 1), (0, 0), (0, 1)), (1, 1, 1, 1, 2))
-    plus = jnp.concatenate([top1, rounded(low1, passed_low)], 0)
-    minus = jnp.concatenate([rounded(top3, passed_top), low3], 0)
-    plus, minus = hop(plus, 0, 1), hop(minus, 0, -1)
-    line = rounded(own, plus, minus)
-    line = [line[k * piece : (k + 1) * piece] for k in range(SIDE)]
+    straight_top, straight_low = hop(top1, 0, 1), hop(low3, 0, -1)
+    low1, top3, own = sums(((1, 1), (3, 0), (0, 0), (0, 1)), (1, 1, 2))
+    low = hop(rounded(low1, passed_low), 0, 1)
+    top = hop(rounded(top3, passed_top), 0, -1)
+    half = own.shape[0] // 2
+    line = rounded(own[:half], straight_top, top), rounded(own[half:], low, straight_low)
+    line = [part[k * piece : (k + 1) * piece] for part in line for k in range(2)]
     both = sent_along_second(line)
     gate, up = both[:, :columns], both[:, columns:]
     act = (jax.nn.silu(gate) * up).astype(jnp.bfloat16)
@@ -268,8 +269,8 @@
     share = half // SIDE
     got = total(both[0], hop_z(both[1], 1), hop_z(both[3], -1), hop_z(both[2], 2))
     done = lax.optimization_barrier(rounded(got, residual))
-    mine = jnp.stack([done, hop_z(done, -1), hop_z(done, 2), hop_z(done, 1)])
-    theirs = other_core(mine)
+    mine = [done, hop_z(done, -1), hop_z(done, 2), hop_z(done, 1)]
+    theirs = [other_core(part) for part in mine]
     out = jnp.zeros((2, SIDE, share, width), jnp.bfloat16)
     for k in range(SIDE):
         out = lax.dynamic_update_slice(out, mine[k][None, None], (core, (iz + k) % SIDE, 0, 0))

time: 134 us -> 128 us (0.955)
  waiting for transfers between devices: 67.7 us -> 57.3 us
  starting transfers between devices: 31.4 us -> 37.2 us
    ppermute x2 -> x5, starting transfers between devices: 6.8 us -> 13.3 us  [other_core(): return lax.ppermute(array, 'core', [(0, 1), (1, 0)])]
    ppermute x6, waiting for transfers between devices: 12.1 us -> 5.93 us  [hop_z(): lax.ppermute(array, 'z', [(i, (i + shift) % SIDE) for i in range(SIDE)])]
    ppermute x13 -> x15, waiting for transfers between devices: 52.6 us -> 49 us  [hop(): return lax.ppermute(array, PLANE, pairs)]
    unnamed x14 -> x10, local copies, waits for them, and re-layouts: 4.9 us -> 3.91 us
    ppermute x2 -> x5, waiting for transfers between devices: 3.01 us -> 2.36 us  [other_core(): return lax.ppermute(array, 'core', [(0, 1), (1, 0)])]
    ppermute x13 -> x15, starting transfers between devices: 16.4 us -> 16.4 us  [hop(): return lax.ppermute(array, PLANE, pairs)]
  transfers between devices with their start and end apart: 21 -> 26, of which waited for: 15 -> 14; matrix products, arithmetic and copies ran while one was open for 2% -> 2% of each run, Pallas kernels for 9% -> 9%
where the time goes in v4:
time: 128 us
  waiting for transfers between devices  57.3 us (45%)
  starting transfers between devices  37.2 us (29%)
  Pallas kernels  24.8 us (19%)
  local copies, waits for them, and re-layouts  5.19 us (4%)
  other arithmetic  2.89 us (2%)
    ppermute x15, waiting for transfers between devices, hop(): return lax.ppermute(array, PLANE, pairs)  49 us
    pallas_call x2, Pallas kernels, partial_sums(): pl.pallas_call(functools.partial(up_kernel, piece, halves, ends), out_sha...  18.9 us
    ppermute x15, starting transfers between devices, hop(): return lax.ppermute(array, PLANE, pairs)  16.4 us
    ppermute x5, starting transfers between devices, other_core(): return lax.ppermute(array, 'core', [(0, 1), (1, 0)])  13.3 us
    ppermute x6, starting transfers between devices, hop_z(): lax.ppermute(array, 'z', [(i, (i + shift) % SIDE) for i in range(SIDE)])  7.53 us
    ppermute x6, waiting for transfers between devices, hop_z(): lax.ppermute(array, 'z', [(i, (i + shift) % SIDE) for i in range(SIDE)])  5.93 us
    pallas_call x1, Pallas kernels, down_sums(): pl.pallas_call(functools.partial(down_kernel, piece), out_shape=(shape, s...  3.94 us
    unnamed x10, local copies, waits for them, and re-layouts  3.91 us
  transfers between devices with their start and end apart: 26, of which 14 were waited for; matrix products, arithmetic and copies ran while one was open for 2% of the time, Pallas kernels for 9%

profile of v4, /device:TPU:1, one launch (start us, length us, event | category | flops | bytes accessed | tf_op | source)
XLA Modules:
  0.0 127.7 jit_solution(17257883343400968872)
XLA Ops:
  0.0 9.5 %partial_sums.3 = (bf16[64,6656]{1,0:T(8,128)(2,1)}, bf16[64,6656]{1,0:T(8,128)(2,1)}, bf16[64,6656]{1,0:T(8,128)(2,1)}, bf16[64,6656]{1,0:T(8,128)(2,1)}) custom-call(bf16[512,1024]{1,0:T(8,128)(2,1)} %states.3, bf16[1024,3328]{1,0:T(8,128)(2,1)} %gate_codes.3, f32[8,3328]{1,0:T(8,128)} %gate_scales.3, bf16[1024,3328]{1,0:T(8,128)(2,1)} %up_codes.3, ...), custom_call_target="tpu_custom_call" | custom-call | flops 3489660928 | bytes 17039360 | tf_op jit(solution)/shard_map/partial_sums/pallas_call | solution.py:132
  9.5 3.6 %collective-permute-start.1 = (bf16[64,6656]{1,0:T(8,128)(2,1)}, bf16[64,6656]{1,0:T(8,128)(2,1)S(1)}, u32[]{:S(2)}, u32[]{:S(2)}) collective-permute-start(bf16[64,6656]{1,0:T(8,128)(2,1)} %get-tuple-element.21), channel_id=1, source_target_pairs={{0,24},{1,97},{8,0},{9,105},{16,8},{17,113},{24,16},{25,121},{32,5... | collective-permute-start | bytes 2555912 | tf_op jit(solution)/shard_map/ppermute | solution.py:29
  13.1 0.0 collective-permute-start
  13.1 2.7 %collective-permute-start.6 = (bf16[64,6656]{1,0:T(8,128)(2,1)}, bf16[64,6656]{1,0:T(8,128)(2,1)S(1)}, u32[]{:S(2)}, u32[]{:S(2)}) collective-permute-start(bf16[64,6656]{1,0:T(8,128)(2,1)} %get-tuple-element.24), channel_id=1, source_target_pairs={{0,24},{1,97},{8,0},{9,105},{16,8},{17,113},{24,16},{25,121},{32,5... | collective-permute-start | bytes 2555912 | tf_op jit(solution)/shard_map/ppermute | solution.py:29
  15.8 9.5 %partial_sums.2 = (bf16[64,6656]{1,0:T(8,128)(2,1)}, bf16[64,6656]{1,0:T(8,128)(2,1)}, bf16[128,6656]{1,0:T(8,128)(2,1)}) custom-call(bf16[512,1024]{1,0:T(8,128)(2,1)} %states.3, bf16[1024,3328]{1,0:T(8,128)(2,1)} %gate_codes.3, f32[8,3328]{1,0:T(8,128)} %gate_scales.3, bf16[1024,3328]{1,0:T(8,128)(2,1)} %up_codes.3, f32[8,3328]{1,0:T(8,128)} %up_scales.3), custom_call_target="tpu_custom_call" | custom-call | flops 3489660928 | bytes 17039360 | tf_op jit(solution)/shard_map/partial_sums/pallas_call | solution.py:132
  25.3 1.4 %add_convert_fusion.3 = bf16[64,6656]{1,0:T(8,128)(2,1)S(1)} fusion(bf16[64,6656]{1,0:T(8,128)(2,1)S(1)} %collective-permute-done.1, bf16[64,6656]{1,0:T(8,128)(2,1)} %get-tuple-element.20), kind=kLoop, calls=%fused_computation.3 | loop fusion | flops 1703936 | bytes 2555904 | tf_op jit(solution)/shard_map/convert_element_type | solution.py:48
  26.7 1.7 %collective-permute-start.2 = (bf16[64,6656]{1,0:T(8,128)(2,1)S(1)}, bf16[64,6656]{1,0:T(8,128)(2,1)S(1)}, u32[]{:S(2)}, u32[]{:S(2)}) collective-permute-start(bf16[64,6656]{1,0:T(8,128)(2,1)S(1)} %add_convert_fusion.3), channel_id=1, source_target_pairs={{0,24},{1,97},{8,0},{9,105},{16,8},{17,113},{24,16},{25,121},{32,5... | collective-permute-start | bytes 2555912 | tf_op jit(solution)/shard_map/ppermute | solution.py:29
  28.4 0.2 add_convert_fusion.1
  28.6 0.1 collective-permute-start.5
  28.7 6.8 %collective-permute-done = bf16[64,6656]{1,0:T(8,128)(2,1)S(1)} collective-permute-done((bf16[64,6656]{1,0:T(8,128)(2,1)}, bf16[64,6656]{1,0:T(8,128)(2,1)S(1)}, u32[]{:S(2)}, u32[]{:S(2)}) %collective-permute-start) | collective-permute-done | bytes 852000 | tf_op jit(solution)/shard_map/ppermute | solution.py:29
  35.5 0.0 collective-permute-done.6
  35.5 5.7 %collective-permute-done.2 = bf16[64,6656]{1,0:T(8,128)(2,1)S(1)} collective-permute-done((bf16[64,6656]{1,0:T(8,128)(2,1)S(1)}, bf16[64,6656]{1,0:T(8,128)(2,1)S(1)}, u32[]{:S(2)}, u32[]{:S(2)}) %collective-permute-start.2) | collective-permute-done | bytes 852000 | tf_op jit(solution)/shard_map/ppermute | solution.py:29
  41.2 3.4 %collective-permute-done.5 = bf16[64,6656]{1,0:T(8,128)(2,1)S(1)} collective-permute-done((bf16[64,6656]{1,0:T(8,128)(2,1)S(1)}, bf16[64,6656]{1,0:T(8,128)(2,1)S(1)}, u32[]{:S(2)}, u32[]{:S(2)}) %collective-permute-start.5) | collective-permute-done | bytes 852000 | tf_op jit(solution)/shard_map/ppermute | solution.py:29
  44.6 0.6 add_convert_fusion.2
  45.2 0.1 fusion.5
  45.3 2.3 %collective-permute-start.7 = (bf16[32,6656]{1,0:T(8,128)(2,1)S(1)}, bf16[32,6656]{1,0:T(8,128)(2,1)S(1)}, u32[]{:S(2)}, u32[]{:S(2)}) collective-permute-start(bf16[32,6656]{1,0:T(8,128)(2,1)S(1)} %get-tuple-element.33), channel_id=1, source_target_pairs={{0,96},{1,25},{8,104},{9,1},{16,112},{17,9},{24,120},{25,17},{32,0... | collective-permute-start | bytes 1277960 | tf_op jit(solution)/shard_map/ppermute | solution.py:29
  47.5 0.5 collective-permute-start.8
  48.1 0.7 collective-permute-start.3
  48.8 8.4 %collective-permute-done.7 = bf16[32,6656]{1,0:T(8,128)(2,1)S(1)} collective-permute-done((bf16[32,6656]{1,0:T(8,128)(2,1)S(1)}, bf16[32,6656]{1,0:T(8,128)(2,1)S(1)}, u32[]{:S(2)}, u32[]{:S(2)}) %collective-permute-start.7) | collective-permute-done | bytes 426016 | tf_op jit(solution)/shard_map/ppermute | solution.py:29
  57.2 3.7 %collective-permute-done.3 = bf16[32,6656]{1,0:T(8,128)(2,1)S(1)} collective-permute-done((bf16[32,6656]{1,0:T(8,128)(2,1)S(1)}, bf16[32,6656]{1,0:T(8,128)(2,1)S(1)}, u32[]{:S(2)}, u32[]{:S(2)}) %collective-permute-start.3) | collective-permute-done | bytes 426016 | tf_op jit(solution)/shard_map/ppermute | solution.py:29
  60.9 0.2 convert_add_fusion
  61.1 0.0 copy-start.1
  61.1 0.1 fusion
  61.2 0.6 collective-permute-start.10
  61.8 0.4 collective-permute-start.11
  62.2 2.3 %collective-permute-start.9 = (bf16[32,3328]{1,0:T(8,128)(2,1)S(1)}, bf16[32,3328]{1,0:T(8,128)(2,1)S(1)}, u32[]{:S(2)}, u32[]{:S(2)}) collective-permute-start(bf16[32,3328]{1,0:T(8,128)(2,1)S(1)} %fusion), channel_id=1, source_target_pairs={{0,96},{1,25},{8,104},{9,1},{16,112},{17,9},{24,120},{25,17},{32,0... | collective-permute-start | bytes 638984 | tf_op jit(solution)/shard_map/ppermute | solution.py:29
  64.5 0.9 constant_dynamic-slice_fusion
  65.4 2.2 %collective-permute-done.10 = bf16[32,3328]{1,0:T(8,128)(2,1)S(1)} collective-permute-done((bf16[32,3328]{1,0:T(8,128)(2,1)S(1)}, bf16[32,3328]{1,0:T(8,128)(2,1)S(1)}, u32[]{:S(2)}, u32[]{:S(2)}) %collective-permute-start.10) | collective-permute-done | bytes 213024 | tf_op jit(solution)/shard_map/ppermute | solution.py:29
  67.6 2.5 %collective-permute-done.11 = bf16[32,3328]{1,0:T(8,128)(2,1)S(1)} collective-permute-done((bf16[32,3328]{1,0:T(8,128)(2,1)S(1)}, bf16[32,3328]{1,0:T(8,128)(2,1)S(1)}, u32[]{:S(2)}, u32[]{:S(2)}) %collective-permute-start.11) | collective-permute-done | bytes 213024 | tf_op jit(solution)/shard_map/ppermute | solution.py:29
  70.1 0.0 collective-permute-done.9
  70.1 0.1 pad_maximum_fusion.rest_0_
  70.1 0.3 collective-permute-start.12
  70.4 0.3 collective-permute-start.13
  70.8 0.9 collective-permute-start.14
  71.7 2.9 %copy-done = bf16[3328,1024]{1,0:T(8,128)(2,1)S(1)} copy-done((bf16[3328,1024]{1,0:T(8,128)(2,1)S(1)}, bf16[3328,1024]{1,0:T(8,128)(2,1)}, u32[]{:S(2)}) %copy-start) | copy-done | bytes 6815768
  74.6 1.9 %fetched_weights.1.rest_4_ = bf16[3328,1024]{1,0:T(8,128)(2,1)S(1)} custom-call(bf16[3328,1024]{1,0:T(8,128)(2,1)S(1)} %copy-done, f32[26,1024]{1,0:T(8,128)S(1)} %copy-done.1), custom_call_target="tpu_custom_call" | custom-call | flops 3407872 | bytes 6815744 | tf_op jit(solution)/shard_map/fetched_weights/pallas_call | solution.py:178
  76.6 5.5 %collective-permute-done.12.rest_1_ = bf16[128,3328]{1,0:T(8,128)(2,1)S(1)} collective-permute-done((bf16[128,3328]{1,0:T(8,128)(2,1)S(1)}, bf16[128,3328]{1,0:T(8,128)(2,1)S(1)}, u32[]{:S(2)}, u32[]{:S(2)}) %collective-permute-start.12) | collective-permute-done | bytes 852000 | tf_op jit(solution)/shard_map/ppermute | solution.py:29
  82.1 1.8 %collective-permute-done.13.rest_2_ = bf16[128,3328]{1,0:T(8,128)(2,1)S(1)} collective-permute-done((bf16[128,3328]{1,0:T(8,128)(2,1)S(1)}, bf16[128,3328]{1,0:T(8,128)(2,1)S(1)}, u32[]{:S(2)}, u32[]{:S(2)}) %collective-permute-start.13) | collective-permute-done | bytes 852000 | tf_op jit(solution)/shard_map/ppermute | solution.py:29
  83.8 9.1 %collective-permute-done.14.rest_3_ = bf16[128,3328]{1,0:T(8,128)(2,1)S(1)} collective-permute-done((bf16[128,3328]{1,0:T(8,128)(2,1)S(1)}, bf16[128,3328]{1,0:T(8,128)(2,1)S(1)}, u32[]{:S(2)}, u32[]{:S(2)}) %collective-permute-start.14) | collective-permute-done | bytes 852000 | tf_op jit(solution)/shard_map/ppermute | solution.py:29
  92.9 3.9 %down_sums.1 = (bf16[4,64,1024]{2,1,0:T(8,128)(2,1)S(1)}, bf16[4,64,1024]{2,1,0:T(8,128)(2,1)S(1)}) custom-call(bf16[128,3328]{1,0:T(8,128)(2,1)S(1)} %pad_maximum_fusion.rest_0_, bf16[128,3328]{1,0:T(8,128)(2,1)S(1)} %collective-permute-done.12.rest_1_, bf16[128,3328]{1,0:T(8,128)(2,1)S(1)} %collective-permute-done.13.rest_2_, ...), custom_call_target="tpu_custom_call" | custom-call | flops 3489660928 | bytes 10223616 | tf_op jit(solution)/shard_map/down_sums/pallas_call | solution.py:220
  96.9 4.9 %collective-permute-start.15 = (bf16[4,64,1024]{2,1,0:T(8,128)(2,1)S(1)}, bf16[4,64,1024]{2,1,0:T(8,128)(2,1)S(1)}, u32[]{:S(2)}, u32[]{:S(2)}) collective-permute-start(bf16[4,64,1024]{2,1,0:T(8,128)(2,1)S(1)} %get-tuple-element.29), channel_id=1, source_target_pairs={{0,1},{1,0},{2,3},{3,2},{4,5},{5,4},{6,7},{7,6},{8,9},{9,8},{10,11... | collective-permute-start | bytes 1572872 | tf_op jit(solution)/shard_map/ppermute | solution.py:37
  101.8 1.5 %collective-permute-done.15 = bf16[4,64,1024]{2,1,0:T(8,128)(2,1)S(1)} collective-permute-done((bf16[4,64,1024]{2,1,0:T(8,128)(2,1)S(1)}, bf16[4,64,1024]{2,1,0:T(8,128)(2,1)S(1)}, u32[]{:S(2)}, u32[]{:S(2)}) %collective-permute-start.15) | collective-permute-done | bytes 524320 | tf_op jit(solution)/shard_map/ppermute | solution.py:37
  103.3 0.2 add_convert_fusion.4
  103.5 1.7 %collective-permute-start.16 = (bf16[64,1024]{1,0:T(8,128)(2,1)S(1)}, bf16[64,1024]{1,0:T(8,128)(2,1)S(1)}, u32[]{:S(2)}, u32[]{:S(2)}) collective-permute-start(bf16[64,1024]{1,0:T(8,128)(2,1)S(1)} %get-tuple-element.35), channel_id=1, source_target_pairs={{0,2},{2,4},{4,6},{6,0},{1,3},{3,5},{5,7},{7,1},{8,10},{10,12},{12... | collective-permute-start | bytes 393224 | tf_op jit(solution)/shard_map/ppermute | solution.py:33
  105.2 2.2 %collective-permute-start.17 = (bf16[64,1024]{1,0:T(8,128)(2,1)S(1)}, bf16[64,1024]{1,0:T(8,128)(2,1)S(1)}, u32[]{:S(2)}, u32[]{:S(2)}) collective-permute-start(bf16[64,1024]{1,0:T(8,128)(2,1)S(1)} %get-tuple-element.37), channel_id=1, source_target_pairs={{0,6},{2,0},{4,2},{6,4},{1,7},{3,1},{5,3},{7,5},{8,14},{10,8},{12,... | collective-permute-start | bytes 393224 | tf_op jit(solution)/shard_map/ppermute | solution.py:33
  107.4 1.2 collective-permute-start.18
  108.7 2.3 %collective-permute-done.16 = bf16[64,1024]{1,0:T(8,128)(2,1)S(1)} collective-permute-done((bf16[64,1024]{1,0:T(8,128)(2,1)S(1)}, bf16[64,1024]{1,0:T(8,128)(2,1)S(1)}, u32[]{:S(2)}, u32[]{:S(2)}) %collective-permute-start.16) | collective-permute-done | bytes 131104 | tf_op jit(solution)/shard_map/ppermute | solution.py:33
  110.9 0.0 collective-permute-done.17
  110.9 3.7 %collective-permute-done.18 = bf16[64,1024]{1,0:T(8,128)(2,1)S(1)} collective-permute-done((bf16[64,1024]{1,0:T(8,128)(2,1)S(1)}, bf16[64,1024]{1,0:T(8,128)(2,1)S(1)}, u32[]{:S(2)}, u32[]{:S(2)}) %collective-permute-start.18) | collective-permute-done | bytes 131104 | tf_op jit(solution)/shard_map/ppermute | solution.py:33
  114.6 0.1 fusion.4
  114.7 0.5 collective-permute-start.19
  115.2 1.9 %collective-permute-start.20 = (bf16[64,1024]{1,0:T(8,128)(2,1)S(1)}, bf16[64,1024]{1,0:T(8,128)(2,1)S(1)}, u32[]{:S(2)}, u32[]{:S(2)}) collective-permute-start(bf16[64,1024]{1,0:T(8,128)(2,1)S(1)} %fusion.4), channel_id=1, source_target_pairs={{0,4},{2,6},{4,0},{6,2},{1,5},{3,7},{5,1},{7,3},{8,12},{10,14},{12... | collective-permute-start | bytes 393224 | tf_op jit(solution)/shard_map/ppermute | solution.py:33
  117.1 0.0 collective-permute-start.21
  117.1 2.1 %collective-permute-start.22 = (bf16[64,1024]{1,0:T(8,128)(2,1)S(1)}, bf16[64,1024]{1,0:T(8,128)(2,1)S(1)}, u32[]{:S(2)}, u32[]{:S(2)}) collective-permute-start(bf16[64,1024]{1,0:T(8,128)(2,1)S(1)} %fusion.4), channel_id=1, source_target_pairs={{0,1},{1,0},{2,3},{3,2},{4,5},{5,4},{6,7},{7,6},{8,9},{9,8},{10,11... | collective-permute-start | bytes 393224 | tf_op jit(solution)/shard_map/ppermute | solution.py:37
  119.2 0.1 broadcast_in_dim.27
  119.3 2.7 %collective-permute-start.23 = (bf16[64,1024]{1,0:T(8,128)(2,1)S(1)}, bf16[64,1024]{1,0:T(8,128)(2,1)S(1)}, u32[]{:S(2)}, u32[]{:S(2)}) collective-permute-start(bf16[64,1024]{1,0:T(8,128)(2,1)S(1)} %collective-permute-done.19), channel_id=1, source_target_pairs={{0,1},{1,0},{2,3},{3,2},{4,5},{5,4},{6,7},{7,6},{8,9},{9,8},{10,11... | collective-permute-start | bytes 393224 | tf_op jit(solution)/shard_map/ppermute | solution.py:37
  122.1 0.0 collective-permute-done.20
  122.1 2.2 %collective-permute-start.24 = (bf16[64,1024]{1,0:T(8,128)(2,1)S(1)}, bf16[64,1024]{1,0:T(8,128)(2,1)S(1)}, u32[]{:S(2)}, u32[]{:S(2)}) collective-permute-start(bf16[64,1024]{1,0:T(8,128)(2,1)S(1)} %collective-permute-done.20), channel_id=1, source_target_pairs={{0,1},{1,0},{2,3},{3,2},{4,5},{5,4},{6,7},{7,6},{8,9},{9,8},{10,11... | collective-permute-start | bytes 393224 | tf_op jit(solution)/shard_map/ppermute | solution.py:37
  124.3 0.0 collective-permute-done.21
  124.3 1.4 %collective-permute-start.25 = (bf16[64,1024]{1,0:T(8,128)(2,1)S(1)}, bf16[64,1024]{1,0:T(8,128)(2,1)S(1)}, u32[]{:S(2)}, u32[]{:S(2)}) collective-permute-start(bf16[64,1024]{1,0:T(8,128)(2,1)S(1)} %collective-permute-done.21), channel_id=1, source_target_pairs={{0,1},{1,0},{2,3},{3,2},{4,5},{5,4},{6,7},{7,6},{8,9},{9,8},{10,11... | collective-permute-start | bytes 393224 | tf_op jit(solution)/shard_map/ppermute | solution.py:37
  125.8 0.0 collective-permute-done.23
  125.9 0.8 collective-permute-done.25
  126.7 0.0 copy-start.3
  126.7 1.0 copy-done.3
  (23 shorter events, 0.2 us)
Async XLA Ops:
  9.5 15.8 %collective-permute-start.1 = (bf16[64,6656]{1,0:T(8,128)(2,1)}, bf16[64,6656]{1,0:T(8,128)(2,1)S(1)}, u32[]{:S(2)}, u32[]{:S(2)}) collective-permute-start(bf16[64,6656]{1,0:T(8,128)(2,1)} %get-tuple-element.21), channel_id=1, source_target_pairs={{0,24},{1,97},{8,0},{9,105},{16,8},{17,113},{24,16},{25,121},{32,5... | collective-permute-start | bytes 2555912 | tf_op jit(solution)/shard_map/ppermute | solution.py:29
  13.1 15.3 %collective-permute-start.4 = (bf16[64,6656]{1,0:T(8,128)(2,1)}, bf16[64,6656]{1,0:T(8,128)(2,1)S(1)}, u32[]{:S(2)}, u32[]{:S(2)}) collective-permute-start(bf16[64,6656]{1,0:T(8,128)(2,1)} %get-tuple-element.23), channel_id=1, source_target_pairs={{0,8},{1,33},{8,16},{9,41},{16,24},{17,49},{24,0},{25,57},{32,40},... | collective-permute-start | bytes 2555912 | tf_op jit(solution)/shard_map/ppermute | solution.py:29
  13.1 22.4 %collective-permute-start = (bf16[64,6656]{1,0:T(8,128)(2,1)}, bf16[64,6656]{1,0:T(8,128)(2,1)S(1)}, u32[]{:S(2)}, u32[]{:S(2)}) collective-permute-start(bf16[64,6656]{1,0:T(8,128)(2,1)} %get-tuple-element.19), channel_id=1, source_target_pairs={{0,8},{1,33},{8,16},{9,41},{16,24},{17,49},{24,0},{25,57},{32,40},... | collective-permute-start | bytes 2555912 | tf_op jit(solution)/shard_map/ppermute | solution.py:29
  13.1 22.4 %collective-permute-start.6 = (bf16[64,6656]{1,0:T(8,128)(2,1)}, bf16[64,6656]{1,0:T(8,128)(2,1)S(1)}, u32[]{:S(2)}, u32[]{:S(2)}) collective-permute-start(bf16[64,6656]{1,0:T(8,128)(2,1)} %get-tuple-element.24), channel_id=1, source_target_pairs={{0,24},{1,97},{8,0},{9,105},{16,8},{17,113},{24,16},{25,121},{32,5... | collective-permute-start | bytes 2555912 | tf_op jit(solution)/shard_map/ppermute | solution.py:29
  25.3 3.1 %copy-start.4 = (bf16[64,6656]{1,0:T(8,128)(2,1)S(1)}, bf16[64,6656]{1,0:T(8,128)(2,1)}, u32[]{:S(2)}) copy-start(bf16[64,6656]{1,0:T(8,128)(2,1)} %get-tuple-element.22) | copy-start | bytes 2555908
  26.7 17.9 %copy-start.2 = (bf16[128,6656]{1,0:T(8,128)(2,1)S(1)}, bf16[128,6656]{1,0:T(8,128)(2,1)}, u32[]{:S(2)}) copy-start(bf16[128,6656]{1,0:T(8,128)(2,1)} %get-tuple-element.18) | copy-start | bytes 5111812
  26.7 14.5 %collective-permute-start.2 = (bf16[64,6656]{1,0:T(8,128)(2,1)S(1)}, bf16[64,6656]{1,0:T(8,128)(2,1)S(1)}, u32[]{:S(2)}, u32[]{:S(2)}) collective-permute-start(bf16[64,6656]{1,0:T(8,128)(2,1)S(1)} %add_convert_fusion.3), channel_id=1, source_target_pairs={{0,24},{1,97},{8,0},{9,105},{16,8},{17,113},{24,16},{25,121},{32,5... | collective-permute-start | bytes 2555912 | tf_op jit(solution)/shard_map/ppermute | solution.py:29
  28.6 16.0 %collective-permute-start.5 = (bf16[64,6656]{1,0:T(8,128)(2,1)S(1)}, bf16[64,6656]{1,0:T(8,128)(2,1)S(1)}, u32[]{:S(2)}, u32[]{:S(2)}) collective-permute-start(bf16[64,6656]{1,0:T(8,128)(2,1)S(1)} %add_convert_fusion.1), channel_id=1, source_target_pairs={{0,8},{1,33},{8,16},{9,41},{16,24},{17,49},{24,0},{25,57},{32,40},... | collective-permute-start | bytes 2555912 | tf_op jit(solution)/shard_map/ppermute | solution.py:29
  45.3 11.9 %collective-permute-start.7 = (bf16[32,6656]{1,0:T(8,128)(2,1)S(1)}, bf16[32,6656]{1,0:T(8,128)(2,1)S(1)}, u32[]{:S(2)}, u32[]{:S(2)}) collective-permute-start(bf16[32,6656]{1,0:T(8,128)(2,1)S(1)} %get-tuple-element.33), channel_id=1, source_target_pairs={{0,96},{1,25},{8,104},{9,1},{16,112},{17,9},{24,120},{25,17},{32,0... | collective-permute-start | bytes 1277960 | tf_op jit(solution)/shard_map/ppermute | solution.py:29
  47.5 9.6 %collective-permute-start.8 = (bf16[32,6656]{1,0:T(8,128)(2,1)S(1)}, bf16[32,6656]{1,0:T(8,128)(2,1)S(1)}, u32[]{:S(2)}, u32[]{:S(2)}) collective-permute-start(bf16[32,6656]{1,0:T(8,128)(2,1)S(1)} %get-tuple-element.34), channel_id=1, source_target_pairs={{0,64},{1,17},{8,72},{9,25},{16,80},{17,1},{24,88},{25,9},{32,96},... | collective-permute-start | bytes 1277960 | tf_op jit(solution)/shard_map/ppermute | solution.py:29
  48.1 12.8 %collective-permute-start.3 = (bf16[32,6656]{1,0:T(8,128)(2,1)S(1)}, bf16[32,6656]{1,0:T(8,128)(2,1)S(1)}, u32[]{:S(2)}, u32[]{:S(2)}) collective-permute-start(bf16[32,6656]{1,0:T(8,128)(2,1)S(1)} %slice.49), channel_id=1, source_target_pairs={{0,32},{1,9},{8,40},{9,17},{16,48},{17,25},{24,56},{25,1},{32,64},... | collective-permute-start | bytes 1277960 | tf_op jit(solution)/shard_map/ppermute | solution.py:29
  61.1 10.6 %copy-start.1 = (f32[26,1024]{1,0:T(8,128)S(1)}, f32[26,1024]{1,0:T(8,128)}, u32[]{:S(2)}) copy-start(f32[26,1024]{1,0:T(8,128)} %scales) | copy-start | bytes 319492
  61.2 6.4 %collective-permute-start.10 = (bf16[32,3328]{1,0:T(8,128)(2,1)S(1)}, bf16[32,3328]{1,0:T(8,128)(2,1)S(1)}, u32[]{:S(2)}, u32[]{:S(2)}) collective-permute-start(bf16[32,3328]{1,0:T(8,128)(2,1)S(1)} %fusion), channel_id=1, source_target_pairs={{0,64},{1,17},{8,72},{9,25},{16,80},{17,1},{24,88},{25,9},{32,96},... | collective-permute-start | bytes 638984 | tf_op jit(solution)/shard_map/ppermute | solution.py:29
  61.8 8.3 %collective-permute-start.11 = (bf16[32,3328]{1,0:T(8,128)(2,1)S(1)}, bf16[32,3328]{1,0:T(8,128)(2,1)S(1)}, u32[]{:S(2)}, u32[]{:S(2)}) collective-permute-start(bf16[32,3328]{1,0:T(8,128)(2,1)S(1)} %fusion), channel_id=1, source_target_pairs={{0,32},{1,9},{8,40},{9,17},{16,48},{17,25},{24,56},{25,1},{32,64},... | collective-permute-start | bytes 638984 | tf_op jit(solution)/shard_map/ppermute | solution.py:29
  62.2 7.9 %collective-permute-start.9 = (bf16[32,3328]{1,0:T(8,128)(2,1)S(1)}, bf16[32,3328]{1,0:T(8,128)(2,1)S(1)}, u32[]{:S(2)}, u32[]{:S(2)}) collective-permute-start(bf16[32,3328]{1,0:T(8,128)(2,1)S(1)} %fusion), channel_id=1, source_target_pairs={{0,96},{1,25},{8,104},{9,1},{16,112},{17,9},{24,120},{25,17},{32,0... | collective-permute-start | bytes 638984 | tf_op jit(solution)/shard_map/ppermute | solution.py:29
  70.1 11.9 %collective-permute-start.12 = (bf16[128,3328]{1,0:T(8,128)(2,1)S(1)}, bf16[128,3328]{1,0:T(8,128)(2,1)S(1)}, u32[]{:S(2)}, u32[]{:S(2)}) collective-permute-start(bf16[128,3328]{1,0:T(8,128)(2,1)S(1)} %pad_maximum_fusion.rest_0_), channel_id=1, source_target_pairs={{0,24},{1,97},{8,0},{9,105},{16,8},{17,113},{24,16},{25,121},{32,5... | collective-permute-start | bytes 2555912 | tf_op jit(solution)/shard_map/ppermute | solution.py:29
  70.4 13.4 %collective-permute-start.13 = (bf16[128,3328]{1,0:T(8,128)(2,1)S(1)}, bf16[128,3328]{1,0:T(8,128)(2,1)S(1)}, u32[]{:S(2)}, u32[]{:S(2)}) collective-permute-start(bf16[128,3328]{1,0:T(8,128)(2,1)S(1)} %pad_maximum_fusion.rest_0_), channel_id=1, source_target_pairs={{0,16},{1,65},{8,24},{9,73},{16,0},{17,81},{24,8},{25,89},{32,48},... | collective-permute-start | bytes 2555912 | tf_op jit(solution)/shard_map/ppermute | solution.py:29
  70.8 22.1 %collective-permute-start.14 = (bf16[128,3328]{1,0:T(8,128)(2,1)S(1)}, bf16[128,3328]{1,0:T(8,128)(2,1)S(1)}, u32[]{:S(2)}, u32[]{:S(2)}) collective-permute-start(bf16[128,3328]{1,0:T(8,128)(2,1)S(1)} %pad_maximum_fusion.rest_0_), channel_id=1, source_target_pairs={{0,8},{1,33},{8,16},{9,41},{16,24},{17,49},{24,0},{25,57},{32,40},... | collective-permute-start | bytes 2555912 | tf_op jit(solution)/shard_map/ppermute | solution.py:29
  71.7 2.9 %copy-start = (bf16[3328,1024]{1,0:T(8,128)(2,1)S(1)}, bf16[3328,1024]{1,0:T(8,128)(2,1)}, u32[]{:S(2)}) copy-start(bf16[3328,1024]{1,0:T(8,128)(2,1)} %codes) | copy-start | bytes 20447236
  96.9 6.4 %collective-permute-start.15 = (bf16[4,64,1024]{2,1,0:T(8,128)(2,1)S(1)}, bf16[4,64,1024]{2,1,0:T(8,128)(2,1)S(1)}, u32[]{:S(2)}, u32[]{:S(2)}) collective-permute-start(bf16[4,64,1024]{2,1,0:T(8,128)(2,1)S(1)} %get-tuple-element.29), channel_id=1, source_target_pairs={{0,1},{1,0},{2,3},{3,2},{4,5},{5,4},{6,7},{7,6},{8,9},{9,8},{10,11... | collective-permute-start | bytes 1572872 | tf_op jit(solution)/shard_map/ppermute | solution.py:37
  103.5 7.4 %collective-permute-start.16 = (bf16[64,1024]{1,0:T(8,128)(2,1)S(1)}, bf16[64,1024]{1,0:T(8,128)(2,1)S(1)}, u32[]{:S(2)}, u32[]{:S(2)}) collective-permute-start(bf16[64,1024]{1,0:T(8,128)(2,1)S(1)} %get-tuple-element.35), channel_id=1, source_target_pairs={{0,2},{2,4},{4,6},{6,0},{1,3},{3,5},{5,7},{7,1},{8,10},{10,12},{12... | collective-permute-start | bytes 393224 | tf_op jit(solution)/shard_map/ppermute | solution.py:33
  105.2 5.7 %collective-permute-start.17 = (bf16[64,1024]{1,0:T(8,128)(2,1)S(1)}, bf16[64,1024]{1,0:T(8,128)(2,1)S(1)}, u32[]{:S(2)}, u32[]{:S(2)}) collective-permute-start(bf16[64,1024]{1,0:T(8,128)(2,1)S(1)} %get-tuple-element.37), channel_id=1, source_target_pairs={{0,6},{2,0},{4,2},{6,4},{1,7},{3,1},{5,3},{7,5},{8,14},{10,8},{12,... | collective-permute-start | bytes 393224 | tf_op jit(solution)/shard_map/ppermute | solution.py:33
  107.4 7.2 %collective-permute-start.18 = (bf16[64,1024]{1,0:T(8,128)(2,1)S(1)}, bf16[64,1024]{1,0:T(8,128)(2,1)S(1)}, u32[]{:S(2)}, u32[]{:S(2)}) collective-permute-start(bf16[64,1024]{1,0:T(8,128)(2,1)S(1)} %get-tuple-element.36), channel_id=1, source_target_pairs={{0,4},{2,6},{4,0},{6,2},{1,5},{3,7},{5,1},{7,3},{8,12},{10,14},{12... | collective-permute-start | bytes 393224 | tf_op jit(solution)/shard_map/ppermute | solution.py:33
  114.7 4.6 %collective-permute-start.19 = (bf16[64,1024]{1,0:T(8,128)(2,1)S(1)}, bf16[64,1024]{1,0:T(8,128)(2,1)S(1)}, u32[]{:S(2)}, u32[]{:S(2)}) collective-permute-start(bf16[64,1024]{1,0:T(8,128)(2,1)S(1)} %fusion.4), channel_id=1, source_target_pairs={{0,6},{2,0},{4,2},{6,4},{1,7},{3,1},{5,3},{7,5},{8,14},{10,8},{12,... | collective-permute-start | bytes 393224 | tf_op jit(solution)/shard_map/ppermute | solution.py:33
  115.2 6.9 %collective-permute-start.20 = (bf16[64,1024]{1,0:T(8,128)(2,1)S(1)}, bf16[64,1024]{1,0:T(8,128)(2,1)S(1)}, u32[]{:S(2)}, u32[]{:S(2)}) collective-permute-start(bf16[64,1024]{1,0:T(8,128)(2,1)S(1)} %fusion.4), channel_id=1, source_target_pairs={{0,4},{2,6},{4,0},{6,2},{1,5},{3,7},{5,1},{7,3},{8,12},{10,14},{12... | collective-permute-start | bytes 393224 | tf_op jit(solution)/shard_map/ppermute | solution.py:33
  117.1 7.2 %collective-permute-start.21 = (bf16[64,1024]{1,0:T(8,128)(2,1)S(1)}, bf16[64,1024]{1,0:T(8,128)(2,1)S(1)}, u32[]{:S(2)}, u32[]{:S(2)}) collective-permute-start(bf16[64,1024]{1,0:T(8,128)(2,1)S(1)} %fusion.4), channel_id=1, source_target_pairs={{0,2},{2,4},{4,6},{6,0},{1,3},{3,5},{5,7},{7,1},{8,10},{10,12},{12... | collective-permute-start | bytes 393224 | tf_op jit(solution)/shard_map/ppermute | solution.py:33
  117.1 8.7 %collective-permute-start.22 = (bf16[64,1024]{1,0:T(8,128)(2,1)S(1)}, bf16[64,1024]{1,0:T(8,128)(2,1)S(1)}, u32[]{:S(2)}, u32[]{:S(2)}) collective-permute-start(bf16[64,1024]{1,0:T(8,128)(2,1)S(1)} %fusion.4), channel_id=1, source_target_pairs={{0,1},{1,0},{2,3},{3,2},{4,5},{5,4},{6,7},{7,6},{8,9},{9,8},{10,11... | collective-permute-start | bytes 393224 | tf_op jit(solution)/shard_map/ppermute | solution.py:37
  119.3 6.5 %collective-permute-start.23 = (bf16[64,1024]{1,0:T(8,128)(2,1)S(1)}, bf16[64,1024]{1,0:T(8,128)(2,1)S(1)}, u32[]{:S(2)}, u32[]{:S(2)}) collective-permute-start(bf16[64,1024]{1,0:T(8,128)(2,1)S(1)} %collective-permute-done.19), channel_id=1, source_target_pairs={{0,1},{1,0},{2,3},{3,2},{4,5},{5,4},{6,7},{7,6},{8,9},{9,8},{10,11... | collective-permute-start | bytes 393224 | tf_op jit(solution)/shard_map/ppermute | solution.py:37
  122.1 3.8 %collective-permute-start.24 = (bf16[64,1024]{1,0:T(8,128)(2,1)S(1)}, bf16[64,1024]{1,0:T(8,128)(2,1)S(1)}, u32[]{:S(2)}, u32[]{:S(2)}) collective-permute-start(bf16[64,1024]{1,0:T(8,128)(2,1)S(1)} %collective-permute-done.20), channel_id=1, source_target_pairs={{0,1},{1,0},{2,3},{3,2},{4,5},{5,4},{6,7},{7,6},{8,9},{9,8},{10,11... | collective-permute-start | bytes 393224 | tf_op jit(solution)/shard_map/ppermute | solution.py:37
  124.3 2.4 %collective-permute-start.25 = (bf16[64,1024]{1,0:T(8,128)(2,1)S(1)}, bf16[64,1024]{1,0:T(8,128)(2,1)S(1)}, u32[]{:S(2)}, u32[]{:S(2)}) collective-permute-start(bf16[64,1024]{1,0:T(8,128)(2,1)S(1)} %collective-permute-done.21), channel_id=1, source_target_pairs={{0,1},{1,0},{2,3},{3,2},{4,5},{5,4},{6,7},{7,6},{8,9},{9,8},{10,11... | collective-permute-start | bytes 393224 | tf_op jit(solution)/shard_map/ppermute | solution.py:37
  126.7 1.0 copy-start.3

commit v5 on v4

--- a/solution.py
+++ b/solution.py
@@ -10,9 +10,9 @@
 BLOCK = 128
 SIDE = 4
 TILES = (512, 896, 896, 1024)
-DEPTH = 2
+DEPTH = 3
 DOWN_TILE = 512
-PARTS = ((0, 0, 4), (1, 0, 4), (2, 0, 4), (3, 0, 4))
+PARTS = ((0, 0, 4), (1, 0, 4), (2, 0, 2), (2, 2, 2), (3, 0, 4))
 PLANE = ("y", "x", "core")
 
 
@@ -192,7 +192,7 @@
 
 
 def down_kernel(piece, *rest):
-    parts, (down_w, mine, theirs, act) = rest[:4], rest[4:]
+    parts, (down_w, mine, theirs, act) = rest[:5], rest[5:]
     place = places()
     for (a, b, count), part in zip(PARTS, parts):
         for k in range(count):
@@ -220,7 +220,7 @@
     return pl.pallas_call(
         functools.partial(down_kernel, piece),
         out_shape=(shape, shape),
-        in_specs=[vmem] * 5,
+        in_specs=[vmem] * 6,
         out_specs=(vmem, vmem),
         scratch_shapes=[pltpu.VMEM((rows, depth), jnp.bfloat16)],
         compiler_params=pltpu.CompilerParams(vmem_limit_bytes=24 * 1024 * 1024),
@@ -261,7 +261,10 @@
     residual = lax.dynamic_slice_in_dim(states, core * (rows // 2) + iz * (rows // 8), rows // 8, 0)
     line, residual, down_codes, down_scales = lax.optimization_barrier((line, residual, down_codes, down_scales))
     down_w = fetched_weights(down_codes, down_scales)
-    parts = (line, hop(line, 0, -1), hop(line, 0, 2), hop(line, 0, 1))
+    ahead, behind = hop(line, 0, -1), hop(line, 0, 1)
+    ahead, behind, down_w = lax.optimization_barrier((ahead, behind, down_w))
+    half = 2 * piece
+    parts = (line, ahead, hop(ahead[:half], 0, -1), hop(behind[half:], 0, 1), behind)
 
     mine, theirs = down_sums(parts, down_w)
     both = rounded(mine, other_core(theirs))

time: 128 us -> 128 us (level)
  starting transfers between devices: 37.2 us -> 40.1 us
  waiting for transfers between devices: 57.3 us -> 55.5 us
  Pallas kernels: 24.8 us -> 23.4 us
    ppermute x15 -> x16, starting transfers between devices: 16.4 us -> 18.5 us  [hop(): return lax.ppermute(array, PLANE, pairs)]
    ppermute x15 -> x16, waiting for transfers between devices: 49 us -> 47.2 us  [hop(): return lax.ppermute(array, PLANE, pairs)]
    pallas_call x2, Pallas kernels: 18.9 us -> 17.5 us  [partial_sums(): pl.pallas_call(functools.partial(up_kernel, piece, halves, ends), out_sha...]
  transfers between devices with their start and end apart: 26 -> 27, of which waited for: 14 -> 15; matrix products, arithmetic and copies ran while one was open for 2% -> 2% of each run, Pallas kernels for 9% -> 8%
where the time goes in v5:
time: 128 us; the launch traced here: 127 us
  waiting for transfers between devices  55.5 us (43%)
  starting transfers between devices  40.1 us (31%)
  Pallas kernels  23.4 us (18%)
  local copies, waits for them, and re-layouts  5.24 us (4%)
  other arithmetic  2.89 us (2%)
    ppermute x16, waiting for transfers between devices, hop(): return lax.ppermute(array, PLANE, pairs)  47.2 us
    ppermute x16, starting transfers between devices, hop(): return lax.ppermute(array, PLANE, pairs)  18.5 us
    pallas_call x2, Pallas kernels, partial_sums(): pl.pallas_call(functools.partial(up_kernel, piece, halves, ends), out_sha...  17.5 us
    ppermute x5, starting transfers between devices, other_core(): return lax.ppermute(array, 'core', [(0, 1), (1, 0)])  14.1 us
    ppermute x6, starting transfers between devices, hop_z(): lax.ppermute(array, 'z', [(i, (i + shift) % SIDE) for i in range(SIDE)])  7.53 us
    ppermute x6, waiting for transfers between devices, hop_z(): lax.ppermute(array, 'z', [(i, (i + shift) % SIDE) for i in range(SIDE)])  5.93 us
    pallas_call x1, Pallas kernels, down_sums(): pl.pallas_call(functools.partial(down_kernel, piece), out_shape=(shape, s...  3.93 us
    unnamed x10, local copies, waits for them, and re-layouts  3.91 us
  transfers between devices with their start and end apart: 27, of which 15 were waited for; matrix products, arithmetic and copies ran while one was open for 2% of the time, Pallas kernels for 8%

profile of v5, /device:TPU:1, one launch (start us, length us, event | category | flops | bytes accessed | tf_op | source)
XLA Modules:
  0.0 127.4 jit_solution(11756076426254356013)
XLA Ops:
  0.0 9.1 %partial_sums.3 = (bf16[64,6656]{1,0:T(8,128)(2,1)}, bf16[64,6656]{1,0:T(8,128)(2,1)}, bf16[64,6656]{1,0:T(8,128)(2,1)}, bf16[64,6656]{1,0:T(8,128)(2,1)}) custom-call(bf16[512,1024]{1,0:T(8,128)(2,1)} %states.3, bf16[1024,3328]{1,0:T(8,128)(2,1)} %gate_codes.3, f32[8,3328]{1,0:T(8,128)} %gate_scales.3, bf16[1024,3328]{1,0:T(8,128)(2,1)} %up_codes.3, ...), custom_call_target="tpu_custom_call" | custom-call | flops 3489660928 | bytes 17039360 | tf_op jit(solution)/shard_map/partial_sums/pallas_call | solution.py:132
  9.1 3.6 %collective-permute-start.1 = (bf16[64,6656]{1,0:T(8,128)(2,1)}, bf16[64,6656]{1,0:T(8,128)(2,1)S(1)}, u32[]{:S(2)}, u32[]{:S(2)}) collective-permute-start(bf16[64,6656]{1,0:T(8,128)(2,1)} %get-tuple-element.24), channel_id=1, source_target_pairs={{0,24},{1,97},{8,0},{9,105},{16,8},{17,113},{24,16},{25,121},{32,5... | collective-permute-start | bytes 2555912 | tf_op jit(solution)/shard_map/ppermute | solution.py:29
  12.7 0.0 collective-permute-start.4
  12.7 0.0 collective-permute-start
  12.7 2.7 %collective-permute-start.6 = (bf16[64,6656]{1,0:T(8,128)(2,1)}, bf16[64,6656]{1,0:T(8,128)(2,1)S(1)}, u32[]{:S(2)}, u32[]{:S(2)}) collective-permute-start(bf16[64,6656]{1,0:T(8,128)(2,1)} %get-tuple-element.27), channel_id=1, source_target_pairs={{0,24},{1,97},{8,0},{9,105},{16,8},{17,113},{24,16},{25,121},{32,5... | collective-permute-start | bytes 2555912 | tf_op jit(solution)/shard_map/ppermute | solution.py:29
  15.4 8.5 %partial_sums.2 = (bf16[64,6656]{1,0:T(8,128)(2,1)}, bf16[64,6656]{1,0:T(8,128)(2,1)}, bf16[128,6656]{1,0:T(8,128)(2,1)}) custom-call(bf16[512,1024]{1,0:T(8,128)(2,1)} %states.3, bf16[1024,3328]{1,0:T(8,128)(2,1)} %gate_codes.3, f32[8,3328]{1,0:T(8,128)} %gate_scales.3, bf16[1024,3328]{1,0:T(8,128)(2,1)} %up_codes.3, f32[8,3328]{1,0:T(8,128)} %up_scales.3), custom_call_target="tpu_custom_call" | custom-call | flops 3489660928 | bytes 17039360 | tf_op jit(solution)/shard_map/partial_sums/pallas_call | solution.py:132
  23.9 0.0 collective-permute-done.1
  23.9 1.4 %add_convert_fusion.3 = bf16[64,6656]{1,0:T(8,128)(2,1)S(1)} fusion(bf16[64,6656]{1,0:T(8,128)(2,1)S(1)} %collective-permute-done.1, bf16[64,6656]{1,0:T(8,128)(2,1)} %get-tuple-element.23), kind=kLoop, calls=%fused_computation.3 | loop fusion | flops 1703936 | bytes 2555904 | tf_op jit(solution)/shard_map/convert_element_type | solution.py:48
  25.3 2.2 %collective-permute-start.2 = (bf16[64,6656]{1,0:T(8,128)(2,1)S(1)}, bf16[64,6656]{1,0:T(8,128)(2,1)S(1)}, u32[]{:S(2)}, u32[]{:S(2)}) collective-permute-start(bf16[64,6656]{1,0:T(8,128)(2,1)S(1)} %add_convert_fusion.3), channel_id=1, source_target_pairs={{0,24},{1,97},{8,0},{9,105},{16,8},{17,113},{24,16},{25,121},{32,5... | collective-permute-start | bytes 2555912 | tf_op jit(solution)/shard_map/ppermute | solution.py:29
  27.6 0.0 collective-permute-done.4
  27.6 0.2 add_convert_fusion.1
  27.8 0.1 collective-permute-start.5
  27.9 7.2 %collective-permute-done = bf16[64,6656]{1,0:T(8,128)(2,1)S(1)} collective-permute-done((bf16[64,6656]{1,0:T(8,128)(2,1)}, bf16[64,6656]{1,0:T(8,128)(2,1)S(1)}, u32[]{:S(2)}, u32[]{:S(2)}) %collective-permute-start) | collective-permute-done | bytes 852000 | tf_op jit(solution)/shard_map/ppermute | solution.py:29
  35.1 0.0 collective-permute-done.6
  35.1 5.7 %collective-permute-done.2 = bf16[64,6656]{1,0:T(8,128)(2,1)S(1)} collective-permute-done((bf16[64,6656]{1,0:T(8,128)(2,1)S(1)}, bf16[64,6656]{1,0:T(8,128)(2,1)S(1)}, u32[]{:S(2)}, u32[]{:S(2)}) %collective-permute-start.2) | collective-permute-done | bytes 852000 | tf_op jit(solution)/shard_map/ppermute | solution.py:29
  40.8 3.4 %collective-permute-done.5 = bf16[64,6656]{1,0:T(8,128)(2,1)S(1)} collective-permute-done((bf16[64,6656]{1,0:T(8,128)(2,1)S(1)}, bf16[64,6656]{1,0:T(8,128)(2,1)S(1)}, u32[]{:S(2)}, u32[]{:S(2)}) %collective-permute-start.5) | collective-permute-done | bytes 852000 | tf_op jit(solution)/shard_map/ppermute | solution.py:29
  44.2 0.6 add_convert_fusion.2
  44.8 0.1 fusion.5
  44.9 2.3 %collective-permute-start.7 = (bf16[32,6656]{1,0:T(8,128)(2,1)S(1)}, bf16[32,6656]{1,0:T(8,128)(2,1)S(1)}, u32[]{:S(2)}, u32[]{:S(2)}) collective-permute-start(bf16[32,6656]{1,0:T(8,128)(2,1)S(1)} %get-tuple-element.39), channel_id=1, source_target_pairs={{0,96},{1,25},{8,104},{9,1},{16,112},{17,9},{24,120},{25,17},{32,0... | collective-permute-start | bytes 1277960 | tf_op jit(solution)/shard_map/ppermute | solution.py:29
  47.2 0.5 collective-permute-start.8
  47.7 0.7 collective-permute-start.3
  48.4 8.4 %collective-permute-done.7 = bf16[32,6656]{1,0:T(8,128)(2,1)S(1)} collective-permute-done((bf16[32,6656]{1,0:T(8,128)(2,1)S(1)}, bf16[32,6656]{1,0:T(8,128)(2,1)S(1)}, u32[]{:S(2)}, u32[]{:S(2)}) %collective-permute-start.7) | collective-permute-done | bytes 426016 | tf_op jit(solution)/shard_map/ppermute | solution.py:29
  56.8 3.7 %collective-permute-done.3 = bf16[32,6656]{1,0:T(8,128)(2,1)S(1)} collective-permute-done((bf16[32,6656]{1,0:T(8,128)(2,1)S(1)}, bf16[32,6656]{1,0:T(8,128)(2,1)S(1)}, u32[]{:S(2)}, u32[]{:S(2)}) %collective-permute-start.3) | collective-permute-done | bytes 426016 | tf_op jit(solution)/shard_map/ppermute | solution.py:29
  60.5 0.2 convert_add_fusion
  60.7 0.0 copy-start.1
  60.7 0.1 fusion
  60.8 0.6 collective-permute-start.10
  61.4 0.4 collective-permute-start.11
  61.8 2.3 %collective-permute-start.9 = (bf16[32,3328]{1,0:T(8,128)(2,1)S(1)}, bf16[32,3328]{1,0:T(8,128)(2,1)S(1)}, u32[]{:S(2)}, u32[]{:S(2)}) collective-permute-start(bf16[32,3328]{1,0:T(8,128)(2,1)S(1)} %fusion), channel_id=1, source_target_pairs={{0,96},{1,25},{8,104},{9,1},{16,112},{17,9},{24,120},{25,17},{32,0... | collective-permute-start | bytes 638984 | tf_op jit(solution)/shard_map/ppermute | solution.py:29
  64.1 0.9 constant_dynamic-slice_fusion
  65.0 2.2 %collective-permute-done.10 = bf16[32,3328]{1,0:T(8,128)(2,1)S(1)} collective-permute-done((bf16[32,3328]{1,0:T(8,128)(2,1)S(1)}, bf16[32,3328]{1,0:T(8,128)(2,1)S(1)}, u32[]{:S(2)}, u32[]{:S(2)}) %collective-permute-start.10) | collective-permute-done | bytes 213024 | tf_op jit(solution)/shard_map/ppermute | solution.py:29
  67.2 2.5 %collective-permute-done.11 = bf16[32,3328]{1,0:T(8,128)(2,1)S(1)} collective-permute-done((bf16[32,3328]{1,0:T(8,128)(2,1)S(1)}, bf16[32,3328]{1,0:T(8,128)(2,1)S(1)}, u32[]{:S(2)}, u32[]{:S(2)}) %collective-permute-start.11) | collective-permute-done | bytes 213024 | tf_op jit(solution)/shard_map/ppermute | solution.py:29
  69.7 0.0 collective-permute-done.9
  69.7 0.1 pad_maximum_fusion.rest_0_
  69.8 0.3 collective-permute-start.12
  70.1 1.2 collective-permute-start.13
  71.3 2.9 %copy-done = bf16[3328,1024]{1,0:T(8,128)(2,1)S(1)} copy-done((bf16[3328,1024]{1,0:T(8,128)(2,1)S(1)}, bf16[3328,1024]{1,0:T(8,128)(2,1)}, u32[]{:S(2)}) %copy-start) | copy-done | bytes 6815768
  74.2 1.9 %fetched_weights.1.rest_5_ = bf16[3328,1024]{1,0:T(8,128)(2,1)S(1)} custom-call(bf16[3328,1024]{1,0:T(8,128)(2,1)S(1)} %copy-done, f32[26,1024]{1,0:T(8,128)S(1)} %copy-done.1), custom_call_target="tpu_custom_call" | custom-call | flops 3407872 | bytes 6815744 | tf_op jit(solution)/shard_map/fetched_weights/pallas_call | solution.py:178
  76.2 5.5 %collective-permute-done.12.rest_1_ = bf16[128,3328]{1,0:T(8,128)(2,1)S(1)} collective-permute-done((bf16[128,3328]{1,0:T(8,128)(2,1)S(1)}, bf16[128,3328]{1,0:T(8,128)(2,1)S(1)}, u32[]{:S(2)}, u32[]{:S(2)}) %collective-permute-start.12) | collective-permute-done | bytes 852000 | tf_op jit(solution)/shard_map/ppermute | solution.py:29
  81.7 1.4 %collective-permute-done.13.rest_4_ = bf16[128,3328]{1,0:T(8,128)(2,1)S(1)} collective-permute-done((bf16[128,3328]{1,0:T(8,128)(2,1)S(1)}, bf16[128,3328]{1,0:T(8,128)(2,1)S(1)}, u32[]{:S(2)}, u32[]{:S(2)}) %collective-permute-start.13) | collective-permute-done | bytes 852000 | tf_op jit(solution)/shard_map/ppermute | solution.py:29
  83.1 0.5 collective-permute-start.14
  83.7 1.1 collective-permute-start.15
  84.8 5.4 %collective-permute-done.14.rest_2_ = bf16[64,3328]{1,0:T(8,128)(2,1)S(1)} collective-permute-done((bf16[64,3328]{1,0:T(8,128)(2,1)S(1)}, bf16[64,3328]{1,0:T(8,128)(2,1)S(1)}, u32[]{:S(2)}, u32[]{:S(2)}) %collective-permute-start.14) | collective-permute-done | bytes 426016 | tf_op jit(solution)/shard_map/ppermute | solution.py:29
  90.2 1.7 %collective-permute-done.15.rest_3_ = bf16[64,3328]{1,0:T(8,128)(2,1)S(1)} collective-permute-done((bf16[64,3328]{1,0:T(8,128)(2,1)S(1)}, bf16[64,3328]{1,0:T(8,128)(2,1)S(1)}, u32[]{:S(2)}, u32[]{:S(2)}) %collective-permute-start.15) | collective-permute-done | bytes 426016 | tf_op jit(solution)/shard_map/ppermute | solution.py:29
  91.9 3.9 %down_sums.1 = (bf16[4,64,1024]{2,1,0:T(8,128)(2,1)S(1)}, bf16[4,64,1024]{2,1,0:T(8,128)(2,1)S(1)}) custom-call(bf16[128,3328]{1,0:T(8,128)(2,1)S(1)} %pad_maximum_fusion.rest_0_, bf16[128,3328]{1,0:T(8,128)(2,1)S(1)} %collective-permute-done.12.rest_1_, bf16[64,3328]{1,0:T(8,128)(2,1)S(1)} %collective-permute-done.14.rest_2_, ...), custom_call_target="tpu_custom_call" | custom-call | flops 3489660928 | bytes 10223616 | tf_op jit(solution)/shard_map/down_sums/pallas_call | solution.py:220
  95.9 5.6 %collective-permute-start.16 = (bf16[4,64,1024]{2,1,0:T(8,128)(2,1)S(1)}, bf16[4,64,1024]{2,1,0:T(8,128)(2,1)S(1)}, u32[]{:S(2)}, u32[]{:S(2)}) collective-permute-start(bf16[4,64,1024]{2,1,0:T(8,128)(2,1)S(1)} %get-tuple-element.35), channel_id=1, source_target_pairs={{0,1},{1,0},{2,3},{3,2},{4,5},{5,4},{6,7},{7,6},{8,9},{9,8},{10,11... | collective-permute-start | bytes 1572872 | tf_op jit(solution)/shard_map/ppermute | solution.py:37
  101.5 1.5 %collective-permute-done.16 = bf16[4,64,1024]{2,1,0:T(8,128)(2,1)S(1)} collective-permute-done((bf16[4,64,1024]{2,1,0:T(8,128)(2,1)S(1)}, bf16[4,64,1024]{2,1,0:T(8,128)(2,1)S(1)}, u32[]{:S(2)}, u32[]{:S(2)}) %collective-permute-start.16) | collective-permute-done | bytes 524320 | tf_op jit(solution)/shard_map/ppermute | solution.py:37
  103.0 0.2 add_convert_fusion.4
  103.3 1.7 %collective-permute-start.17 = (bf16[64,1024]{1,0:T(8,128)(2,1)S(1)}, bf16[64,1024]{1,0:T(8,128)(2,1)S(1)}, u32[]{:S(2)}, u32[]{:S(2)}) collective-permute-start(bf16[64,1024]{1,0:T(8,128)(2,1)S(1)} %get-tuple-element.41), channel_id=1, source_target_pairs={{0,2},{2,4},{4,6},{6,0},{1,3},{3,5},{5,7},{7,1},{8,10},{10,12},{12... | collective-permute-start | bytes 393224 | tf_op jit(solution)/shard_map/ppermute | solution.py:33
  105.0 2.2 %collective-permute-start.18 = (bf16[64,1024]{1,0:T(8,128)(2,1)S(1)}, bf16[64,1024]{1,0:T(8,128)(2,1)S(1)}, u32[]{:S(2)}, u32[]{:S(2)}) collective-permute-start(bf16[64,1024]{1,0:T(8,128)(2,1)S(1)} %get-tuple-element.43), channel_id=1, source_target_pairs={{0,6},{2,0},{4,2},{6,4},{1,7},{3,1},{5,3},{7,5},{8,14},{10,8},{12,... | collective-permute-start | bytes 393224 | tf_op jit(solution)/shard_map/ppermute | solution.py:33
  107.2 1.2 collective-permute-start.19
  108.4 2.3 %collective-permute-done.17 = bf16[64,1024]{1,0:T(8,128)(2,1)S(1)} collective-permute-done((bf16[64,1024]{1,0:T(8,128)(2,1)S(1)}, bf16[64,1024]{1,0:T(8,128)(2,1)S(1)}, u32[]{:S(2)}, u32[]{:S(2)}) %collective-permute-start.17) | collective-permute-done | bytes 131104 | tf_op jit(solution)/shard_map/ppermute | solution.py:33
  110.7 3.7 %collective-permute-done.19 = bf16[64,1024]{1,0:T(8,128)(2,1)S(1)} collective-permute-done((bf16[64,1024]{1,0:T(8,128)(2,1)S(1)}, bf16[64,1024]{1,0:T(8,128)(2,1)S(1)}, u32[]{:S(2)}, u32[]{:S(2)}) %collective-permute-start.19) | collective-permute-done | bytes 131104 | tf_op jit(solution)/shard_map/ppermute | solution.py:33
  114.3 0.1 fusion.4
  114.4 0.5 collective-permute-start.20
  114.9 1.9 %collective-permute-start.21 = (bf16[64,1024]{1,0:T(8,128)(2,1)S(1)}, bf16[64,1024]{1,0:T(8,128)(2,1)S(1)}, u32[]{:S(2)}, u32[]{:S(2)}) collective-permute-start(bf16[64,1024]{1,0:T(8,128)(2,1)S(1)} %fusion.4), channel_id=1, source_target_pairs={{0,4},{2,6},{4,0},{6,2},{1,5},{3,7},{5,1},{7,3},{8,12},{10,14},{12... | collective-permute-start | bytes 393224 | tf_op jit(solution)/shard_map/ppermute | solution.py:33
  116.8 2.1 %collective-permute-start.23 = (bf16[64,1024]{1,0:T(8,128)(2,1)S(1)}, bf16[64,1024]{1,0:T(8,128)(2,1)S(1)}, u32[]{:S(2)}, u32[]{:S(2)}) collective-permute-start(bf16[64,1024]{1,0:T(8,128)(2,1)S(1)} %fusion.4), channel_id=1, source_target_pairs={{0,1},{1,0},{2,3},{3,2},{4,5},{5,4},{6,7},{7,6},{8,9},{9,8},{10,11... | collective-permute-start | bytes 393224 | tf_op jit(solution)/shard_map/ppermute | solution.py:37
  118.9 0.1 broadcast_in_dim.27
  119.1 2.7 %collective-permute-start.24 = (bf16[64,1024]{1,0:T(8,128)(2,1)S(1)}, bf16[64,1024]{1,0:T(8,128)(2,1)S(1)}, u32[]{:S(2)}, u32[]{:S(2)}) collective-permute-start(bf16[64,1024]{1,0:T(8,128)(2,1)S(1)} %collective-permute-done.20), channel_id=1, source_target_pairs={{0,1},{1,0},{2,3},{3,2},{4,5},{5,4},{6,7},{7,6},{8,9},{9,8},{10,11... | collective-permute-start | bytes 393224 | tf_op jit(solution)/shard_map/ppermute | solution.py:37
  121.8 2.2 %collective-permute-start.25 = (bf16[64,1024]{1,0:T(8,128)(2,1)S(1)}, bf16[64,1024]{1,0:T(8,128)(2,1)S(1)}, u32[]{:S(2)}, u32[]{:S(2)}) collective-permute-start(bf16[64,1024]{1,0:T(8,128)(2,1)S(1)} %collective-permute-done.21), channel_id=1, source_target_pairs={{0,1},{1,0},{2,3},{3,2},{4,5},{5,4},{6,7},{7,6},{8,9},{9,8},{10,11... | collective-permute-start | bytes 393224 | tf_op jit(solution)/shard_map/ppermute | solution.py:37
  124.1 1.4 %collective-permute-start.26 = (bf16[64,1024]{1,0:T(8,128)(2,1)S(1)}, bf16[64,1024]{1,0:T(8,128)(2,1)S(1)}, u32[]{:S(2)}, u32[]{:S(2)}) collective-permute-start(bf16[64,1024]{1,0:T(8,128)(2,1)S(1)} %collective-permute-done.22), channel_id=1, source_target_pairs={{0,1},{1,0},{2,3},{3,2},{4,5},{5,4},{6,7},{7,6},{8,9},{9,8},{10,11... | collective-permute-start | bytes 393224 | tf_op jit(solution)/shard_map/ppermute | solution.py:37
  125.6 0.8 collective-permute-done.26
  126.4 0.0 copy-start.3
  126.4 1.0 copy-done.3
  (27 shorter events, 0.3 us)
Async XLA Ops:
  9.1 14.8 %collective-permute-start.1 = (bf16[64,6656]{1,0:T(8,128)(2,1)}, bf16[64,6656]{1,0:T(8,128)(2,1)S(1)}, u32[]{:S(2)}, u32[]{:S(2)}) collective-permute-start(bf16[64,6656]{1,0:T(8,128)(2,1)} %get-tuple-element.24), channel_id=1, source_target_pairs={{0,24},{1,97},{8,0},{9,105},{16,8},{17,113},{24,16},{25,121},{32,5... | collective-permute-start | bytes 2555912 | tf_op jit(solution)/shard_map/ppermute | solution.py:29
  12.7 14.9 %collective-permute-start.4 = (bf16[64,6656]{1,0:T(8,128)(2,1)}, bf16[64,6656]{1,0:T(8,128)(2,1)S(1)}, u32[]{:S(2)}, u32[]{:S(2)}) collective-permute-start(bf16[64,6656]{1,0:T(8,128)(2,1)} %get-tuple-element.26), channel_id=1, source_target_pairs={{0,8},{1,33},{8,16},{9,41},{16,24},{17,49},{24,0},{25,57},{32,40},... | collective-permute-start | bytes 2555912 | tf_op jit(solution)/shard_map/ppermute | solution.py:29
  12.7 22.4 %collective-permute-start = (bf16[64,6656]{1,0:T(8,128)(2,1)}, bf16[64,6656]{1,0:T(8,128)(2,1)S(1)}, u32[]{:S(2)}, u32[]{:S(2)}) collective-permute-start(bf16[64,6656]{1,0:T(8,128)(2,1)} %get-tuple-element.22), channel_id=1, source_target_pairs={{0,8},{1,33},{8,16},{9,41},{16,24},{17,49},{24,0},{25,57},{32,40},... | collective-permute-start | bytes 2555912 | tf_op jit(solution)/shard_map/ppermute | solution.py:29
  12.7 22.4 %collective-permute-start.6 = (bf16[64,6656]{1,0:T(8,128)(2,1)}, bf16[64,6656]{1,0:T(8,128)(2,1)S(1)}, u32[]{:S(2)}, u32[]{:S(2)}) collective-permute-start(bf16[64,6656]{1,0:T(8,128)(2,1)} %get-tuple-element.27), channel_id=1, source_target_pairs={{0,24},{1,97},{8,0},{9,105},{16,8},{17,113},{24,16},{25,121},{32,5... | collective-permute-start | bytes 2555912 | tf_op jit(solution)/shard_map/ppermute | solution.py:29
  23.9 3.7 %copy-start.4 = (bf16[64,6656]{1,0:T(8,128)(2,1)S(1)}, bf16[64,6656]{1,0:T(8,128)(2,1)}, u32[]{:S(2)}) copy-start(bf16[64,6656]{1,0:T(8,128)(2,1)} %get-tuple-element.25) | copy-start | bytes 2555908
  25.3 18.9 %copy-start.2 = (bf16[128,6656]{1,0:T(8,128)(2,1)S(1)}, bf16[128,6656]{1,0:T(8,128)(2,1)}, u32[]{:S(2)}) copy-start(bf16[128,6656]{1,0:T(8,128)(2,1)} %get-tuple-element.21) | copy-start | bytes 5111812
  25.3 15.5 %collective-permute-start.2 = (bf16[64,6656]{1,0:T(8,128)(2,1)S(1)}, bf16[64,6656]{1,0:T(8,128)(2,1)S(1)}, u32[]{:S(2)}, u32[]{:S(2)}) collective-permute-start(bf16[64,6656]{1,0:T(8,128)(2,1)S(1)} %add_convert_fusion.3), channel_id=1, source_target_pairs={{0,24},{1,97},{8,0},{9,105},{16,8},{17,113},{24,16},{25,121},{32,5... | collective-permute-start | bytes 2555912 | tf_op jit(solution)/shard_map/ppermute | solution.py:29
  27.8 16.4 %collective-permute-start.5 = (bf16[64,6656]{1,0:T(8,128)(2,1)S(1)}, bf16[64,6656]{1,0:T(8,128)(2,1)S(1)}, u32[]{:S(2)}, u32[]{:S(2)}) collective-permute-start(bf16[64,6656]{1,0:T(8,128)(2,1)S(1)} %add_convert_fusion.1), channel_id=1, source_target_pairs={{0,8},{1,33},{8,16},{9,41},{16,24},{17,49},{24,0},{25,57},{32,40},... | collective-permute-start | bytes 2555912 | tf_op jit(solution)/shard_map/ppermute | solution.py:29
  44.9 11.9 %collective-permute-start.7 = (bf16[32,6656]{1,0:T(8,128)(2,1)S(1)}, bf16[32,6656]{1,0:T(8,128)(2,1)S(1)}, u32[]{:S(2)}, u32[]{:S(2)}) collective-permute-start(bf16[32,6656]{1,0:T(8,128)(2,1)S(1)} %get-tuple-element.39), channel_id=1, source_target_pairs={{0,96},{1,25},{8,104},{9,1},{16,112},{17,9},{24,120},{25,17},{32,0... | collective-permute-start | bytes 1277960 | tf_op jit(solution)/shard_map/ppermute | solution.py:29
  47.2 9.6 %collective-permute-start.8 = (bf16[32,6656]{1,0:T(8,128)(2,1)S(1)}, bf16[32,6656]{1,0:T(8,128)(2,1)S(1)}, u32[]{:S(2)}, u32[]{:S(2)}) collective-permute-start(bf16[32,6656]{1,0:T(8,128)(2,1)S(1)} %get-tuple-element.40), channel_id=1, source_target_pairs={{0,64},{1,17},{8,72},{9,25},{16,80},{17,1},{24,88},{25,9},{32,96},... | collective-permute-start | bytes 1277960 | tf_op jit(solution)/shard_map/ppermute | solution.py:29
  47.7 12.8 %collective-permute-start.3 = (bf16[32,6656]{1,0:T(8,128)(2,1)S(1)}, bf16[32,6656]{1,0:T(8,128)(2,1)S(1)}, u32[]{:S(2)}, u32[]{:S(2)}) collective-permute-start(bf16[32,6656]{1,0:T(8,128)(2,1)S(1)} %slice.57), channel_id=1, source_target_pairs={{0,32},{1,9},{8,40},{9,17},{16,48},{17,25},{24,56},{25,1},{32,64},... | collective-permute-start | bytes 1277960 | tf_op jit(solution)/shard_map/ppermute | solution.py:29
  60.7 10.6 %copy-start.1 = (f32[26,1024]{1,0:T(8,128)S(1)}, f32[26,1024]{1,0:T(8,128)}, u32[]{:S(2)}) copy-start(f32[26,1024]{1,0:T(8,128)} %scales) | copy-start | bytes 319492
  60.8 6.4 %collective-permute-start.10 = (bf16[32,3328]{1,0:T(8,128)(2,1)S(1)}, bf16[32,3328]{1,0:T(8,128)(2,1)S(1)}, u32[]{:S(2)}, u32[]{:S(2)}) collective-permute-start(bf16[32,3328]{1,0:T(8,128)(2,1)S(1)} %fusion), channel_id=1, source_target_pairs={{0,64},{1,17},{8,72},{9,25},{16,80},{17,1},{24,88},{25,9},{32,96},... | collective-permute-start | bytes 638984 | tf_op jit(solution)/shard_map/ppermute | solution.py:29
  61.4 8.3 %collective-permute-start.11 = (bf16[32,3328]{1,0:T(8,128)(2,1)S(1)}, bf16[32,3328]{1,0:T(8,128)(2,1)S(1)}, u32[]{:S(2)}, u32[]{:S(2)}) collective-permute-start(bf16[32,3328]{1,0:T(8,128)(2,1)S(1)} %fusion), channel_id=1, source_target_pairs={{0,32},{1,9},{8,40},{9,17},{16,48},{17,25},{24,56},{25,1},{32,64},... | collective-permute-start | bytes 638984 | tf_op jit(solution)/shard_map/ppermute | solution.py:29
  61.8 7.9 %collective-permute-start.9 = (bf16[32,3328]{1,0:T(8,128)(2,1)S(1)}, bf16[32,3328]{1,0:T(8,128)(2,1)S(1)}, u32[]{:S(2)}, u32[]{:S(2)}) collective-permute-start(bf16[32,3328]{1,0:T(8,128)(2,1)S(1)} %fusion), channel_id=1, source_target_pairs={{0,96},{1,25},{8,104},{9,1},{16,112},{17,9},{24,120},{25,17},{32,0... | collective-permute-start | bytes 638984 | tf_op jit(solution)/shard_map/ppermute | solution.py:29
  69.8 11.9 %collective-permute-start.12 = (bf16[128,3328]{1,0:T(8,128)(2,1)S(1)}, bf16[128,3328]{1,0:T(8,128)(2,1)S(1)}, u32[]{:S(2)}, u32[]{:S(2)}) collective-permute-start(bf16[128,3328]{1,0:T(8,128)(2,1)S(1)} %pad_maximum_fusion.rest_0_), channel_id=1, source_target_pairs={{0,24},{1,97},{8,0},{9,105},{16,8},{17,113},{24,16},{25,121},{32,5... | collective-permute-start | bytes 2555912 | tf_op jit(solution)/shard_map/ppermute | solution.py:29
  70.1 13.0 %collective-permute-start.13 = (bf16[128,3328]{1,0:T(8,128)(2,1)S(1)}, bf16[128,3328]{1,0:T(8,128)(2,1)S(1)}, u32[]{:S(2)}, u32[]{:S(2)}) collective-permute-start(bf16[128,3328]{1,0:T(8,128)(2,1)S(1)} %pad_maximum_fusion.rest_0_), channel_id=1, source_target_pairs={{0,8},{1,33},{8,16},{9,41},{16,24},{17,49},{24,0},{25,57},{32,40},... | collective-permute-start | bytes 2555912 | tf_op jit(solution)/shard_map/ppermute | solution.py:29
  71.3 2.9 %copy-start = (bf16[3328,1024]{1,0:T(8,128)(2,1)S(1)}, bf16[3328,1024]{1,0:T(8,128)(2,1)}, u32[]{:S(2)}) copy-start(bf16[3328,1024]{1,0:T(8,128)(2,1)} %codes) | copy-start | bytes 20447236
  83.1 7.0 %collective-permute-start.14 = (bf16[64,3328]{1,0:T(8,128)(2,1)S(1)}, bf16[64,3328]{1,0:T(8,128)(2,1)S(1)}, u32[]{:S(2)}, u32[]{:S(2)}) collective-permute-start(bf16[64,3328]{1,0:T(8,128)(2,1)S(1)} %slice.50), channel_id=1, source_target_pairs={{0,24},{1,97},{8,0},{9,105},{16,8},{17,113},{24,16},{25,121},{32,5... | collective-permute-start | bytes 1277960 | tf_op jit(solution)/shard_map/ppermute | solution.py:29
  83.7 8.3 %collective-permute-start.15 = (bf16[64,3328]{1,0:T(8,128)(2,1)S(1)}, bf16[64,3328]{1,0:T(8,128)(2,1)S(1)}, u32[]{:S(2)}, u32[]{:S(2)}) collective-permute-start(bf16[64,3328]{1,0:T(8,128)(2,1)S(1)} %slice.51), channel_id=1, source_target_pairs={{0,8},{1,33},{8,16},{9,41},{16,24},{17,49},{24,0},{25,57},{32,40},... | collective-permute-start | bytes 1277960 | tf_op jit(solution)/shard_map/ppermute | solution.py:29
  95.9 7.2 %collective-permute-start.16 = (bf16[4,64,1024]{2,1,0:T(8,128)(2,1)S(1)}, bf16[4,64,1024]{2,1,0:T(8,128)(2,1)S(1)}, u32[]{:S(2)}, u32[]{:S(2)}) collective-permute-start(bf16[4,64,1024]{2,1,0:T(8,128)(2,1)S(1)} %get-tuple-element.35), channel_id=1, source_target_pairs={{0,1},{1,0},{2,3},{3,2},{4,5},{5,4},{6,7},{7,6},{8,9},{9,8},{10,11... | collective-permute-start | bytes 1572872 | tf_op jit(solution)/shard_map/ppermute | solution.py:37
  103.3 7.4 %collective-permute-start.17 = (bf16[64,1024]{1,0:T(8,128)(2,1)S(1)}, bf16[64,1024]{1,0:T(8,128)(2,1)S(1)}, u32[]{:S(2)}, u32[]{:S(2)}) collective-permute-start(bf16[64,1024]{1,0:T(8,128)(2,1)S(1)} %get-tuple-element.41), channel_id=1, source_target_pairs={{0,2},{2,4},{4,6},{6,0},{1,3},{3,5},{5,7},{7,1},{8,10},{10,12},{12... | collective-permute-start | bytes 393224 | tf_op jit(solution)/shard_map/ppermute | solution.py:33
  105.0 5.7 %collective-permute-start.18 = (bf16[64,1024]{1,0:T(8,128)(2,1)S(1)}, bf16[64,1024]{1,0:T(8,128)(2,1)S(1)}, u32[]{:S(2)}, u32[]{:S(2)}) collective-permute-start(bf16[64,1024]{1,0:T(8,128)(2,1)S(1)} %get-tuple-element.43), channel_id=1, source_target_pairs={{0,6},{2,0},{4,2},{6,4},{1,7},{3,1},{5,3},{7,5},{8,14},{10,8},{12,... | collective-permute-start | bytes 393224 | tf_op jit(solution)/shard_map/ppermute | solution.py:33
  107.2 7.2 %collective-permute-start.19 = (bf16[64,1024]{1,0:T(8,128)(2,1)S(1)}, bf16[64,1024]{1,0:T(8,128)(2,1)S(1)}, u32[]{:S(2)}, u32[]{:S(2)}) collective-permute-start(bf16[64,1024]{1,0:T(8,128)(2,1)S(1)} %get-tuple-element.42), channel_id=1, source_target_pairs={{0,4},{2,6},{4,0},{6,2},{1,5},{3,7},{5,1},{7,3},{8,12},{10,14},{12... | collective-permute-start | bytes 393224 | tf_op jit(solution)/shard_map/ppermute | solution.py:33
  114.4 4.6 %collective-permute-start.20 = (bf16[64,1024]{1,0:T(8,128)(2,1)S(1)}, bf16[64,1024]{1,0:T(8,128)(2,1)S(1)}, u32[]{:S(2)}, u32[]{:S(2)}) collective-permute-start(bf16[64,1024]{1,0:T(8,128)(2,1)S(1)} %fusion.4), channel_id=1, source_target_pairs={{0,6},{2,0},{4,2},{6,4},{1,7},{3,1},{5,3},{7,5},{8,14},{10,8},{12,... | collective-permute-start | bytes 393224 | tf_op jit(solution)/shard_map/ppermute | solution.py:33
  114.9 6.9 %collective-permute-start.21 = (bf16[64,1024]{1,0:T(8,128)(2,1)S(1)}, bf16[64,1024]{1,0:T(8,128)(2,1)S(1)}, u32[]{:S(2)}, u32[]{:S(2)}) collective-permute-start(bf16[64,1024]{1,0:T(8,128)(2,1)S(1)} %fusion.4), channel_id=1, source_target_pairs={{0,4},{2,6},{4,0},{6,2},{1,5},{3,7},{5,1},{7,3},{8,12},{10,14},{12... | collective-permute-start | bytes 393224 | tf_op jit(solution)/shard_map/ppermute | solution.py:33
  116.8 7.2 %collective-permute-start.22 = (bf16[64,1024]{1,0:T(8,128)(2,1)S(1)}, bf16[64,1024]{1,0:T(8,128)(2,1)S(1)}, u32[]{:S(2)}, u32[]{:S(2)}) collective-permute-start(bf16[64,1024]{1,0:T(8,128)(2,1)S(1)} %fusion.4), channel_id=1, source_target_pairs={{0,2},{2,4},{4,6},{6,0},{1,3},{3,5},{5,7},{7,1},{8,10},{10,12},{12... | collective-permute-start | bytes 393224 | tf_op jit(solution)/shard_map/ppermute | solution.py:33
  116.8 8.7 %collective-permute-start.23 = (bf16[64,1024]{1,0:T(8,128)(2,1)S(1)}, bf16[64,1024]{1,0:T(8,128)(2,1)S(1)}, u32[]{:S(2)}, u32[]{:S(2)}) collective-permute-start(bf16[64,1024]{1,0:T(8,128)(2,1)S(1)} %fusion.4), channel_id=1, source_target_pairs={{0,1},{1,0},{2,3},{3,2},{4,5},{5,4},{6,7},{7,6},{8,9},{9,8},{10,11... | collective-permute-start | bytes 393224 | tf_op jit(solution)/shard_map/ppermute | solution.py:37
  119.1 6.5 %collective-permute-start.24 = (bf16[64,1024]{1,0:T(8,128)(2,1)S(1)}, bf16[64,1024]{1,0:T(8,128)(2,1)S(1)}, u32[]{:S(2)}, u32[]{:S(2)}) collective-permute-start(bf16[64,1024]{1,0:T(8,128)(2,1)S(1)} %collective-permute-done.20), channel_id=1, source_target_pairs={{0,1},{1,0},{2,3},{3,2},{4,5},{5,4},{6,7},{7,6},{8,9},{9,8},{10,11... | collective-permute-start | bytes 393224 | tf_op jit(solution)/shard_map/ppermute | solution.py:37
  121.8 3.8 %collective-permute-start.25 = (bf16[64,1024]{1,0:T(8,128)(2,1)S(1)}, bf16[64,1024]{1,0:T(8,128)(2,1)S(1)}, u32[]{:S(2)}, u32[]{:S(2)}) collective-permute-start(bf16[64,1024]{1,0:T(8,128)(2,1)S(1)} %collective-permute-done.21), channel_id=1, source_target_pairs={{0,1},{1,0},{2,3},{3,2},{4,5},{5,4},{6,7},{7,6},{8,9},{9,8},{10,11... | collective-permute-start | bytes 393224 | tf_op jit(solution)/shard_map/ppermute | solution.py:37
  124.1 2.4 %collective-permute-start.26 = (bf16[64,1024]{1,0:T(8,128)(2,1)S(1)}, bf16[64,1024]{1,0:T(8,128)(2,1)S(1)}, u32[]{:S(2)}, u32[]{:S(2)}) collective-permute-start(bf16[64,1024]{1,0:T(8,128)(2,1)S(1)} %collective-permute-done.22), channel_id=1, source_target_pairs={{0,1},{1,0},{2,3},{3,2},{4,5},{5,4},{6,7},{7,6},{8,9},{9,8},{10,11... | collective-permute-start | bytes 393224 | tf_op jit(solution)/shard_map/ppermute | solution.py:37
  126.4 1.0 copy-start.3
